TPU v7x, 32 devices: a whole 2x2x4 slice. The times are simulated.
32 devices in a mesh: gy: 4 (over x, core), gz: 2 (over y), ga: 4 (over z).
Axes of the slice: x: 2, y: 2, z: 4, core: 2. Of those that a mesh axis runs over, the one named last changes fastest.
Arguments:
- fields: float32 [16, 256, 8, 512], P(None, 'gy', 'gz', 'ga'), may hold values from -6 to 6
- section_start: float32 [16, 256, 8, 512], P(None, 'gy', 'gz', 'ga'), may hold values from -6 to 6
- velocity: float32 [3, 256, 8, 512], P(None, 'gy', 'gz', 'ga'), may hold values from -4 to 4
- diffusivity: float32 [16], replicated, may hold values from 0.02 to 0.2
- reaction: float32 [16, 16], replicated, may hold values from -1.5 to 1.5
- x_factor: bfloat16 [512, 64], replicated, may hold values from -0.25 to 0.25
- y_factor: float32 [256, 64], replicated, may hold values from -6 to 6
Outputs:
- new_fields: float32 [16, 256, 8, 512], P(None, 'gy', 'gz', 'ga')
- x_gram: float32 [512, 512], P(('gy', 'gz'))
- y_products: float32 [8, 256, 64], P(('gz', 'gy'))
All inputs are finite; a program needn't handle non-finite values.
Results may differ from a plain program's by a relative error of at most 0.0028.
Values may be sent and summed in bfloat16 or wider, within the bound.
No kernel may reach another device: no remote copies, remote signals or barrier semaphores. Data moves between devices by JAX's collectives and lax.ppermute only.
A program may use at most 64 MiB of HBM per device.

v0:
```python
import functools

import jax
import jax.numpy as jnp
from jax import lax
from jax.experimental import pallas as pl
from jax.experimental.pallas import tpu as pltpu
from jax.sharding import PartitionSpec as P


time_step = 0.4
old_share, new_share = 0.75, 0.25
TILE = 32
SUB = 16
VMEM = pl.BlockSpec(memory_space=pltpu.VMEM)
SMEM = pl.BlockSpec(memory_space=pltpu.SMEM)
ANY = pl.BlockSpec(memory_space=pl.ANY)
f32, bf16 = jnp.float32, jnp.bfloat16
sds = jax.ShapeDtypeStruct
MIB = 1024 * 1024


def swap_pairs(count, turn):
    if turn == 0:
        return [(i, i ^ 1) for i in range(count)]
    return [(i, (i + (1 if i % 2 else -1)) % count) for i in range(count)]


def turns(count):
    return 1 if count == 2 else 2


def ring_pairs(count, step):
    return [(i, (i + step) % count) for i in range(count)]


def corner_mask(lanes):
    row = lax.broadcasted_iota(jnp.int32, (8, lanes), 0)
    lane = lax.broadcasted_iota(jnp.int32, (8, lanes), 1)
    return jnp.where(
        ((row == 0) & (lane == 0)) | ((row == 1) & (lane == lanes - 1)), 1.0, 0.0
    ).astype(bf16)


def rows_of(ref, v, segments):
    return jnp.concatenate([ref[v, first : first + count, :] for first, count in segments], axis=0)


def pack_kernel(z_cells, counts, plan, f_hbm, *refs):
    outs, (f_ref, sem) = refs[:-2], refs[-2:]
    variables, rows, lanes = f_ref.shape
    n_y, n_z, n_a = counts
    n_sem = sem.shape[0]
    step = variables // n_sem
    loads = [
        pltpu.make_async_copy(
            f_hbm.at[pl.ds(i * step, step)], f_ref.at[pl.ds(i * step, step)], sem.at[i]
        )
        for i in range(n_sem)
    ]
    for load in loads:
        load.start()
    y_refs, outs = outs[: turns(n_y)], outs[turns(n_y) :]
    x_refs, z_refs = outs[: turns(n_a)], outs[turns(n_a) :]
    odd_y, odd_z, odd_a = (lax.rem(lax.axis_index(a), 2) for a in ("gy", "gz", "ga"))
    pick = corner_mask(lanes)
    for v in range(variables):
        if v % step == 0:
            loads[v // step].wait()
        for c, segments in enumerate(plan):
            size = sum(count for _, count in segments)
            at = 0
            for first, count in segments:
                y_count = count // z_cells
                for turn in range(turns(n_z)):
                    start = first + jnp.where(odd_z == turn, z_cells - 1, 0)
                    z_refs[c * turns(n_z) + turn][v, at : at + y_count, :] = f_ref[
                        v, pl.ds(start, y_count, stride=z_cells), :
                    ].astype(bf16)
                at += y_count
            edges = lax.dot_general(
                pick, rows_of(f_ref, v, segments).astype(bf16), (((1,), (1,)), ((), ())),
                preferred_element_type=f32,
            )
            for turn in range(turns(n_a)):
                x_refs[turn][c : c + 1, v * size : (v + 1) * size] = jnp.where(
                    odd_a == turn, edges[1:2, :], edges[0:1, :]
                )
        for turn in range(turns(n_y)):
            y_refs[turn][v] = jnp.where(
                odd_y == turn, f_ref[v, rows - z_cells :, :], f_ref[v, :z_cells, :]
            )


def low_high(axis, count, halos):
    index = lax.axis_index(axis)
    odd = lax.rem(index, 2)
    a, b = halos[0], halos[-1]

    def pick(value_of):
        first, second = value_of(a), value_of(b)
        low = jnp.where(odd == 1, first, second)
        high = jnp.where(odd == 1, second, first)
        zero = jnp.zeros_like(low)
        return jnp.where(index > 0, low, zero), jnp.where(index < count - 1, high, zero)

    return pick


def mix_kernel(r_ref, after, out_ref):
    count = r_ref.shape[0]
    size = out_ref.shape[0]
    spread = jnp.where(
        lax.broadcasted_iota(jnp.int32, (size, count), 0) // SUB
        == lax.broadcasted_iota(jnp.int32, (size, count), 1),
        1.0,
        0.0,
    ).astype(bf16)
    scaled = (r_ref[...] * (new_share * time_step)).astype(bf16)
    left = lax.dot_general(spread, scaled, (((1,), (0,)), ((), ())), preferred_element_type=f32)
    both = lax.dot_general(
        left.astype(bf16), spread, (((1,), (1,)), ((), ())), preferred_element_type=f32
    )
    row = lax.broadcasted_iota(jnp.int32, (size, size), 0)
    col = lax.broadcasted_iota(jnp.int32, (size, size), 1)
    out_ref[...] = jnp.where(row % SUB == col % SUB, both, 0.0).astype(bf16)


def stencil_kernel(
    z_cells, counts, index, segments, has_prior, has_y, diffusion, f_hbm, s_hbm, vel_hbm, mix_ref, *rest
):
    n_y, n_z, parts = counts
    x_refs, rest = rest[: turns(parts)], rest[turns(parts) :]
    z_refs, rest = rest[: turns(n_z)], rest[turns(n_z) :]
    if has_y:
        y_refs, rest = rest[: turns(n_y)], rest[turns(n_y) :]
    rest = rest[1:] if has_prior else rest
    new_hbm, rest = rest[0], rest[1:]
    snaps, (padded, edge, zface, react, start_ref, vel_ref, new_ref, f_sem, in_sem, vel_sem, out_sem) = (
        rest[:parts], rest[parts:]
    )
    variables, rows, lanes = f_hbm.shape
    pad = -(-z_cells // 8) * 8
    span = segments[0][1] + 2 * pad
    tile = TILE
    chunk = sum(count for _, count in segments)
    me = lax.axis_index("ga")
    is_buffer = me == parts - 1

    loads, starts, winds = [], [], []
    for i, (first, count) in enumerate(segments):
        low, high = max(first - pad, 0), min(first + count + pad, rows)
        loads.append(
            pltpu.make_async_copy(
                f_hbm.at[:, pl.ds(low, high - low), :],
                padded.at[:, pl.ds(i * span + low - first + pad, high - low), :],
                f_sem.at[i],
            )
        )
        loads[-1].start()
    tile_rows = [first + k * tile for first, count in segments for k in range(count // tile)]
    for t, row in enumerate(tile_rows):
        source, target = pl.ds(row, tile), pl.ds(t * tile, tile)
        starts.append(
            pltpu.make_async_copy(s_hbm.at[:, source, :], start_ref.at[:, target, :], in_sem.at[t])
        )
        winds.append(
            pltpu.make_async_copy(vel_hbm.at[:, source, :], vel_ref.at[:, target, :], vel_sem.at[t])
        )
        starts[-1].start()
        winds[-1].start()

    put = corner_mask(lanes)
    side = lax.broadcasted_iota(jnp.int32, (8, chunk), 0)
    y_count = chunk // z_cells
    x_pair = low_high("ga", parts, x_refs)
    z_pair = low_high("gz", n_z, z_refs)
    for v in range(variables):
        first, second = x_pair(lambda ref: ref[index : index + 1, v * chunk : (v + 1) * chunk])
        first = jnp.broadcast_to(first, (8, chunk))
        second = jnp.broadcast_to(second, (8, chunk))
        both = jnp.where(side == 0, first, jnp.where(side == 1, second, 0.0)).astype(bf16)
        edge[v] = lax.dot_general(both, put, (((0,), (0,)), ((), ())), preferred_element_type=f32)
        first, second = z_pair(lambda ref: ref[v].astype(f32))
        zface[v, pl.ds(0, y_count, stride=z_cells), :] = first
        zface[v, pl.ds(z_cells - 1, y_count, stride=z_cells), :] = second
    for load in loads:
        load.wait()
    for i, (first, count) in enumerate(segments):
        if first == 0 or first + count == rows:
            low, high = low_high("gy", n_y, y_refs)(lambda ref: ref[...])
            if first == 0:
                padded[:, i * span + pad - z_cells : i * span + pad, :] = low
            else:
                padded[:, i * span + pad + count : i * span + pad + count + z_cells, :] = high

    rate = new_share * time_step
    group = variables // parts
    tiles = segments[0][1] // tile

    def out_copy(t):
        row = segments[0][0] + t * tile
        if len(segments) > 1:
            gap = segments[1][0] - segments[0][0] - segments[0][1]
            row = row + lax.div(t, tiles) * gap
        at = pl.multiple_of(t * tile, tile)
        return pltpu.make_async_copy(
            new_ref.at[:, pl.ds(at, tile), :],
            new_hbm.at[:, pl.ds(pl.multiple_of(row, 8), tile), :],
            out_sem.at[t],
        )

    def in_copies(t):
        row = segments[0][0] + t * tile
        if len(segments) > 1:
            gap = segments[1][0] - segments[0][0] - segments[0][1]
            row = row + lax.div(t, tiles) * gap
        source, target = pl.ds(pl.multiple_of(row, 8), tile), pl.ds(pl.multiple_of(t * tile, tile), tile)
        return (
            pltpu.make_async_copy(s_hbm.at[:, source, :], start_ref.at[:, target, :], in_sem.at[t]),
            pltpu.make_async_copy(vel_hbm.at[:, source, :], vel_ref.at[:, target, :], vel_sem.at[t]),
        )

    def body(t, carry):
        at = pl.multiple_of(t * tile, tile)
        base = pl.multiple_of(at + lax.div(t, tiles) * (2 * pad), 8)
        blocks = []
        for sub in range(tile // SUB):
            blocks.append(
                jnp.concatenate(
                    [padded[w, pl.ds(base + pad + sub * SUB, SUB), :].astype(bf16) for w in range(variables)],
                    axis=0,
                )
            )
        react[...] = jnp.dot(
            mix_ref[...], jnp.concatenate(blocks, axis=1), preferred_element_type=f32
        )
        for copy in in_copies(t):
            copy.wait()
        lane = lax.broadcasted_iota(jnp.int32, (tile, lanes), 1)
        z_at = lax.rem(lax.broadcasted_iota(jnp.int32, (tile, lanes), 0), z_cells)
        v_x = vel_ref[0, pl.ds(at, tile), :] * (0.5 * rate)
        v_y = vel_ref[1, pl.ds(at, tile), :] * (0.5 * rate)
        v_z = vel_ref[2, pl.ds(at, tile), :] * (0.5 * rate)
        for part in range(parts):
            target = lax.rem(me + part, parts)
            for j in range(group):
                v = target * group + j
                spread = diffusion[v] * rate
                center = padded[v, pl.ds(base + pad, tile), :]
                y_minus = padded[v, pl.ds(base + pad - z_cells, tile), :]
                y_plus = padded[v, pl.ds(base + pad + z_cells, tile), :]
                face = zface[v, pl.ds(at, tile), :]
                z_minus = jnp.where(z_at == 0, face, padded[v, pl.ds(base + pad - 1, tile), :])
                z_plus = jnp.where(z_at == z_cells - 1, face, padded[v, pl.ds(base + pad + 1, tile), :])
                sides = edge[v, pl.ds(at, tile), :]
                x_minus = jnp.where(lane == 0, sides, pltpu.roll(center, 1, 1))
                x_plus = jnp.where(lane == lanes - 1, sides, pltpu.roll(center, lanes - 1, 1))
                mixed = jnp.concatenate(
                    [
                        react[pl.ds(pl.multiple_of(v * SUB, SUB), SUB), sub * lanes : (sub + 1) * lanes]
                        for sub in range(tile // SUB)
                    ],
                    axis=0,
                )
                around = (y_plus + y_minus) + (z_plus + z_minus) + (x_plus + x_minus)
                carried = v_x * (x_plus - x_minus) + v_y * (y_plus - y_minus) + v_z * (z_plus - z_minus)
                value = (
                    old_share * start_ref[v, pl.ds(at, tile), :]
                    + (new_share - 6.0 * spread) * center
                    + (spread * around - carried)
                    + mixed
                )
                value = jnp.where(is_buffer, center, value)
                new_ref[v, pl.ds(at, tile), :] = value
                snaps[part][j, pl.ds(at, tile), :] = value.astype(bf16)
        out_copy(t).start()
        return carry

    lax.fori_loop(0, chunk // tile, body, 0)
    for t in range(chunk // tile):
        out_copy(t).wait()


def gather_rows(parts, me, pieces, wide):
    group, rows, lanes = pieces[0].shape
    for part in range(parts):
        source = lax.rem(me - part + parts, parts)
        at = pl.multiple_of(source * lanes, lanes)
        for j in range(group):
            wide[j * rows : (j + 1) * rows, pl.ds(at, lanes)] = pieces[part][j]


def project(z_cells, group, rows, xf_ref, wide, proj, store):
    y_cells = rows // z_cells
    proj[...] = lax.dot_general(
        wide[...], xf_ref[...], (((1,), (1,)), ((), ())), preferred_element_type=f32
    )
    for z in range(z_cells):
        cols = [proj[pl.ds(j * rows + z, y_cells, stride=z_cells), :] for j in range(group)]
        store(z, jnp.concatenate(cols, axis=1).astype(bf16))


def part_gram_kernel(z_cells, parts, has_prior, xf_ref, *refs):
    pieces, refs = refs[:parts], refs[parts:]
    if has_prior:
        prior, refs = refs[0], refs[1:]
    gram_ref, proj_ref, wide, proj = refs
    group, rows, _ = pieces[0].shape
    gather_rows(parts, lax.axis_index("ga"), pieces, wide)
    data = wide[...]
    gram = lax.dot_general(data, data, (((0,), (0,)), ((), ())), preferred_element_type=f32)
    gram_ref[...] = prior[...] + gram if has_prior else gram

    def store(z, value):
        proj_ref[z] = value

    project(z_cells, group, rows, xf_ref, wide, proj, store)


def last_gram_kernel(z_cells, parts, n_y, n_z, plan, xf_ref, *refs):
    priors = len(plan) - 1
    pieces, refs = refs[:parts], refs[parts:]
    prior, refs = refs[0], refs[1:]
    prior_proj, refs = refs[:priors], refs[priors:]
    outs, (wide, proj, gram, full) = refs[: n_y * n_z], refs[n_y * n_z :]
    group, rows, _ = pieces[0].shape
    me, my_y, my_z = (lax.axis_index(a) for a in ("ga", "gy", "gz"))
    gather_rows(parts, me, pieces, wide)

    def place(z, value, segments):
        at = 0
        for first, count in segments:
            y_count = count // z_cells
            full[z, first // z_cells : first // z_cells + y_count, :] = value[at : at + y_count]
            at += y_count

    project(z_cells, group, rows, xf_ref, wide, proj, lambda z, value: place(z, value, plan[-1]))
    for i in range(priors):
        for z in range(z_cells):
            place(z, prior_proj[i][z], plan[i])
    data = wide[...]
    gram[...] = prior[...] + lax.dot_general(
        data, data, (((0,), (0,)), ((), ())), preferred_element_type=f32
    )
    own = gram.shape[0] // (n_y * n_z)
    width = gram.shape[1]
    layers = z_cells // n_y
    cols = full.shape[2]
    for d_y in range(n_y):
        for d_z in range(n_z):
            out = outs[d_y * n_z + d_z]
            y_to, z_to = lax.rem(my_y + d_y, n_y), lax.rem(my_z + d_z, n_z)
            at = pl.multiple_of((y_to * n_z + z_to) * own, own)
            out[:own, :width] = gram[pl.ds(at, own), :].astype(bf16)
            if d_z == 0:
                for layer in range(layers):
                    out[: full.shape[1], width + layer * cols : width + (layer + 1) * cols] = full[
                        y_to * layers + layer
                    ]


def layer_kernel(n_y, n_z, own, layers, y_scale, x_scale, yf_ref, *refs):
    pieces, (out_ref, m_ref) = refs[: n_y * n_z], refs[n_y * n_z :]
    rank, y_size = yf_ref.shape
    y_cells = y_size // n_y
    cols = m_ref.shape[2]
    width = pieces[0].shape[1] - layers * cols
    my_y = lax.axis_index("gy")
    for d_y in range(n_y):
        source = lax.rem(my_y - d_y + n_y, n_y)
        at = pl.multiple_of(source * y_cells, y_cells)
        for layer in range(layers):
            m_ref[layer, pl.ds(at, y_cells), :] = pieces[d_y * n_z][
                :y_cells, width + layer * cols : width + (layer + 1) * cols
            ]
    for layer in range(layers):
        m = m_ref[layer]
        y_gram = lax.dot_general(m, m, (((1,), (1,)), ((), ())), preferred_element_type=f32) * y_scale
        prod = lax.dot_general(
            yf_ref[...], y_gram, (((1,), (0,)), ((), ())), preferred_element_type=f32,
            precision=lax.Precision.HIGHEST,
        )
        if own != rank:
            out_ref[...] = jnp.zeros_like(out_ref)
        out_ref[:rank, width + layer * y_size : width + (layer + 1) * y_size] = prod.astype(bf16)
    total = pieces[0][:own, :width].astype(f32)
    for i in range(1, n_y * n_z):
        total = total + pieces[i][:own, :width].astype(f32)
    out_ref[:own, :width] = (total * x_scale).astype(bf16)


def last_kernel(width, parts, *refs):
    pieces, (gram_ref, prod_ref) = refs[:parts], refs[parts:]
    total = pieces[0][...].astype(f32)
    for i in range(1, parts):
        total = total + pieces[i][...].astype(f32)
    gram_ref[...] = total[: gram_ref.shape[0], :width]
    layers, rank, y_size = prod_ref.shape
    for layer in range(layers):
        prod_ref[layer] = total[:rank, width + layer * y_size : width + (layer + 1) * y_size]


def call(kernel, out_shapes, in_specs, scratch=(), limit=16, flops=0, moved=0):
    return pl.pallas_call(
        kernel,
        out_shape=out_shapes,
        in_specs=in_specs,
        out_specs=[VMEM] * len(out_shapes),
        scratch_shapes=list(scratch),
        cost_estimate=pl.CostEstimate(flops=flops, bytes_accessed=moved, transcendentals=0),
        compiler_params=pltpu.CompilerParams(vmem_limit_bytes=limit * MIB),
    )


def shards(fields, section_start, velocity, diffusivity, reaction, x_factor, y_factor):
    variables, y_cells, z_cells, lanes = fields.shape
    rows = y_cells * z_cells
    n_y, n_z, n_a = (lax.axis_size(a) for a in ("gy", "gz", "ga"))
    g_y, g_z, _ = (lax.axis_index(a) for a in ("gy", "gz", "ga"))
    f = fields.reshape(variables, rows, lanes)
    s = section_start.reshape(variables, rows, lanes)
    vel = velocity.reshape(3, rows, lanes)
    x_size = n_a * lanes
    y_size = n_y * y_cells
    rank, y_rank = x_factor.shape[1], y_factor.shape[1]
    group = variables // n_a
    owners = n_y * n_z
    own = x_size // owners
    layers = z_cells // n_y
    pad = -(-z_cells // 8) * 8
    tile = TILE
    quarter = rows // 4
    plan = (((quarter, 2 * quarter),), ((0, quarter), (3 * quarter, quarter)))
    chunk = 2 * quarter
    y_part = chunk // z_cells
    counts = (n_y, n_z, n_a)
    in_hbm = functools.partial(pltpu.with_memory_space_constraint, memory_space=pltpu.HBM)
    packed = call(
        functools.partial(pack_kernel, z_cells, counts, plan),
        [sds((variables, z_cells, lanes), f32)] * turns(n_y)
        + [sds((len(plan), variables * chunk), f32)] * turns(n_a)
        + [sds((variables, y_part, lanes), bf16)] * (turns(n_z) * len(plan)),
        [ANY],
        scratch=[
            pltpu.VMEM((variables, rows, lanes), f32),
            pltpu.SemaphoreType.DMA((min(variables, 8),)),
        ],
        limit=12,
    )(in_hbm(f))
    y_faces, packed = packed[: turns(n_y)], packed[turns(n_y) :]
    x_edges, z_faces = packed[: turns(n_a)], packed[turns(n_a) :]

    def halo(axis, count, faces):
        return [lax.ppermute(face, axis, swap_pairs(count, turn)) for turn, face in enumerate(faces)]

    mix = call(
        mix_kernel, [sds((variables * SUB, variables * SUB), bf16)], [VMEM, ANY], limit=8
    )(reaction, y_faces[0])[0]

    def stencil(index, prior, x_halos, z_halos, y_halos):
        segments = plan[index]
        tiles = chunk // tile
        operands = [diffusivity, f, in_hbm(s), in_hbm(vel), mix, *x_halos, *z_halos, *y_halos]
        specs = [SMEM, ANY, ANY, ANY] + [VMEM] * (len(operands) - 4)
        aliases = {}
        if prior is not None:
            aliases = {len(operands): 0}
            operands.append(prior)
            specs.append(ANY)
        return pl.pallas_call(
            functools.partial(stencil_kernel, z_cells, counts, index, segments, prior is not None, bool(y_halos)),
            out_shape=[sds((variables, rows, lanes), f32)] + [sds((group, chunk, lanes), bf16)] * n_a,
            in_specs=specs,
            out_specs=[ANY] + [VMEM] * n_a,
            scratch_shapes=[
                pltpu.VMEM((variables, chunk + 2 * pad * len(segments), lanes), f32),
                pltpu.VMEM((variables, chunk, lanes), f32),
                pltpu.VMEM((variables, chunk, lanes), f32),
                pltpu.VMEM((variables * SUB, tile // SUB * lanes), f32),
                pltpu.VMEM((variables, chunk, lanes), f32),
                pltpu.VMEM((3, chunk, lanes), f32),
                pltpu.VMEM((variables, chunk, lanes), f32),
                pltpu.SemaphoreType.DMA((len(segments),)),
                pltpu.SemaphoreType.DMA((tiles,)),
                pltpu.SemaphoreType.DMA((tiles,)),
                pltpu.SemaphoreType.DMA((tiles,)),
            ],
            input_output_aliases=aliases,
            name="stencil",
            compiler_params=pltpu.CompilerParams(vmem_limit_bytes=20 * MIB),
        )(*operands)

    def exchange(snaps):
        received = [snaps[0]]
        for k in range(1, n_a):
            received.append(lax.ppermute(snaps[k], "ga", ring_pairs(n_a, k)))
        return received

    early_z, late_z = z_faces[: turns(n_z)], z_faces[turns(n_z) :]
    z_halos = halo("gz", n_z, early_z)
    x_halos = halo("ga", n_a, x_edges)
    results = stencil(0, None, x_halos, z_halos, ())
    new_fields = results[0]
    chunks = [exchange(results[1:])]
    y_faces, late_z, _ = lax.optimization_barrier((tuple(y_faces), tuple(late_z), results[2]))
    y_halos = halo("gy", n_y, y_faces)
    z_halos = halo("gz", n_z, late_z)
    results = stencil(1, new_fields, x_halos, z_halos, y_halos)
    new_fields = results[0]
    chunks.append(exchange(results[1:]))

    scratch = [pltpu.VMEM((group * chunk, x_size), bf16), pltpu.VMEM((group * chunk, rank), f32)]
    gram, projs = None, []
    direct = owners <= 8
    for index in range(len(plan) - 1 if direct else len(plan)):
        gram, proj = call(
            functools.partial(part_gram_kernel, z_cells, n_a, gram is not None),
            [sds((x_size, x_size), f32), sds((z_cells, y_part, group * rank), bf16)],
            [VMEM] * (n_a + 1 + (gram is not None)),
            scratch=scratch,
        )(x_factor.T, *chunks[index], *([] if gram is None else [gram]))
        projs.append(proj)
    cols = layers * group * rank
    piece_rows = max(own, y_cells)
    if direct:
        pieces = call(
            functools.partial(last_gram_kernel, z_cells, n_a, n_y, n_z, plan),
            [
                sds((piece_rows if d_z == 0 else own, x_size + (cols if d_z == 0 else 0)), bf16)
                for _ in range(n_y)
                for d_z in range(n_z)
            ],
            [VMEM] * (n_a + 2 + len(projs)),
            scratch=scratch
            + [pltpu.VMEM((x_size, x_size), f32), pltpu.VMEM((z_cells, y_cells, group * rank), bf16)],
        )(x_factor.T, *chunks[-1], gram, *projs)
        received = [pieces[0]]
        for d_y in range(n_y):
            for d_z in range(n_z):
                if d_y or d_z:
                    pairs = [
                        (y * n_z + z, (y + d_y) % n_y * n_z + (z + d_z) % n_z)
                        for y in range(n_y)
                        for z in range(n_z)
                    ]
                    received.append(lax.ppermute(pieces[d_y * n_z + d_z], ("gy", "gz"), pairs))
    else:
        half = quarter // z_cells
        proj = jnp.concatenate([projs[1][:, :half], projs[0], projs[1][:, half:]], axis=1)
        full = lax.all_to_all(
            proj.reshape(n_y, layers, y_cells, group * rank), "gy", split_axis=0, concat_axis=0, tiled=True
        )
        blocks = lax.all_to_all(
            gram.astype(bf16).reshape(owners, own, x_size), ("gy", "gz"), split_axis=0, concat_axis=0, tiled=True
        )
        full = full.transpose(0, 2, 1, 3).reshape(n_y, y_cells, cols)
        received = []
        for d_y in range(n_y):
            for d_z in range(n_z):
                source = (g_y - d_y + n_y) % n_y * n_z + (g_z - d_z + n_z) % n_z
                block = lax.dynamic_index_in_dim(blocks, source, 0, keepdims=False)
                if d_z == 0:
                    block = jnp.pad(block, ((0, piece_rows - own), (0, 0)))
                    side = lax.dynamic_index_in_dim(full, (g_y - d_y + n_y) % n_y, 0, keepdims=False)
                    side = jnp.pad(side, ((0, piece_rows - y_cells), (0, 0)))
                    block = jnp.concatenate([block, side], axis=1)
                received.append(block)
    payload = call(
        functools.partial(
            layer_kernel, n_y, n_z, own, layers, 1.0 / (variables * rank), 1.0 / (variables * rows * owners)
        ),
        [sds((max(own, y_rank), x_size + layers * y_size), bf16)],
        [VMEM] * (1 + owners),
        scratch=[pltpu.VMEM((layers, y_size, group * rank), bf16)],
    )(y_factor.T, *received)[0]
    payloads = [payload] + [lax.ppermute(payload, "ga", ring_pairs(n_a, k)) for k in range(1, n_a)]
    x_gram, products = call(
        functools.partial(last_kernel, x_size, n_a),
        [sds((own, x_size), f32), sds((layers, y_rank, y_size), f32)],
        [VMEM] * n_a,
        limit=8,
    )(*payloads)
    return (
        new_fields.reshape(fields.shape),
        x_gram,
        jnp.swapaxes(products, 1, 2),
    )


def solution(mesh):
    block = P(None, "gy", "gz", "ga")
    in_specs = (block, block, block, P(), P(), P(), P())
    out_specs = (block, P(("gy", "gz"), None), P(("gz", "gy"), None, None))

    return jax.shard_map(shards, mesh=mesh, in_specs=in_specs, out_specs=out_specs, check_vma=False)
```

profile of v0, /device:TPU:0, one launch (start us, length us, event | category | flops | bytes accessed | tf_op | source)
XLA Modules:
  0.0 69.4 jit_solution(15574650838194933447)
XLA Ops:
  0.7 2.7 %shard_map.94 = (f32[16,4,128]{2,1,0:T(4,128)S(1)}, f32[16,4,128]{2,1,0:T(4,128)S(1)}, f32[2,2048]{1,0:T(2,128)S(1)}, f32[2,2048]{1,0:T(2,128)S(1)}, bf16[16,32,...) custom-call(f32[16,256,128]{2,1,0:T(8,128)} %bitcast.7), custom_call_target="tpu_custom_call" | custom-call | tf_op jit(solution)/shard_map/pallas_call | solution.py:439
  3.4 3.1 %collective-permute-start.2 = (bf16[16,32,128]{2,1,0:T(8,128)(2,1)S(1)}, bf16[16,32,128]{2,1,0:T(8,128)(2,1)S(1)}, u32[]{:S(2)}, u32[]{:S(2)}) collective-permute-start(bf16[16,32,128]{2,1,0:T(8,128)(2,1)S(1)} %get-tuple-element.39), channel_id=1, source_target_pairs={{0,4},{4,0},{1,5},{5,1},{2,6},{6,2},{3,7},{7,3},{8,12},{12,8},{9,1... | collective-permute-start | bytes 393224 | tf_op jit(solution)/shard_map/ppermute | solution.py:455
  6.5 1.6 %collective-permute-start = (f32[2,2048]{1,0:T(2,128)S(1)}, f32[2,2048]{1,0:T(2,128)S(1)}, u32[]{:S(2)}, u32[]{:S(2)}) collective-permute-start(f32[2,2048]{1,0:T(2,128)S(1)} %get-tuple-element.35), channel_id=1, source_target_pairs={{0,1},{1,0},{2,3},{3,2},{4,5},{5,4},{6,7},{7,6},{8,9},{9,8},{10,11... | collective-permute-start | bytes 49160 | tf_op jit(solution)/shard_map/ppermute | solution.py:455
  8.0 2.5 %collective-permute-start.1 = (f32[2,2048]{1,0:T(2,128)S(1)}, f32[2,2048]{1,0:T(2,128)S(1)}, u32[]{:S(2)}, u32[]{:S(2)}) collective-permute-start(f32[2,2048]{1,0:T(2,128)S(1)} %get-tuple-element.36), channel_id=1, source_target_pairs={{0,3},{1,2},{2,1},{3,0},{4,7},{5,6},{6,5},{7,4},{8,11},{9,10},{10,... | collective-permute-start | bytes 49160 | tf_op jit(solution)/shard_map/ppermute | solution.py:455
  10.8 2.7 %collective-permute-done.1.rest_1_ = f32[2,2048]{1,0:T(2,128)S(1)} collective-permute-done((f32[2,2048]{1,0:T(2,128)S(1)}, f32[2,2048]{1,0:T(2,128)S(1)}, u32[]{:S(2)}, u32[]{:S(2)}) %collective-permute-start.1) | collective-permute-done | bytes 16416 | tf_op jit(solution)/shard_map/ppermute | solution.py:455
  13.6 4.2 %stencil.2 = (f32[16,256,128]{2,1,0:T(8,128)}, bf16[4,128,128]{2,1,0:T(8,128)(2,1)S(1)}, bf16[4,128,128]{2,1,0:T(8,128)(2,1)S(1)}, bf16[4,128,128]{2,1,0:T(8,128)(2,1)S(1)}, bf16[4,128,128]{2,1,0:T(8,128)(2,1)S(1)}) custom-call(f32[16]{0:T(128)S(1)} %copy-done.4, f32[16,256,128]{2,1,0:T(8,128)S(1)} %bitcast.8, f32[16,256,128]{2,1,0:T(8,128)} %bitcast.13, ...), custom_call_target="tpu_custom_call" | custom-call | tf_op jit(solution)/shard_map/stencil/pallas_call | solution.py:471
  19.2 1.6 %collective-permute-start.5 = (f32[16,4,128]{2,1,0:T(4,128)S(1)}, f32[16,4,128]{2,1,0:T(4,128)S(1)}, u32[]{:S(2)}, u32[]{:S(2)}) collective-permute-start(f32[16,4,128]{2,1,0:T(4,128)S(1)} %get-tuple-element.43), channel_id=1, source_target_pairs={{0,24},{8,16},{16,8},{24,0},{1,25},{9,17},{17,9},{25,1},{2,26},{10... | collective-permute-start | bytes 98312 | tf_op jit(solution)/shard_map/ppermute | solution.py:455
  20.8 2.3 %collective-permute-start.9 = (bf16[4,128,128]{2,1,0:T(8,128)(2,1)S(1)}, bf16[4,128,128]{2,1,0:T(8,128)(2,1)S(1)}, u32[]{:S(2)}, u32[]{:S(2)}) collective-permute-start(bf16[4,128,128]{2,1,0:T(8,128)(2,1)S(1)} %get-tuple-element.40), channel_id=1, source_target_pairs={{0,1},{1,2},{2,3},{3,0},{4,5},{5,6},{6,7},{7,4},{8,9},{9,10},{10,1... | collective-permute-start | bytes 393224 | tf_op jit(solution)/shard_map/ppermute | solution.py:497
  23.0 1.6 %collective-permute-start.11 = (bf16[4,128,128]{2,1,0:T(8,128)(2,1)S(1)}, bf16[4,128,128]{2,1,0:T(8,128)(2,1)S(1)}, u32[]{:S(2)}, u32[]{:S(2)}) collective-permute-start(bf16[4,128,128]{2,1,0:T(8,128)(2,1)S(1)} %get-tuple-element.52), channel_id=1, source_target_pairs={{0,3},{1,0},{2,1},{3,2},{4,7},{5,4},{6,5},{7,6},{8,11},{9,8},{10,9... | collective-permute-start | bytes 393224 | tf_op jit(solution)/shard_map/ppermute | solution.py:497
  24.6 4.2 %stencil.3 = (f32[16,256,128]{2,1,0:T(8,128)}, bf16[4,128,128]{2,1,0:T(8,128)(2,1)S(1)}, bf16[4,128,128]{2,1,0:T(8,128)(2,1)S(1)}, bf16[4,128,128]{2,1,0:T(8,128)(2,1)S(1)}, bf16[4,128,128]{2,1,0:T(8,128)(2,1)S(1)}) custom-call(f32[16]{0:T(128)S(1)} %copy-done.4, f32[16,256,128]{2,1,0:T(8,128)S(1)} %bitcast.9, ...), custom_call_target="tpu_custom_call", output_to_operand_aliasing={{0}: (10, {})} | custom-call | tf_op jit(solution)/shard_map/stencil/pallas_call | solution.py:471
  29.4 0.8 %collective-permute-start.7 = (bf16[4,128,128]{2,1,0:T(8,128)(2,1)S(1)}, bf16[4,128,128]{2,1,0:T(8,128)(2,1)S(1)}, u32[]{:S(2)}, u32[]{:S(2)}) collective-permute-start(bf16[4,128,128]{2,1,0:T(8,128)(2,1)S(1)} %get-tuple-element.48), channel_id=1, source_target_pairs={{0,2},{1,3},{2,0},{3,1},{4,6},{5,7},{6,4},{7,5},{8,10},{9,11},{10,... | collective-permute-start | bytes 393224 | tf_op jit(solution)/shard_map/ppermute | solution.py:497
  30.2 2.6 %collective-permute-start.8 = (bf16[4,128,128]{2,1,0:T(8,128)(2,1)S(1)}, bf16[4,128,128]{2,1,0:T(8,128)(2,1)S(1)}, u32[]{:S(2)}, u32[]{:S(2)}) collective-permute-start(bf16[4,128,128]{2,1,0:T(8,128)(2,1)S(1)} %get-tuple-element.49), channel_id=1, source_target_pairs={{0,3},{1,0},{2,1},{3,2},{4,7},{5,4},{6,5},{7,6},{8,11},{9,8},{10,9... | collective-permute-start | bytes 393224 | tf_op jit(solution)/shard_map/ppermute | solution.py:497
  32.8 0.8 %shard_map.96 = (f32[512,512]{1,0:T(8,128)S(1)}, bf16[4,32,256]{2,1,0:T(8,128)(2,1)S(1)}) custom-call(bf16[64,512]{1,0:T(8,128)(2,1)S(1)} %bitcast.10, bf16[4,128,128]{2,1,0:T(8,128)(2,1)S(1)} %get-tuple-element.50.refs_0_, bf16[4,128,128]{2,1,0:T(8,128)(2,1)S(1)} %collective-permute-done.9.refs_1_, ...), custom_call_target="tpu_custom_call" | custom-call | tf_op jit(solution)/shard_map/pallas_call | solution.py:517
  33.6 3.5 %collective-permute-done.6.refs_1_ = bf16[4,128,128]{2,1,0:T(8,128)(2,1)S(1)} collective-permute-done((bf16[4,128,128]{2,1,0:T(8,128)(2,1)S(1)}, bf16[4,128,128]{2,1,0:T(8,128)(2,1)S(1)}, u32[]{:S(2)}, u32[]{:S(2)}) %collective-permute-start.6) | collective-permute-done | bytes 131104 | tf_op jit(solution)/shard_map/ppermute | solution.py:497
  37.1 4.1 %collective-permute-done.7.refs_2_ = bf16[4,128,128]{2,1,0:T(8,128)(2,1)S(1)} collective-permute-done((bf16[4,128,128]{2,1,0:T(8,128)(2,1)S(1)}, bf16[4,128,128]{2,1,0:T(8,128)(2,1)S(1)}, u32[]{:S(2)}, u32[]{:S(2)}) %collective-permute-start.7) | collective-permute-done | bytes 131104 | tf_op jit(solution)/shard_map/ppermute | solution.py:497
  42.1 1.6 %collective-permute-start.12 = (bf16[64,512]{1,0:T(8,128)(2,1)S(1)}, bf16[64,512]{1,0:T(8,128)(2,1)S(1)}, u32[]{:S(2)}, u32[]{:S(2)}) collective-permute-start(bf16[64,512]{1,0:T(8,128)(2,1)S(1)} %get-tuple-element.56), channel_id=1, source_target_pairs={{0,4},{4,0},{8,12},{12,8},{16,20},{20,16},{24,28},{28,24},{1,5},{5... | collective-permute-start | bytes 196616 | tf_op jit(solution)/shard_map/ppermute | solution.py:547
  44.4 1.3 %collective-permute-start.15 = (bf16[64,768]{1,0:T(8,128)(2,1)S(1)}, bf16[64,768]{1,0:T(8,128)(2,1)S(1)}, u32[]{:S(2)}, u32[]{:S(2)}) collective-permute-start(bf16[64,768]{1,0:T(8,128)(2,1)S(1)} %get-tuple-element.59), channel_id=1, source_target_pairs={{0,16},{4,20},{8,24},{12,28},{16,0},{20,4},{24,8},{28,12},{1,17},{... | collective-permute-start | bytes 294920 | tf_op jit(solution)/shard_map/ppermute | solution.py:547
  46.4 1.7 %collective-permute-start.16 = (bf16[64,512]{1,0:T(8,128)(2,1)S(1)}, bf16[64,512]{1,0:T(8,128)(2,1)S(1)}, u32[]{:S(2)}, u32[]{:S(2)}) collective-permute-start(bf16[64,512]{1,0:T(8,128)(2,1)S(1)} %get-tuple-element.60), channel_id=1, source_target_pairs={{0,20},{4,16},{8,28},{12,24},{16,4},{20,0},{24,12},{28,8},{1,21},{... | collective-permute-start | bytes 196616 | tf_op jit(solution)/shard_map/ppermute | solution.py:547
  48.2 1.0 %collective-permute-start.18 = (bf16[64,512]{1,0:T(8,128)(2,1)S(1)}, bf16[64,512]{1,0:T(8,128)(2,1)S(1)}, u32[]{:S(2)}, u32[]{:S(2)}) collective-permute-start(bf16[64,512]{1,0:T(8,128)(2,1)S(1)} %get-tuple-element.62), channel_id=1, source_target_pairs={{0,28},{4,24},{8,4},{12,0},{16,12},{20,8},{24,20},{28,16},{1,29},{... | collective-permute-start | bytes 196616 | tf_op jit(solution)/shard_map/ppermute | solution.py:547
  49.2 4.7 %collective-permute-done.16.refs_5_ = bf16[64,512]{1,0:T(8,128)(2,1)S(1)} collective-permute-done((bf16[64,512]{1,0:T(8,128)(2,1)S(1)}, bf16[64,512]{1,0:T(8,128)(2,1)S(1)}, u32[]{:S(2)}, u32[]{:S(2)}) %collective-permute-start.16) | collective-permute-done | bytes 65568 | tf_op jit(solution)/shard_map/ppermute | solution.py:547
  54.4 3.0 %collective-permute-start.21 = (bf16[64,768]{1,0:T(8,128)(2,1)S(1)}, bf16[64,768]{1,0:T(8,128)(2,1)S(1)}, u32[]{:S(2)}, u32[]{:S(2)}) collective-permute-start(bf16[64,768]{1,0:T(8,128)(2,1)S(1)} %shard_map.98.refs_0_), channel_id=1, source_target_pairs={{0,3},{1,0},{2,1},{3,2},{4,7},{5,4},{6,5},{7,6},{8,11},{9,8},{10,9... | collective-permute-start | bytes 294920 | tf_op jit(solution)/shard_map/ppermute | solution.py:577
  57.5 1.7 %collective-permute-start.20 = (bf16[64,768]{1,0:T(8,128)(2,1)S(1)}, bf16[64,768]{1,0:T(8,128)(2,1)S(1)}, u32[]{:S(2)}, u32[]{:S(2)}) collective-permute-start(bf16[64,768]{1,0:T(8,128)(2,1)S(1)} %shard_map.98.refs_0_), channel_id=1, source_target_pairs={{0,2},{1,3},{2,0},{3,1},{4,6},{5,7},{6,4},{7,5},{8,10},{9,11},{10,... | collective-permute-start | bytes 294920 | tf_op jit(solution)/shard_map/ppermute | solution.py:577
  59.2 2.0 %collective-permute-done.21.refs_3_ = bf16[64,768]{1,0:T(8,128)(2,1)S(1)} collective-permute-done((bf16[64,768]{1,0:T(8,128)(2,1)S(1)}, bf16[64,768]{1,0:T(8,128)(2,1)S(1)}, u32[]{:S(2)}, u32[]{:S(2)}) %collective-permute-start.21) | collective-permute-done | bytes 98336 | tf_op jit(solution)/shard_map/ppermute | solution.py:577
  61.2 7.5 %collective-permute-done.20.refs_2_ = bf16[64,768]{1,0:T(8,128)(2,1)S(1)} collective-permute-done((bf16[64,768]{1,0:T(8,128)(2,1)S(1)}, bf16[64,768]{1,0:T(8,128)(2,1)S(1)}, u32[]{:S(2)}, u32[]{:S(2)}) %collective-permute-start.20) | collective-permute-done | bytes 98336 | tf_op jit(solution)/shard_map/ppermute | solution.py:577
  (38 shorter events, 5.8 us)
Async XLA Ops:
  0.6 13.0 %copy-start = (f32[16,64,4,128]{3,2,1,0:T(4,128)S(1)}, f32[16,64,4,128]{3,2,1,0:T(4,128)}, u32[]{:S(2)}) copy-start(f32[16,64,4,128]{3,2,1,0:T(4,128)} %param.7) | copy-start | bytes 6291460
  3.4 10.2 %collective-permute-start.2 = (bf16[16,32,128]{2,1,0:T(8,128)(2,1)S(1)}, bf16[16,32,128]{2,1,0:T(8,128)(2,1)S(1)}, u32[]{:S(2)}, u32[]{:S(2)}) collective-permute-start(bf16[16,32,128]{2,1,0:T(8,128)(2,1)S(1)} %get-tuple-element.39), channel_id=1, source_target_pairs={{0,4},{4,0},{1,5},{5,1},{2,6},{6,2},{3,7},{7,3},{8,12},{12,8},{9,1... | collective-permute-start | bytes 393224 | tf_op jit(solution)/shard_map/ppermute | solution.py:455
  6.5 4.4 %collective-permute-start = (f32[2,2048]{1,0:T(2,128)S(1)}, f32[2,2048]{1,0:T(2,128)S(1)}, u32[]{:S(2)}, u32[]{:S(2)}) collective-permute-start(f32[2,2048]{1,0:T(2,128)S(1)} %get-tuple-element.35), channel_id=1, source_target_pairs={{0,1},{1,0},{2,3},{3,2},{4,5},{5,4},{6,7},{7,6},{8,9},{9,8},{10,11... | collective-permute-start | bytes 49160 | tf_op jit(solution)/shard_map/ppermute | solution.py:455
  8.0 5.5 %collective-permute-start.1 = (f32[2,2048]{1,0:T(2,128)S(1)}, f32[2,2048]{1,0:T(2,128)S(1)}, u32[]{:S(2)}, u32[]{:S(2)}) collective-permute-start(f32[2,2048]{1,0:T(2,128)S(1)} %get-tuple-element.36), channel_id=1, source_target_pairs={{0,3},{1,2},{2,1},{3,0},{4,7},{5,6},{6,5},{7,4},{8,11},{9,10},{10,... | collective-permute-start | bytes 49160 | tf_op jit(solution)/shard_map/ppermute | solution.py:455
  17.8 6.8 %collective-permute-start.3 = (bf16[16,32,128]{2,1,0:T(8,128)(2,1)S(1)}, bf16[16,32,128]{2,1,0:T(8,128)(2,1)S(1)}, u32[]{:S(2)}, u32[]{:S(2)}) collective-permute-start(bf16[16,32,128]{2,1,0:T(8,128)(2,1)S(1)} %get-tuple-element.41), channel_id=1, source_target_pairs={{0,4},{4,0},{1,5},{5,1},{2,6},{6,2},{3,7},{7,3},{8,12},{12,8},{9,1... | collective-permute-start | bytes 393224 | tf_op jit(solution)/shard_map/ppermute | solution.py:455
  18.4 11.8 %collective-permute-start.10 = (bf16[4,128,128]{2,1,0:T(8,128)(2,1)S(1)}, bf16[4,128,128]{2,1,0:T(8,128)(2,1)S(1)}, u32[]{:S(2)}, u32[]{:S(2)}) collective-permute-start(bf16[4,128,128]{2,1,0:T(8,128)(2,1)S(1)} %get-tuple-element.51), channel_id=1, source_target_pairs={{0,2},{1,3},{2,0},{3,1},{4,6},{5,7},{6,4},{7,5},{8,10},{9,11},{10,... | collective-permute-start | bytes 393224 | tf_op jit(solution)/shard_map/ppermute | solution.py:497
  19.2 3.9 %collective-permute-start.4 = (f32[16,4,128]{2,1,0:T(4,128)S(1)}, f32[16,4,128]{2,1,0:T(4,128)S(1)}, u32[]{:S(2)}, u32[]{:S(2)}) collective-permute-start(f32[16,4,128]{2,1,0:T(4,128)S(1)} %get-tuple-element.42.after), channel_id=1, source_target_pairs={{0,8},{8,0},{16,24},{24,16},{1,9},{9,1},{17,25},{25,17},{2,10},{10... | collective-permute-start | bytes 98312 | tf_op jit(solution)/shard_map/ppermute | solution.py:455
  19.2 5.4 %collective-permute-start.5 = (f32[16,4,128]{2,1,0:T(4,128)S(1)}, f32[16,4,128]{2,1,0:T(4,128)S(1)}, u32[]{:S(2)}, u32[]{:S(2)}) collective-permute-start(f32[16,4,128]{2,1,0:T(4,128)S(1)} %get-tuple-element.43), channel_id=1, source_target_pairs={{0,24},{8,16},{16,8},{24,0},{1,25},{9,17},{17,9},{25,1},{2,26},{10... | collective-permute-start | bytes 98312 | tf_op jit(solution)/shard_map/ppermute | solution.py:455
  20.8 12.0 %collective-permute-start.9 = (bf16[4,128,128]{2,1,0:T(8,128)(2,1)S(1)}, bf16[4,128,128]{2,1,0:T(8,128)(2,1)S(1)}, u32[]{:S(2)}, u32[]{:S(2)}) collective-permute-start(bf16[4,128,128]{2,1,0:T(8,128)(2,1)S(1)} %get-tuple-element.40), channel_id=1, source_target_pairs={{0,1},{1,2},{2,3},{3,0},{4,5},{5,6},{6,7},{7,4},{8,9},{9,10},{10,1... | collective-permute-start | bytes 393224 | tf_op jit(solution)/shard_map/ppermute | solution.py:497
  23.0 9.7 %collective-permute-start.11 = (bf16[4,128,128]{2,1,0:T(8,128)(2,1)S(1)}, bf16[4,128,128]{2,1,0:T(8,128)(2,1)S(1)}, u32[]{:S(2)}, u32[]{:S(2)}) collective-permute-start(bf16[4,128,128]{2,1,0:T(8,128)(2,1)S(1)} %get-tuple-element.52), channel_id=1, source_target_pairs={{0,3},{1,0},{2,1},{3,2},{4,7},{5,4},{6,5},{7,6},{8,11},{9,8},{10,9... | collective-permute-start | bytes 393224 | tf_op jit(solution)/shard_map/ppermute | solution.py:497
  28.9 25.0 %copy-start.2 = (f32[256,64]{0,1:T(8,128)S(1)}, f32[256,64]{0,1:T(8,128)}, u32[]{:S(2)}) copy-start(f32[256,64]{0,1:T(8,128)} %param.13) | copy-start | bytes 196612
  28.9 8.3 %collective-permute-start.6 = (bf16[4,128,128]{2,1,0:T(8,128)(2,1)S(1)}, bf16[4,128,128]{2,1,0:T(8,128)(2,1)S(1)}, u32[]{:S(2)}, u32[]{:S(2)}) collective-permute-start(bf16[4,128,128]{2,1,0:T(8,128)(2,1)S(1)} %get-tuple-element.47), channel_id=1, source_target_pairs={{0,1},{1,2},{2,3},{3,0},{4,5},{5,6},{6,7},{7,4},{8,9},{9,10},{10,1... | collective-permute-start | bytes 393224 | tf_op jit(solution)/shard_map/ppermute | solution.py:497
  29.4 11.9 %collective-permute-start.7 = (bf16[4,128,128]{2,1,0:T(8,128)(2,1)S(1)}, bf16[4,128,128]{2,1,0:T(8,128)(2,1)S(1)}, u32[]{:S(2)}, u32[]{:S(2)}) collective-permute-start(bf16[4,128,128]{2,1,0:T(8,128)(2,1)S(1)} %get-tuple-element.48), channel_id=1, source_target_pairs={{0,2},{1,3},{2,0},{3,1},{4,6},{5,7},{6,4},{7,5},{8,10},{9,11},{10,... | collective-permute-start | bytes 393224 | tf_op jit(solution)/shard_map/ppermute | solution.py:497
  30.2 11.1 %collective-permute-start.8 = (bf16[4,128,128]{2,1,0:T(8,128)(2,1)S(1)}, bf16[4,128,128]{2,1,0:T(8,128)(2,1)S(1)}, u32[]{:S(2)}, u32[]{:S(2)}) collective-permute-start(bf16[4,128,128]{2,1,0:T(8,128)(2,1)S(1)} %get-tuple-element.49), channel_id=1, source_target_pairs={{0,3},{1,0},{2,1},{3,2},{4,7},{5,4},{6,5},{7,6},{8,11},{9,8},{10,9... | collective-permute-start | bytes 393224 | tf_op jit(solution)/shard_map/ppermute | solution.py:497
  42.1 4.3 %collective-permute-start.12 = (bf16[64,512]{1,0:T(8,128)(2,1)S(1)}, bf16[64,512]{1,0:T(8,128)(2,1)S(1)}, u32[]{:S(2)}, u32[]{:S(2)}) collective-permute-start(bf16[64,512]{1,0:T(8,128)(2,1)S(1)} %get-tuple-element.56), channel_id=1, source_target_pairs={{0,4},{4,0},{8,12},{12,8},{16,20},{20,16},{24,28},{28,24},{1,5},{5... | collective-permute-start | bytes 196616 | tf_op jit(solution)/shard_map/ppermute | solution.py:547
  43.6 4.6 %collective-permute-start.14 = (bf16[64,512]{1,0:T(8,128)(2,1)S(1)}, bf16[64,512]{1,0:T(8,128)(2,1)S(1)}, u32[]{:S(2)}, u32[]{:S(2)}) collective-permute-start(bf16[64,512]{1,0:T(8,128)(2,1)S(1)} %get-tuple-element.58), channel_id=1, source_target_pairs={{0,12},{4,8},{8,20},{12,16},{16,28},{20,24},{24,4},{28,0},{1,13},{... | collective-permute-start | bytes 196616 | tf_op jit(solution)/shard_map/ppermute | solution.py:547
  43.6 10.2 %collective-permute-start.13 = (bf16[64,768]{1,0:T(8,128)(2,1)S(1)}, bf16[64,768]{1,0:T(8,128)(2,1)S(1)}, u32[]{:S(2)}, u32[]{:S(2)}) collective-permute-start(bf16[64,768]{1,0:T(8,128)(2,1)S(1)} %get-tuple-element.57), channel_id=1, source_target_pairs={{0,8},{4,12},{8,16},{12,20},{16,24},{20,28},{24,0},{28,4},{1,9},{5... | collective-permute-start | bytes 294920 | tf_op jit(solution)/shard_map/ppermute | solution.py:547
  44.4 9.4 %collective-permute-start.15 = (bf16[64,768]{1,0:T(8,128)(2,1)S(1)}, bf16[64,768]{1,0:T(8,128)(2,1)S(1)}, u32[]{:S(2)}, u32[]{:S(2)}) collective-permute-start(bf16[64,768]{1,0:T(8,128)(2,1)S(1)} %get-tuple-element.59), channel_id=1, source_target_pairs={{0,16},{4,20},{8,24},{12,28},{16,0},{20,4},{24,8},{28,12},{1,17},{... | collective-permute-start | bytes 294920 | tf_op jit(solution)/shard_map/ppermute | solution.py:547
  45.7 8.1 %collective-permute-start.17 = (bf16[64,768]{1,0:T(8,128)(2,1)S(1)}, bf16[64,768]{1,0:T(8,128)(2,1)S(1)}, u32[]{:S(2)}, u32[]{:S(2)}) collective-permute-start(bf16[64,768]{1,0:T(8,128)(2,1)S(1)} %get-tuple-element.61), channel_id=1, source_target_pairs={{0,24},{4,28},{8,0},{12,4},{16,8},{20,12},{24,16},{28,20},{1,25},{... | collective-permute-start | bytes 294920 | tf_op jit(solution)/shard_map/ppermute | solution.py:547
  46.4 7.5 %collective-permute-start.16 = (bf16[64,512]{1,0:T(8,128)(2,1)S(1)}, bf16[64,512]{1,0:T(8,128)(2,1)S(1)}, u32[]{:S(2)}, u32[]{:S(2)}) collective-permute-start(bf16[64,512]{1,0:T(8,128)(2,1)S(1)} %get-tuple-element.60), channel_id=1, source_target_pairs={{0,20},{4,16},{8,28},{12,24},{16,4},{20,0},{24,12},{28,8},{1,21},{... | collective-permute-start | bytes 196616 | tf_op jit(solution)/shard_map/ppermute | solution.py:547
  48.2 5.6 %collective-permute-start.18 = (bf16[64,512]{1,0:T(8,128)(2,1)S(1)}, bf16[64,512]{1,0:T(8,128)(2,1)S(1)}, u32[]{:S(2)}, u32[]{:S(2)}) collective-permute-start(bf16[64,512]{1,0:T(8,128)(2,1)S(1)} %get-tuple-element.62), channel_id=1, source_target_pairs={{0,28},{4,24},{8,4},{12,0},{16,12},{20,8},{24,20},{28,16},{1,29},{... | collective-permute-start | bytes 196616 | tf_op jit(solution)/shard_map/ppermute | solution.py:547
  54.4 6.8 %collective-permute-start.21 = (bf16[64,768]{1,0:T(8,128)(2,1)S(1)}, bf16[64,768]{1,0:T(8,128)(2,1)S(1)}, u32[]{:S(2)}, u32[]{:S(2)}) collective-permute-start(bf16[64,768]{1,0:T(8,128)(2,1)S(1)} %shard_map.98.refs_0_), channel_id=1, source_target_pairs={{0,3},{1,0},{2,1},{3,2},{4,7},{5,4},{6,5},{7,6},{8,11},{9,8},{10,9... | collective-permute-start | bytes 294920 | tf_op jit(solution)/shard_map/ppermute | solution.py:577
  57.5 11.2 %collective-permute-start.20 = (bf16[64,768]{1,0:T(8,128)(2,1)S(1)}, bf16[64,768]{1,0:T(8,128)(2,1)S(1)}, u32[]{:S(2)}, u32[]{:S(2)}) collective-permute-start(bf16[64,768]{1,0:T(8,128)(2,1)S(1)} %shard_map.98.refs_0_), channel_id=1, source_target_pairs={{0,2},{1,3},{2,0},{3,1},{4,6},{5,7},{6,4},{7,5},{8,10},{9,11},{10,... | collective-permute-start | bytes 294920 | tf_op jit(solution)/shard_map/ppermute | solution.py:577
  59.2 9.5 %collective-permute-start.19 = (bf16[64,768]{1,0:T(8,128)(2,1)S(1)}, bf16[64,768]{1,0:T(8,128)(2,1)S(1)}, u32[]{:S(2)}, u32[]{:S(2)}) collective-permute-start(bf16[64,768]{1,0:T(8,128)(2,1)S(1)} %shard_map.98.refs_0_), channel_id=1, source_target_pairs={{0,1},{1,2},{2,3},{3,0},{4,5},{5,6},{6,7},{7,4},{8,9},{9,10},{10,1... | collective-permute-start | bytes 294920 | tf_op jit(solution)/shard_map/ppermute | solution.py:577
  (3 other events, 31.0 us)
where the time goes:
time: 69.6 us; the launch traced here: 69.4 us
  starting transfers between devices  29 us (42%)
  waiting for transfers between devices  25.3 us (36%)
  Pallas kernels  14.3 us (21%)
  between operations  0.76 us (1%)
    ppermute x3, waiting for transfers between devices, shards(): lax.ppermute(payload, 'ga', ring_pairs(n_a, k))  9.5 us
    ppermute x6, starting transfers between devices, halo(): lax.ppermute(face, axis, swap_pairs(count, turn))  9.29 us
    ppermute x6, starting transfers between devices, exchange(): received.append(lax.ppermute(snaps[k], 'ga', ring_pairs(n_a, k)))  8.49 us
    pallas_call x2, Pallas kernels, stencil(): pl.pallas_call(functools.partial(stencil_kernel, z_cells, counts, index,...  8.46 us
    ppermute x6, waiting for transfers between devices, exchange(): received.append(lax.ppermute(snaps[k], 'ga', ring_pairs(n_a, k)))  7.69 us
    ppermute x7, starting transfers between devices, shards(): received.append(lax.ppermute(pieces[d_y * n_z + d_z], ('gy', 'gz'), pairs))  6.41 us
    ppermute x7, waiting for transfers between devices, shards(): received.append(lax.ppermute(pieces[d_y * n_z + d_z], ('gy', 'gz'), pairs))  5.39 us
    ppermute x3, starting transfers between devices, shards(): lax.ppermute(payload, 'ga', ring_pairs(n_a, k))  4.78 us
  transfers between devices with their start and end apart: 22, of which 8 were waited for; matrix products, arithmetic and copies ran while one was open for 0% of the time, Pallas kernels for 8%

commit v1 on v0

--- a/solution.py
+++ b/solution.py
@@ -47,7 +47,7 @@
 
 
 def pack_kernel(z_cells, counts, plan, f_hbm, *refs):
-    outs, (f_ref, sem) = refs[:-2], refs[-2:]
+    f_ref, outs, sem = refs[0], refs[1:-1], refs[-1]
     variables, rows, lanes = f_ref.shape
     n_y, n_z, n_a = counts
     n_sem = sem.shape[0]
@@ -127,7 +127,7 @@
 
 
 def stencil_kernel(
-    z_cells, counts, index, segments, has_prior, has_y, diffusion, f_hbm, s_hbm, vel_hbm, mix_ref, *rest
+    z_cells, counts, index, segments, has_prior, has_y, diffusion, s_hbm, vel_hbm, f_ref, mix_ref, *rest
 ):
     n_y, n_z, parts = counts
     x_refs, rest = rest[: turns(parts)], rest[turns(parts) :]
@@ -136,37 +136,23 @@
         y_refs, rest = rest[: turns(n_y)], rest[turns(n_y) :]
     rest = rest[1:] if has_prior else rest
     new_hbm, rest = rest[0], rest[1:]
-    snaps, (padded, edge, zface, react, start_ref, vel_ref, new_ref, f_sem, in_sem, vel_sem, out_sem) = (
+    snaps, (ends, edge, zface, react, start_ref, vel_ref, new_ref, in_sem, vel_sem, out_sem) = (
         rest[:parts], rest[parts:]
     )
-    variables, rows, lanes = f_hbm.shape
+    variables, rows, lanes = f_ref.shape
     pad = -(-z_cells // 8) * 8
-    span = segments[0][1] + 2 * pad
     tile = TILE
     chunk = sum(count for _, count in segments)
     me = lax.axis_index("ga")
     is_buffer = me == parts - 1
 
-    loads, starts, winds = [], [], []
-    for i, (first, count) in enumerate(segments):
-        low, high = max(first - pad, 0), min(first + count + pad, rows)
-        loads.append(
-            pltpu.make_async_copy(
-                f_hbm.at[:, pl.ds(low, high - low), :],
-                padded.at[:, pl.ds(i * span + low - first + pad, high - low), :],
-                f_sem.at[i],
-            )
-        )
-        loads[-1].start()
+    starts, winds, writes = [], [], []
     tile_rows = [first + k * tile for first, count in segments for k in range(count // tile)]
     for t, row in enumerate(tile_rows):
-        source, target = pl.ds(row, tile), pl.ds(t * tile, tile)
-        starts.append(
-            pltpu.make_async_copy(s_hbm.at[:, source, :], start_ref.at[:, target, :], in_sem.at[t])
-        )
-        winds.append(
-            pltpu.make_async_copy(vel_hbm.at[:, source, :], vel_ref.at[:, target, :], vel_sem.at[t])
-        )
+        there, here = pl.ds(row, tile), pl.ds(t * tile, tile)
+        starts.append(pltpu.make_async_copy(s_hbm.at[:, there, :], start_ref.at[:, here, :], in_sem.at[t]))
+        winds.append(pltpu.make_async_copy(vel_hbm.at[:, there, :], vel_ref.at[:, here, :], vel_sem.at[t]))
+        writes.append(pltpu.make_async_copy(new_ref.at[:, here, :], new_hbm.at[:, there, :], out_sem.at[t]))
         starts[-1].start()
         winds[-1].start()
 
@@ -184,102 +170,74 @@
         first, second = z_pair(lambda ref: ref[v].astype(f32))
         zface[v, pl.ds(0, y_count, stride=z_cells), :] = first
         zface[v, pl.ds(z_cells - 1, y_count, stride=z_cells), :] = second
-    for load in loads:
-        load.wait()
-    for i, (first, count) in enumerate(segments):
-        if first == 0 or first + count == rows:
-            low, high = low_high("gy", n_y, y_refs)(lambda ref: ref[...])
-            if first == 0:
-                padded[:, i * span + pad - z_cells : i * span + pad, :] = low
-            else:
-                padded[:, i * span + pad + count : i * span + pad + count + z_cells, :] = high
+    if has_y:
+        low, high = low_high("gy", n_y, y_refs)(lambda ref: ref[...])
+        ends[0, :, pad - z_cells : pad, :] = low
+        ends[0, :, pad:, :] = f_ref[:, : tile + pad, :]
+        ends[1, :, : tile + pad, :] = f_ref[:, rows - tile - pad :, :]
+        ends[1, :, tile + pad : tile + pad + z_cells, :] = high
 
     rate = new_share * time_step
     group = variables // parts
-    tiles = segments[0][1] // tile
-
-    def out_copy(t):
-        row = segments[0][0] + t * tile
-        if len(segments) > 1:
-            gap = segments[1][0] - segments[0][0] - segments[0][1]
-            row = row + lax.div(t, tiles) * gap
-        at = pl.multiple_of(t * tile, tile)
-        return pltpu.make_async_copy(
-            new_ref.at[:, pl.ds(at, tile), :],
-            new_hbm.at[:, pl.ds(pl.multiple_of(row, 8), tile), :],
-            out_sem.at[t],
-        )
-
-    def in_copies(t):
-        row = segments[0][0] + t * tile
-        if len(segments) > 1:
-            gap = segments[1][0] - segments[0][0] - segments[0][1]
-            row = row + lax.div(t, tiles) * gap
-        source, target = pl.ds(pl.multiple_of(row, 8), tile), pl.ds(pl.multiple_of(t * tile, tile), tile)
-        return (
-            pltpu.make_async_copy(s_hbm.at[:, source, :], start_ref.at[:, target, :], in_sem.at[t]),
-            pltpu.make_async_copy(vel_hbm.at[:, source, :], vel_ref.at[:, target, :], vel_sem.at[t]),
-        )
-
-    def body(t, carry):
-        at = pl.multiple_of(t * tile, tile)
-        base = pl.multiple_of(at + lax.div(t, tiles) * (2 * pad), 8)
+    lane = lax.broadcasted_iota(jnp.int32, (SUB, lanes), 1)
+    z_at = lax.rem(lax.broadcasted_iota(jnp.int32, (SUB, lanes), 0), z_cells)
+    for t, row in enumerate(tile_rows):
+        slot = t % 2
         blocks = []
         for sub in range(tile // SUB):
+            at = row + sub * SUB
             blocks.append(
-                jnp.concatenate(
-                    [padded[w, pl.ds(base + pad + sub * SUB, SUB), :].astype(bf16) for w in range(variables)],
-                    axis=0,
-                )
+                jnp.concatenate([f_ref[w, at : at + SUB, :].astype(bf16) for w in range(variables)], axis=0)
             )
-        react[...] = jnp.dot(
-            mix_ref[...], jnp.concatenate(blocks, axis=1), preferred_element_type=f32
-        )
-        for copy in in_copies(t):
-            copy.wait()
-        lane = lax.broadcasted_iota(jnp.int32, (tile, lanes), 1)
-        z_at = lax.rem(lax.broadcasted_iota(jnp.int32, (tile, lanes), 0), z_cells)
-        v_x = vel_ref[0, pl.ds(at, tile), :] * (0.5 * rate)
-        v_y = vel_ref[1, pl.ds(at, tile), :] * (0.5 * rate)
-        v_z = vel_ref[2, pl.ds(at, tile), :] * (0.5 * rate)
-        for part in range(parts):
-            target = lax.rem(me + part, parts)
-            for j in range(group):
-                v = target * group + j
-                spread = diffusion[v] * rate
-                center = padded[v, pl.ds(base + pad, tile), :]
-                y_minus = padded[v, pl.ds(base + pad - z_cells, tile), :]
-                y_plus = padded[v, pl.ds(base + pad + z_cells, tile), :]
-                face = zface[v, pl.ds(at, tile), :]
-                z_minus = jnp.where(z_at == 0, face, padded[v, pl.ds(base + pad - 1, tile), :])
-                z_plus = jnp.where(z_at == z_cells - 1, face, padded[v, pl.ds(base + pad + 1, tile), :])
-                sides = edge[v, pl.ds(at, tile), :]
-                x_minus = jnp.where(lane == 0, sides, pltpu.roll(center, 1, 1))
-                x_plus = jnp.where(lane == lanes - 1, sides, pltpu.roll(center, lanes - 1, 1))
-                mixed = jnp.concatenate(
-                    [
-                        react[pl.ds(pl.multiple_of(v * SUB, SUB), SUB), sub * lanes : (sub + 1) * lanes]
-                        for sub in range(tile // SUB)
-                    ],
-                    axis=0,
-                )
-                around = (y_plus + y_minus) + (z_plus + z_minus) + (x_plus + x_minus)
-                carried = v_x * (x_plus - x_minus) + v_y * (y_plus - y_minus) + v_z * (z_plus - z_minus)
-                value = (
-                    old_share * start_ref[v, pl.ds(at, tile), :]
-                    + (new_share - 6.0 * spread) * center
-                    + (spread * around - carried)
-                    + mixed
-                )
-                value = jnp.where(is_buffer, center, value)
-                new_ref[v, pl.ds(at, tile), :] = value
-                snaps[part][j, pl.ds(at, tile), :] = value.astype(bf16)
-        out_copy(t).start()
-        return carry
-
-    lax.fori_loop(0, chunk // tile, body, 0)
-    for t in range(chunk // tile):
-        out_copy(t).wait()
+        react[slot] = jnp.dot(mix_ref[...], jnp.concatenate(blocks, axis=1), preferred_element_type=f32)
+        starts[t].wait()
+        winds[t].wait()
+        for sub in range(tile // SUB):
+            at, here = row + sub * SUB, t * tile + sub * SUB
+
+            def rows_at(v, offset):
+                if row == 0:
+                    return ends[0, v, pad + sub * SUB + offset : pad + (sub + 1) * SUB + offset, :]
+                if row == rows - tile:
+                    return ends[1, v, pad + sub * SUB + offset : pad + (sub + 1) * SUB + offset, :]
+                return f_ref[v, at + offset : at + SUB + offset, :]
+
+            v_x = vel_ref[0, here : here + SUB, :] * (0.5 * rate)
+            v_y = vel_ref[1, here : here + SUB, :] * (0.5 * rate)
+            v_z = vel_ref[2, here : here + SUB, :] * (0.5 * rate)
+            for part in range(parts):
+                target = lax.rem(me + part, parts)
+                for j in range(group):
+                    v = target * group + j
+                    spread = diffusion[v] * rate
+                    center = rows_at(v, 0)
+                    y_minus = rows_at(v, -z_cells)
+                    y_plus = rows_at(v, z_cells)
+                    face = zface[v, here : here + SUB, :]
+                    z_minus = jnp.where(z_at == 0, face, rows_at(v, -1))
+                    z_plus = jnp.where(z_at == z_cells - 1, face, rows_at(v, 1))
+                    sides = edge[v, here : here + SUB, :]
+                    x_minus = jnp.where(lane == 0, sides, pltpu.roll(center, 1, 1))
+                    x_plus = jnp.where(lane == lanes - 1, sides, pltpu.roll(center, lanes - 1, 1))
+                    mixed = react[
+                        slot, pl.ds(pl.multiple_of(v * SUB, SUB), SUB), sub * lanes : (sub + 1) * lanes
+                    ]
+                    around = (y_plus + y_minus) + (z_plus + z_minus) + (x_plus + x_minus)
+                    carried = (
+                        v_x * (x_plus - x_minus) + v_y * (y_plus - y_minus) + v_z * (z_plus - z_minus)
+                    )
+                    value = (
+                        old_share * start_ref[v, here : here + SUB, :]
+                        + (new_share - 6.0 * spread) * center
+                        + (spread * around - carried)
+                        + mixed
+                    )
+                    value = jnp.where(is_buffer, center, value)
+                    new_ref[v, here : here + SUB, :] = value
+                    snaps[part][j, here : here + SUB, :] = value.astype(bf16)
+        writes[t].start()
+    for write in writes:
+        write.wait()
 
 
 def gather_rows(parts, me, pieces, wide):
@@ -438,21 +396,23 @@
     in_hbm = functools.partial(pltpu.with_memory_space_constraint, memory_space=pltpu.HBM)
     packed = call(
         functools.partial(pack_kernel, z_cells, counts, plan),
-        [sds((variables, z_cells, lanes), f32)] * turns(n_y)
+        [sds((variables, rows, lanes), f32)]
+        + [sds((variables, z_cells, lanes), f32)] * turns(n_y)
         + [sds((len(plan), variables * chunk), f32)] * turns(n_a)
         + [sds((variables, y_part, lanes), bf16)] * (turns(n_z) * len(plan)),
         [ANY],
-        scratch=[
-            pltpu.VMEM((variables, rows, lanes), f32),
-            pltpu.SemaphoreType.DMA((min(variables, 8),)),
-        ],
+        scratch=[pltpu.SemaphoreType.DMA((min(variables, 8),))],
         limit=12,
     )(in_hbm(f))
+    f, packed = packed[0], packed[1:]
     y_faces, packed = packed[: turns(n_y)], packed[turns(n_y) :]
     x_edges, z_faces = packed[: turns(n_a)], packed[turns(n_a) :]
 
     def halo(axis, count, faces):
-        return [lax.ppermute(face, axis, swap_pairs(count, turn)) for turn, face in enumerate(faces)]
+        received = []
+        for turn, face in enumerate(faces):
+            received.append(lax.ppermute(face, axis, swap_pairs(count, turn)))
+        return received
 
     mix = call(
         mix_kernel, [sds((variables * SUB, variables * SUB), bf16)], [VMEM, ANY], limit=8
@@ -461,8 +421,8 @@
     def stencil(index, prior, x_halos, z_halos, y_halos):
         segments = plan[index]
         tiles = chunk // tile
-        operands = [diffusivity, f, in_hbm(s), in_hbm(vel), mix, *x_halos, *z_halos, *y_halos]
-        specs = [SMEM, ANY, ANY, ANY] + [VMEM] * (len(operands) - 4)
+        operands = [diffusivity, in_hbm(s), in_hbm(vel), f, mix, *x_halos, *z_halos, *y_halos]
+        specs = [SMEM, ANY, ANY] + [VMEM] * (len(operands) - 3)
         aliases = {}
         if prior is not None:
             aliases = {len(operands): 0}
@@ -474,14 +434,13 @@
             in_specs=specs,
             out_specs=[ANY] + [VMEM] * n_a,
             scratch_shapes=[
-                pltpu.VMEM((variables, chunk + 2 * pad * len(segments), lanes), f32),
+                pltpu.VMEM((2, variables, tile + 2 * pad, lanes), f32),
                 pltpu.VMEM((variables, chunk, lanes), f32),
                 pltpu.VMEM((variables, chunk, lanes), f32),
-                pltpu.VMEM((variables * SUB, tile // SUB * lanes), f32),
+                pltpu.VMEM((2, variables * SUB, tile // SUB * lanes), f32),
                 pltpu.VMEM((variables, chunk, lanes), f32),
                 pltpu.VMEM((3, chunk, lanes), f32),
                 pltpu.VMEM((variables, chunk, lanes), f32),
-                pltpu.SemaphoreType.DMA((len(segments),)),
                 pltpu.SemaphoreType.DMA((tiles,)),
                 pltpu.SemaphoreType.DMA((tiles,)),
                 pltpu.SemaphoreType.DMA((tiles,)),
@@ -500,11 +459,11 @@
     early_z, late_z = z_faces[: turns(n_z)], z_faces[turns(n_z) :]
     z_halos = halo("gz", n_z, early_z)
     x_halos = halo("ga", n_a, x_edges)
+    y_halos = halo("gy", n_y, y_faces)
     results = stencil(0, None, x_halos, z_halos, ())
     new_fields = results[0]
     chunks = [exchange(results[1:])]
-    y_faces, late_z, _ = lax.optimization_barrier((tuple(y_faces), tuple(late_z), results[2]))
-    y_halos = halo("gy", n_y, y_faces)
+    late_z, _ = lax.optimization_barrier((tuple(late_z), results[2]))
     z_halos = halo("gz", n_z, late_z)
     results = stencil(1, new_fields, x_halos, z_halos, y_halos)
     new_fields = results[0]

time: 69.6 us -> 68.2 us (0.980)
  Pallas kernels: 14.3 us -> 13 us
    pallas_call x2, Pallas kernels: 8.46 us -> 7.24 us  [stencil(): pl.pallas_call(functools.partial(stencil_kernel, z_cells, counts, index,...]
    ppermute x6, starting transfers between devices: 8.49 us -> 9.51 us  [exchange(): received.append(lax.ppermute(snaps[k], 'ga', ring_pairs(n_a, k)))]
  transfers between devices with their start and end apart: 22 -> 22, of which waited for: 8 -> 8; matrix products, arithmetic and copies ran while one was open for 0% -> 0% of each run, Pallas kernels for 8% -> 7%
where the time goes in v1:
time: 68.2 us; the launch traced here: 68 us
  starting transfers between devices  29.1 us (43%)
  waiting for transfers between devices  25.1 us (37%)
  Pallas kernels  13 us (19%)
  between operations  0.75 us (1%)
    ppermute x6, starting transfers between devices, exchange(): received.append(lax.ppermute(snaps[k], 'ga', ring_pairs(n_a, k)))  9.51 us
    ppermute x3, waiting for transfers between devices, shards(): lax.ppermute(payload, 'ga', ring_pairs(n_a, k))  9.44 us
    ppermute x6, starting transfers between devices, halo(): received.append(lax.ppermute(face, axis, swap_pairs(count, turn)))  9.29 us
    pallas_call x2, Pallas kernels, stencil(): pl.pallas_call(functools.partial(stencil_kernel, z_cells, counts, index,...  7.24 us
    ppermute x6, waiting for transfers between devices, exchange(): received.append(lax.ppermute(snaps[k], 'ga', ring_pairs(n_a, k)))  7.02 us
    ppermute x7, waiting for transfers between devices, shards(): received.append(lax.ppermute(pieces[d_y * n_z + d_z], ('gy', 'gz'), pairs))  5.92 us
    ppermute x7, starting transfers between devices, shards(): received.append(lax.ppermute(pieces[d_y * n_z + d_z], ('gy', 'gz'), pairs))  5.83 us
    ppermute x3, starting transfers between devices, shards(): lax.ppermute(payload, 'ga', ring_pairs(n_a, k))  4.52 us
  transfers between devices with their start and end apart: 22, of which 8 were waited for; matrix products, arithmetic and copies ran while one was open for 0% of the time, Pallas kernels for 7%

profile of v1, /device:TPU:0, one launch (start us, length us, event | category | flops | bytes accessed | tf_op | source)
XLA Modules:
  0.0 68.0 jit_solution(4138712510411748602)
XLA Ops:
  0.7 2.6 %shard_map.94 = (f32[16,256,128]{2,1,0:T(8,128)S(1)}, f32[16,4,128]{2,1,0:T(4,128)S(1)}, f32[16,4,128]{2,1,0:T(4,128)S(1)}, f32[2,2048]{1,0:T(2,128)S(1)}, f32[2...) custom-call(f32[16,256,128]{2,1,0:T(8,128)} %bitcast.13), custom_call_target="tpu_custom_call" | custom-call | tf_op jit(solution)/shard_map/pallas_call | solution.py:397
  3.3 3.1 %collective-permute-start.2 = (bf16[16,32,128]{2,1,0:T(8,128)(2,1)S(1)}, bf16[16,32,128]{2,1,0:T(8,128)(2,1)S(1)}, u32[]{:S(2)}, u32[]{:S(2)}) collective-permute-start(bf16[16,32,128]{2,1,0:T(8,128)(2,1)S(1)} %get-tuple-element.38), channel_id=1, source_target_pairs={{0,4},{4,0},{1,5},{5,1},{2,6},{6,2},{3,7},{7,3},{8,12},{12,8},{9,1... | collective-permute-start | bytes 393224 | tf_op jit(solution)/shard_map/ppermute | solution.py:414
  6.3 1.6 %collective-permute-start = (f32[2,2048]{1,0:T(2,128)S(1)}, f32[2,2048]{1,0:T(2,128)S(1)}, u32[]{:S(2)}, u32[]{:S(2)}) collective-permute-start(f32[2,2048]{1,0:T(2,128)S(1)} %get-tuple-element.35), channel_id=1, source_target_pairs={{0,1},{1,0},{2,3},{3,2},{4,5},{5,4},{6,7},{7,6},{8,9},{9,8},{10,11... | collective-permute-start | bytes 49160 | tf_op jit(solution)/shard_map/ppermute | solution.py:414
  7.9 2.5 %collective-permute-start.1 = (f32[2,2048]{1,0:T(2,128)S(1)}, f32[2,2048]{1,0:T(2,128)S(1)}, u32[]{:S(2)}, u32[]{:S(2)}) collective-permute-start(f32[2,2048]{1,0:T(2,128)S(1)} %get-tuple-element.36), channel_id=1, source_target_pairs={{0,3},{1,2},{2,1},{3,0},{4,7},{5,6},{6,5},{7,4},{8,11},{9,10},{10,... | collective-permute-start | bytes 49160 | tf_op jit(solution)/shard_map/ppermute | solution.py:414
  10.7 2.7 %collective-permute-done.1.rest_1_ = f32[2,2048]{1,0:T(2,128)S(1)} collective-permute-done((f32[2,2048]{1,0:T(2,128)S(1)}, f32[2,2048]{1,0:T(2,128)S(1)}, u32[]{:S(2)}, u32[]{:S(2)}) %collective-permute-start.1) | collective-permute-done | bytes 16416 | tf_op jit(solution)/shard_map/ppermute | solution.py:414
  13.4 3.7 %stencil.2 = (f32[16,256,128]{2,1,0:T(8,128)}, bf16[4,128,128]{2,1,0:T(8,128)(2,1)S(1)}, bf16[4,128,128]{2,1,0:T(8,128)(2,1)S(1)}, bf16[4,128,128]{2,1,0:T(8,128)(2,1)S(1)}, bf16[4,128,128]{2,1,0:T(8,128)(2,1)S(1)}) custom-call(f32[16]{0:T(128)S(1)} %copy-done.3, f32[16,256,128]{2,1,0:T(8,128)} %bitcast.10, f32[3,256,128]{2,1,0:T(8,128)} %bitcast.14, ...), custom_call_target="tpu_custom_call" | custom-call | tf_op jit(solution)/shard_map/stencil/pallas_call | solution.py:431
  17.7 0.8 %collective-permute-start.10 = (bf16[4,128,128]{2,1,0:T(8,128)(2,1)S(1)}, bf16[4,128,128]{2,1,0:T(8,128)(2,1)S(1)}, u32[]{:S(2)}, u32[]{:S(2)}) collective-permute-start(bf16[4,128,128]{2,1,0:T(8,128)(2,1)S(1)} %get-tuple-element.49), channel_id=1, source_target_pairs={{0,2},{1,3},{2,0},{3,1},{4,6},{5,7},{6,4},{7,5},{8,10},{9,11},{10,... | collective-permute-start | bytes 393224 | tf_op jit(solution)/shard_map/ppermute | solution.py:456
  18.5 1.6 %collective-permute-start.4 = (f32[16,4,128]{2,1,0:T(4,128)S(1)}, f32[16,4,128]{2,1,0:T(4,128)S(1)}, u32[]{:S(2)}, u32[]{:S(2)}) collective-permute-start(f32[16,4,128]{2,1,0:T(4,128)S(1)} %get-tuple-element.34.after), channel_id=1, source_target_pairs={{0,8},{8,0},{16,24},{24,16},{1,9},{9,1},{17,25},{25,17},{2,10},{10... | collective-permute-start | bytes 98312 | tf_op jit(solution)/shard_map/ppermute | solution.py:414
  20.1 2.2 %collective-permute-start.9 = (bf16[4,128,128]{2,1,0:T(8,128)(2,1)S(1)}, bf16[4,128,128]{2,1,0:T(8,128)(2,1)S(1)}, u32[]{:S(2)}, u32[]{:S(2)}) collective-permute-start(bf16[4,128,128]{2,1,0:T(8,128)(2,1)S(1)} %get-tuple-element.39), channel_id=1, source_target_pairs={{0,1},{1,2},{2,3},{3,0},{4,5},{5,6},{6,7},{7,4},{8,9},{9,10},{10,1... | collective-permute-start | bytes 393224 | tf_op jit(solution)/shard_map/ppermute | solution.py:456
  22.3 1.6 %collective-permute-start.11 = (bf16[4,128,128]{2,1,0:T(8,128)(2,1)S(1)}, bf16[4,128,128]{2,1,0:T(8,128)(2,1)S(1)}, u32[]{:S(2)}, u32[]{:S(2)}) collective-permute-start(bf16[4,128,128]{2,1,0:T(8,128)(2,1)S(1)} %get-tuple-element.50), channel_id=1, source_target_pairs={{0,3},{1,0},{2,1},{3,2},{4,7},{5,4},{6,5},{7,6},{8,11},{9,8},{10,9... | collective-permute-start | bytes 393224 | tf_op jit(solution)/shard_map/ppermute | solution.py:456
  23.9 3.6 %stencil.3 = (f32[16,256,128]{2,1,0:T(8,128)}, bf16[4,128,128]{2,1,0:T(8,128)(2,1)S(1)}, bf16[4,128,128]{2,1,0:T(8,128)(2,1)S(1)}, bf16[4,128,128]{2,1,0:T(8,128)(2,1)S(1)}, bf16[4,128,128]{2,1,0:T(8,128)(2,1)S(1)}) custom-call(f32[16]{0:T(128)S(1)} %copy-done.3, f32[16,256,128]{2,1,0:T(8,128)} %bitcast.11, ...), custom_call_target="tpu_custom_call", output_to_operand_aliasing={{0}: (10, {})} | custom-call | tf_op jit(solution)/shard_map/stencil/pallas_call | solution.py:431
  28.0 1.9 %collective-permute-start.7 = (bf16[4,128,128]{2,1,0:T(8,128)(2,1)S(1)}, bf16[4,128,128]{2,1,0:T(8,128)(2,1)S(1)}, u32[]{:S(2)}, u32[]{:S(2)}) collective-permute-start(bf16[4,128,128]{2,1,0:T(8,128)(2,1)S(1)} %get-tuple-element.46), channel_id=1, source_target_pairs={{0,2},{1,3},{2,0},{3,1},{4,6},{5,7},{6,4},{7,5},{8,10},{9,11},{10,... | collective-permute-start | bytes 393224 | tf_op jit(solution)/shard_map/ppermute | solution.py:456
  29.9 2.5 %collective-permute-start.8 = (bf16[4,128,128]{2,1,0:T(8,128)(2,1)S(1)}, bf16[4,128,128]{2,1,0:T(8,128)(2,1)S(1)}, u32[]{:S(2)}, u32[]{:S(2)}) collective-permute-start(bf16[4,128,128]{2,1,0:T(8,128)(2,1)S(1)} %get-tuple-element.47), channel_id=1, source_target_pairs={{0,3},{1,0},{2,1},{3,2},{4,7},{5,4},{6,5},{7,6},{8,11},{9,8},{10,9... | collective-permute-start | bytes 393224 | tf_op jit(solution)/shard_map/ppermute | solution.py:456
  32.4 0.8 %shard_map.96 = (f32[512,512]{1,0:T(8,128)S(1)}, bf16[4,32,256]{2,1,0:T(8,128)(2,1)S(1)}) custom-call(bf16[64,512]{1,0:T(8,128)(2,1)S(1)} %bitcast.7, bf16[4,128,128]{2,1,0:T(8,128)(2,1)S(1)} %get-tuple-element.48.refs_0_, bf16[4,128,128]{2,1,0:T(8,128)(2,1)S(1)} %collective-permute-done.9.refs_1_, bf16[4,128,128]{2,1,0:T(8,128)(2,1)S(1)} %collective-permute-done.10.refs_2_, ...), custom_call_target="tpu_custom_call" | custom-call | tf_op jit(solution)/shard_map/pallas_call | solution.py:476
  33.3 2.5 %collective-permute-done.6.refs_1_ = bf16[4,128,128]{2,1,0:T(8,128)(2,1)S(1)} collective-permute-done((bf16[4,128,128]{2,1,0:T(8,128)(2,1)S(1)}, bf16[4,128,128]{2,1,0:T(8,128)(2,1)S(1)}, u32[]{:S(2)}, u32[]{:S(2)}) %collective-permute-start.6) | collective-permute-done | bytes 131104 | tf_op jit(solution)/shard_map/ppermute | solution.py:456
  35.8 4.5 %collective-permute-done.7.refs_2_ = bf16[4,128,128]{2,1,0:T(8,128)(2,1)S(1)} collective-permute-done((bf16[4,128,128]{2,1,0:T(8,128)(2,1)S(1)}, bf16[4,128,128]{2,1,0:T(8,128)(2,1)S(1)}, u32[]{:S(2)}, u32[]{:S(2)}) %collective-permute-start.7) | collective-permute-done | bytes 131104 | tf_op jit(solution)/shard_map/ppermute | solution.py:456
  40.3 0.8 %shard_map.97 = (bf16[64,768]{1,0:T(8,128)(2,1)S(1)}, bf16[64,512]{1,0:T(8,128)(2,1)S(1)}, bf16[64,768]{1,0:T(8,128)(2,1)S(1)}, bf16[64,512]{1,0:T(8,128)(2,1)S(...) custom-call(bf16[64,512]{1,0:T(8,128)(2,1)S(1)} %bitcast.8, ...), custom_call_target="tpu_custom_call" | custom-call | tf_op jit(solution)/shard_map/pallas_call | solution.py:486
  41.0 1.5 %collective-permute-start.12 = (bf16[64,512]{1,0:T(8,128)(2,1)S(1)}, bf16[64,512]{1,0:T(8,128)(2,1)S(1)}, u32[]{:S(2)}, u32[]{:S(2)}) collective-permute-start(bf16[64,512]{1,0:T(8,128)(2,1)S(1)} %get-tuple-element.54), channel_id=1, source_target_pairs={{0,4},{4,0},{8,12},{12,8},{16,20},{20,16},{24,28},{28,24},{1,5},{5... | collective-permute-start | bytes 196616 | tf_op jit(solution)/shard_map/ppermute | solution.py:506
  42.9 1.8 %collective-permute-start.15 = (bf16[64,768]{1,0:T(8,128)(2,1)S(1)}, bf16[64,768]{1,0:T(8,128)(2,1)S(1)}, u32[]{:S(2)}, u32[]{:S(2)}) collective-permute-start(bf16[64,768]{1,0:T(8,128)(2,1)S(1)} %get-tuple-element.57), channel_id=1, source_target_pairs={{0,16},{4,20},{8,24},{12,28},{16,0},{20,4},{24,8},{28,12},{1,17},{... | collective-permute-start | bytes 294920 | tf_op jit(solution)/shard_map/ppermute | solution.py:506
  45.4 1.6 %collective-permute-start.16 = (bf16[64,512]{1,0:T(8,128)(2,1)S(1)}, bf16[64,512]{1,0:T(8,128)(2,1)S(1)}, u32[]{:S(2)}, u32[]{:S(2)}) collective-permute-start(bf16[64,512]{1,0:T(8,128)(2,1)S(1)} %get-tuple-element.58), channel_id=1, source_target_pairs={{0,20},{4,16},{8,28},{12,24},{16,4},{20,0},{24,12},{28,8},{1,21},{... | collective-permute-start | bytes 196616 | tf_op jit(solution)/shard_map/ppermute | solution.py:506
  47.7 5.1 %collective-permute-done.16.refs_5_ = bf16[64,512]{1,0:T(8,128)(2,1)S(1)} collective-permute-done((bf16[64,512]{1,0:T(8,128)(2,1)S(1)}, bf16[64,512]{1,0:T(8,128)(2,1)S(1)}, u32[]{:S(2)}, u32[]{:S(2)}) %collective-permute-start.16) | collective-permute-done | bytes 65568 | tf_op jit(solution)/shard_map/ppermute | solution.py:506
  53.3 3.9 %collective-permute-start.21 = (bf16[64,768]{1,0:T(8,128)(2,1)S(1)}, bf16[64,768]{1,0:T(8,128)(2,1)S(1)}, u32[]{:S(2)}, u32[]{:S(2)}) collective-permute-start(bf16[64,768]{1,0:T(8,128)(2,1)S(1)} %shard_map.98.refs_0_), channel_id=1, source_target_pairs={{0,3},{1,0},{2,1},{3,2},{4,7},{5,4},{6,5},{7,6},{8,11},{9,8},{10,9... | collective-permute-start | bytes 294920 | tf_op jit(solution)/shard_map/ppermute | solution.py:536
  57.9 2.6 %collective-permute-done.21.refs_3_ = bf16[64,768]{1,0:T(8,128)(2,1)S(1)} collective-permute-done((bf16[64,768]{1,0:T(8,128)(2,1)S(1)}, bf16[64,768]{1,0:T(8,128)(2,1)S(1)}, u32[]{:S(2)}, u32[]{:S(2)}) %collective-permute-start.21) | collective-permute-done | bytes 98336 | tf_op jit(solution)/shard_map/ppermute | solution.py:536
  60.5 6.8 %collective-permute-done.20.refs_2_ = bf16[64,768]{1,0:T(8,128)(2,1)S(1)} collective-permute-done((bf16[64,768]{1,0:T(8,128)(2,1)S(1)}, bf16[64,768]{1,0:T(8,128)(2,1)S(1)}, u32[]{:S(2)}, u32[]{:S(2)}) %collective-permute-start.20) | collective-permute-done | bytes 98336 | tf_op jit(solution)/shard_map/ppermute | solution.py:536
  (36 shorter events, 5.1 us)
Async XLA Ops:
  0.6 12.8 %copy-start.3 = (f32[16]{0:T(128)S(1)}, f32[16]{0:T(128)}, u32[]{:S(2)}) copy-start(f32[16]{0:T(128)} %diffusion.3) | copy-start | bytes 196
  3.3 10.2 %collective-permute-start.2 = (bf16[16,32,128]{2,1,0:T(8,128)(2,1)S(1)}, bf16[16,32,128]{2,1,0:T(8,128)(2,1)S(1)}, u32[]{:S(2)}, u32[]{:S(2)}) collective-permute-start(bf16[16,32,128]{2,1,0:T(8,128)(2,1)S(1)} %get-tuple-element.38), channel_id=1, source_target_pairs={{0,4},{4,0},{1,5},{5,1},{2,6},{6,2},{3,7},{7,3},{8,12},{12,8},{9,1... | collective-permute-start | bytes 393224 | tf_op jit(solution)/shard_map/ppermute | solution.py:414
  6.3 4.4 %collective-permute-start = (f32[2,2048]{1,0:T(2,128)S(1)}, f32[2,2048]{1,0:T(2,128)S(1)}, u32[]{:S(2)}, u32[]{:S(2)}) collective-permute-start(f32[2,2048]{1,0:T(2,128)S(1)} %get-tuple-element.35), channel_id=1, source_target_pairs={{0,1},{1,0},{2,3},{3,2},{4,5},{5,4},{6,7},{7,6},{8,9},{9,8},{10,11... | collective-permute-start | bytes 49160 | tf_op jit(solution)/shard_map/ppermute | solution.py:414
  7.9 5.5 %collective-permute-start.1 = (f32[2,2048]{1,0:T(2,128)S(1)}, f32[2,2048]{1,0:T(2,128)S(1)}, u32[]{:S(2)}, u32[]{:S(2)}) collective-permute-start(f32[2,2048]{1,0:T(2,128)S(1)} %get-tuple-element.36), channel_id=1, source_target_pairs={{0,3},{1,2},{2,1},{3,0},{4,7},{5,6},{6,5},{7,4},{8,11},{9,10},{10,... | collective-permute-start | bytes 49160 | tf_op jit(solution)/shard_map/ppermute | solution.py:414
  17.1 6.8 %collective-permute-start.3 = (bf16[16,32,128]{2,1,0:T(8,128)(2,1)S(1)}, bf16[16,32,128]{2,1,0:T(8,128)(2,1)S(1)}, u32[]{:S(2)}, u32[]{:S(2)}) collective-permute-start(bf16[16,32,128]{2,1,0:T(8,128)(2,1)S(1)} %get-tuple-element.40), channel_id=1, source_target_pairs={{0,4},{4,0},{1,5},{5,1},{2,6},{6,2},{3,7},{7,3},{8,12},{12,8},{9,1... | collective-permute-start | bytes 393224 | tf_op jit(solution)/shard_map/ppermute | solution.py:414
  17.7 12.3 %collective-permute-start.10 = (bf16[4,128,128]{2,1,0:T(8,128)(2,1)S(1)}, bf16[4,128,128]{2,1,0:T(8,128)(2,1)S(1)}, u32[]{:S(2)}, u32[]{:S(2)}) collective-permute-start(bf16[4,128,128]{2,1,0:T(8,128)(2,1)S(1)} %get-tuple-element.49), channel_id=1, source_target_pairs={{0,2},{1,3},{2,0},{3,1},{4,6},{5,7},{6,4},{7,5},{8,10},{9,11},{10,... | collective-permute-start | bytes 393224 | tf_op jit(solution)/shard_map/ppermute | solution.py:456
  18.5 3.9 %collective-permute-start.5 = (f32[16,4,128]{2,1,0:T(4,128)S(1)}, f32[16,4,128]{2,1,0:T(4,128)S(1)}, u32[]{:S(2)}, u32[]{:S(2)}) collective-permute-start(f32[16,4,128]{2,1,0:T(4,128)S(1)} %get-tuple-element.41), channel_id=1, source_target_pairs={{0,24},{8,16},{16,8},{24,0},{1,25},{9,17},{17,9},{25,1},{2,26},{10... | collective-permute-start | bytes 98312 | tf_op jit(solution)/shard_map/ppermute | solution.py:414
  18.5 5.4 %collective-permute-start.4 = (f32[16,4,128]{2,1,0:T(4,128)S(1)}, f32[16,4,128]{2,1,0:T(4,128)S(1)}, u32[]{:S(2)}, u32[]{:S(2)}) collective-permute-start(f32[16,4,128]{2,1,0:T(4,128)S(1)} %get-tuple-element.34.after), channel_id=1, source_target_pairs={{0,8},{8,0},{16,24},{24,16},{1,9},{9,1},{17,25},{25,17},{2,10},{10... | collective-permute-start | bytes 98312 | tf_op jit(solution)/shard_map/ppermute | solution.py:414
  20.1 12.3 %collective-permute-start.9 = (bf16[4,128,128]{2,1,0:T(8,128)(2,1)S(1)}, bf16[4,128,128]{2,1,0:T(8,128)(2,1)S(1)}, u32[]{:S(2)}, u32[]{:S(2)}) collective-permute-start(bf16[4,128,128]{2,1,0:T(8,128)(2,1)S(1)} %get-tuple-element.39), channel_id=1, source_target_pairs={{0,1},{1,2},{2,3},{3,0},{4,5},{5,6},{6,7},{7,4},{8,9},{9,10},{10,1... | collective-permute-start | bytes 393224 | tf_op jit(solution)/shard_map/ppermute | solution.py:456
  22.3 10.1 %collective-permute-start.11 = (bf16[4,128,128]{2,1,0:T(8,128)(2,1)S(1)}, bf16[4,128,128]{2,1,0:T(8,128)(2,1)S(1)}, u32[]{:S(2)}, u32[]{:S(2)}) collective-permute-start(bf16[4,128,128]{2,1,0:T(8,128)(2,1)S(1)} %get-tuple-element.50), channel_id=1, source_target_pairs={{0,3},{1,0},{2,1},{3,2},{4,7},{5,4},{6,5},{7,6},{8,11},{9,8},{10,9... | collective-permute-start | bytes 393224 | tf_op jit(solution)/shard_map/ppermute | solution.py:456
  27.5 25.3 %copy-start.1 = (f32[256,64]{0,1:T(8,128)S(1)}, f32[256,64]{0,1:T(8,128)}, u32[]{:S(2)}) copy-start(f32[256,64]{0,1:T(8,128)} %param.13) | copy-start | bytes 196612
  27.5 8.3 %collective-permute-start.6 = (bf16[4,128,128]{2,1,0:T(8,128)(2,1)S(1)}, bf16[4,128,128]{2,1,0:T(8,128)(2,1)S(1)}, u32[]{:S(2)}, u32[]{:S(2)}) collective-permute-start(bf16[4,128,128]{2,1,0:T(8,128)(2,1)S(1)} %get-tuple-element.45), channel_id=1, source_target_pairs={{0,1},{1,2},{2,3},{3,0},{4,5},{5,6},{6,7},{7,4},{8,9},{9,10},{10,1... | collective-permute-start | bytes 393224 | tf_op jit(solution)/shard_map/ppermute | solution.py:456
  28.0 12.2 %collective-permute-start.7 = (bf16[4,128,128]{2,1,0:T(8,128)(2,1)S(1)}, bf16[4,128,128]{2,1,0:T(8,128)(2,1)S(1)}, u32[]{:S(2)}, u32[]{:S(2)}) collective-permute-start(bf16[4,128,128]{2,1,0:T(8,128)(2,1)S(1)} %get-tuple-element.46), channel_id=1, source_target_pairs={{0,2},{1,3},{2,0},{3,1},{4,6},{5,7},{6,4},{7,5},{8,10},{9,11},{10,... | collective-permute-start | bytes 393224 | tf_op jit(solution)/shard_map/ppermute | solution.py:456
  29.9 10.3 %collective-permute-start.8 = (bf16[4,128,128]{2,1,0:T(8,128)(2,1)S(1)}, bf16[4,128,128]{2,1,0:T(8,128)(2,1)S(1)}, u32[]{:S(2)}, u32[]{:S(2)}) collective-permute-start(bf16[4,128,128]{2,1,0:T(8,128)(2,1)S(1)} %get-tuple-element.47), channel_id=1, source_target_pairs={{0,3},{1,0},{2,1},{3,2},{4,7},{5,4},{6,5},{7,6},{8,11},{9,8},{10,9... | collective-permute-start | bytes 393224 | tf_op jit(solution)/shard_map/ppermute | solution.py:456
  41.0 4.3 %collective-permute-start.12 = (bf16[64,512]{1,0:T(8,128)(2,1)S(1)}, bf16[64,512]{1,0:T(8,128)(2,1)S(1)}, u32[]{:S(2)}, u32[]{:S(2)}) collective-permute-start(bf16[64,512]{1,0:T(8,128)(2,1)S(1)} %get-tuple-element.54), channel_id=1, source_target_pairs={{0,4},{4,0},{8,12},{12,8},{16,20},{20,16},{24,28},{28,24},{1,5},{5... | collective-permute-start | bytes 196616 | tf_op jit(solution)/shard_map/ppermute | solution.py:506
  42.6 4.6 %collective-permute-start.14 = (bf16[64,512]{1,0:T(8,128)(2,1)S(1)}, bf16[64,512]{1,0:T(8,128)(2,1)S(1)}, u32[]{:S(2)}, u32[]{:S(2)}) collective-permute-start(bf16[64,512]{1,0:T(8,128)(2,1)S(1)} %get-tuple-element.56), channel_id=1, source_target_pairs={{0,12},{4,8},{8,20},{12,16},{16,28},{20,24},{24,4},{28,0},{1,13},{... | collective-permute-start | bytes 196616 | tf_op jit(solution)/shard_map/ppermute | solution.py:506
  42.6 10.2 %collective-permute-start.13 = (bf16[64,768]{1,0:T(8,128)(2,1)S(1)}, bf16[64,768]{1,0:T(8,128)(2,1)S(1)}, u32[]{:S(2)}, u32[]{:S(2)}) collective-permute-start(bf16[64,768]{1,0:T(8,128)(2,1)S(1)} %get-tuple-element.55), channel_id=1, source_target_pairs={{0,8},{4,12},{8,16},{12,20},{16,24},{20,28},{24,0},{28,4},{1,9},{5... | collective-permute-start | bytes 294920 | tf_op jit(solution)/shard_map/ppermute | solution.py:506
  42.9 9.9 %collective-permute-start.15 = (bf16[64,768]{1,0:T(8,128)(2,1)S(1)}, bf16[64,768]{1,0:T(8,128)(2,1)S(1)}, u32[]{:S(2)}, u32[]{:S(2)}) collective-permute-start(bf16[64,768]{1,0:T(8,128)(2,1)S(1)} %get-tuple-element.57), channel_id=1, source_target_pairs={{0,16},{4,20},{8,24},{12,28},{16,0},{20,4},{24,8},{28,12},{1,17},{... | collective-permute-start | bytes 294920 | tf_op jit(solution)/shard_map/ppermute | solution.py:506
  44.7 8.1 %collective-permute-start.17 = (bf16[64,768]{1,0:T(8,128)(2,1)S(1)}, bf16[64,768]{1,0:T(8,128)(2,1)S(1)}, u32[]{:S(2)}, u32[]{:S(2)}) collective-permute-start(bf16[64,768]{1,0:T(8,128)(2,1)S(1)} %get-tuple-element.59), channel_id=1, source_target_pairs={{0,24},{4,28},{8,0},{12,4},{16,8},{20,12},{24,16},{28,20},{1,25},{... | collective-permute-start | bytes 294920 | tf_op jit(solution)/shard_map/ppermute | solution.py:506
  45.4 7.4 %collective-permute-start.16 = (bf16[64,512]{1,0:T(8,128)(2,1)S(1)}, bf16[64,512]{1,0:T(8,128)(2,1)S(1)}, u32[]{:S(2)}, u32[]{:S(2)}) collective-permute-start(bf16[64,512]{1,0:T(8,128)(2,1)S(1)} %get-tuple-element.58), channel_id=1, source_target_pairs={{0,20},{4,16},{8,28},{12,24},{16,4},{20,0},{24,12},{28,8},{1,21},{... | collective-permute-start | bytes 196616 | tf_op jit(solution)/shard_map/ppermute | solution.py:506
  47.2 5.6 %collective-permute-start.18 = (bf16[64,512]{1,0:T(8,128)(2,1)S(1)}, bf16[64,512]{1,0:T(8,128)(2,1)S(1)}, u32[]{:S(2)}, u32[]{:S(2)}) collective-permute-start(bf16[64,512]{1,0:T(8,128)(2,1)S(1)} %get-tuple-element.60), channel_id=1, source_target_pairs={{0,28},{4,24},{8,4},{12,0},{16,12},{20,8},{24,20},{28,16},{1,29},{... | collective-permute-start | bytes 196616 | tf_op jit(solution)/shard_map/ppermute | solution.py:506
  53.3 7.1 %collective-permute-start.21 = (bf16[64,768]{1,0:T(8,128)(2,1)S(1)}, bf16[64,768]{1,0:T(8,128)(2,1)S(1)}, u32[]{:S(2)}, u32[]{:S(2)}) collective-permute-start(bf16[64,768]{1,0:T(8,128)(2,1)S(1)} %shard_map.98.refs_0_), channel_id=1, source_target_pairs={{0,3},{1,0},{2,1},{3,2},{4,7},{5,4},{6,5},{7,6},{8,11},{9,8},{10,9... | collective-permute-start | bytes 294920 | tf_op jit(solution)/shard_map/ppermute | solution.py:536
  57.2 10.1 %collective-permute-start.20 = (bf16[64,768]{1,0:T(8,128)(2,1)S(1)}, bf16[64,768]{1,0:T(8,128)(2,1)S(1)}, u32[]{:S(2)}, u32[]{:S(2)}) collective-permute-start(bf16[64,768]{1,0:T(8,128)(2,1)S(1)} %shard_map.98.refs_0_), channel_id=1, source_target_pairs={{0,2},{1,3},{2,0},{3,1},{4,6},{5,7},{6,4},{7,5},{8,10},{9,11},{10,... | collective-permute-start | bytes 294920 | tf_op jit(solution)/shard_map/ppermute | solution.py:536
  57.8 9.5 %collective-permute-start.19 = (bf16[64,768]{1,0:T(8,128)(2,1)S(1)}, bf16[64,768]{1,0:T(8,128)(2,1)S(1)}, u32[]{:S(2)}, u32[]{:S(2)}) collective-permute-start(bf16[64,768]{1,0:T(8,128)(2,1)S(1)} %shard_map.98.refs_0_), channel_id=1, source_target_pairs={{0,1},{1,2},{2,3},{3,0},{4,5},{5,6},{6,7},{7,4},{8,9},{9,10},{10,1... | collective-permute-start | bytes 294920 | tf_op jit(solution)/shard_map/ppermute | solution.py:536
  (2 other events, 18.3 us)

commit v2 on v1

--- a/solution.py
+++ b/solution.py
@@ -24,6 +24,18 @@
     if turn == 0:
         return [(i, i ^ 1) for i in range(count)]
     return [(i, (i + (1 if i % 2 else -1)) % count) for i in range(count)]
+
+
+def partner(count, index, step):
+    if count & (count - 1) == 0:
+        return index ^ step
+    return (index + step) % count
+
+
+def origin(count, index, step):
+    if count & (count - 1) == 0:
+        return index ^ step
+    return (index - step + count) % count
 
 
 def turns(count):
@@ -107,7 +119,9 @@
     return pick
 
 
-def mix_kernel(r_ref, after, out_ref):
+def mix_kernel(r_ref, vel_hbm, after, out_ref, vel_ref, sem):
+    load = pltpu.make_async_copy(vel_hbm, vel_ref, sem)
+    load.start()
     count = r_ref.shape[0]
     size = out_ref.shape[0]
     spread = jnp.where(
@@ -124,21 +138,19 @@
     row = lax.broadcasted_iota(jnp.int32, (size, size), 0)
     col = lax.broadcasted_iota(jnp.int32, (size, size), 1)
     out_ref[...] = jnp.where(row % SUB == col % SUB, both, 0.0).astype(bf16)
+    load.wait()
 
 
 def stencil_kernel(
-    z_cells, counts, index, segments, has_prior, has_y, diffusion, s_hbm, vel_hbm, f_ref, mix_ref, *rest
+    z_cells, counts, index, segments, has_y, diffusion, vel_ref, start_ref, f_ref, mix_ref, *rest
 ):
     n_y, n_z, parts = counts
     x_refs, rest = rest[: turns(parts)], rest[turns(parts) :]
     z_refs, rest = rest[: turns(n_z)], rest[turns(n_z) :]
     if has_y:
         y_refs, rest = rest[: turns(n_y)], rest[turns(n_y) :]
-    rest = rest[1:] if has_prior else rest
-    new_hbm, rest = rest[0], rest[1:]
-    snaps, (ends, edge, zface, react, start_ref, vel_ref, new_ref, in_sem, vel_sem, out_sem) = (
-        rest[:parts], rest[parts:]
-    )
+    new_ref, rest = rest[0], rest[1:]
+    snaps, (ends, edge, zface, react) = rest[:parts], rest[parts:]
     variables, rows, lanes = f_ref.shape
     pad = -(-z_cells // 8) * 8
     tile = TILE
@@ -146,15 +158,7 @@
     me = lax.axis_index("ga")
     is_buffer = me == parts - 1
 
-    starts, winds, writes = [], [], []
     tile_rows = [first + k * tile for first, count in segments for k in range(count // tile)]
-    for t, row in enumerate(tile_rows):
-        there, here = pl.ds(row, tile), pl.ds(t * tile, tile)
-        starts.append(pltpu.make_async_copy(s_hbm.at[:, there, :], start_ref.at[:, here, :], in_sem.at[t]))
-        winds.append(pltpu.make_async_copy(vel_hbm.at[:, there, :], vel_ref.at[:, here, :], vel_sem.at[t]))
-        writes.append(pltpu.make_async_copy(new_ref.at[:, here, :], new_hbm.at[:, there, :], out_sem.at[t]))
-        starts[-1].start()
-        winds[-1].start()
 
     put = corner_mask(lanes)
     side = lax.broadcasted_iota(jnp.int32, (8, chunk), 0)
@@ -190,8 +194,6 @@
                 jnp.concatenate([f_ref[w, at : at + SUB, :].astype(bf16) for w in range(variables)], axis=0)
             )
         react[slot] = jnp.dot(mix_ref[...], jnp.concatenate(blocks, axis=1), preferred_element_type=f32)
-        starts[t].wait()
-        winds[t].wait()
         for sub in range(tile // SUB):
             at, here = row + sub * SUB, t * tile + sub * SUB
 
@@ -202,9 +204,9 @@
                     return ends[1, v, pad + sub * SUB + offset : pad + (sub + 1) * SUB + offset, :]
                 return f_ref[v, at + offset : at + SUB + offset, :]
 
-            v_x = vel_ref[0, here : here + SUB, :] * (0.5 * rate)
-            v_y = vel_ref[1, here : here + SUB, :] * (0.5 * rate)
-            v_z = vel_ref[2, here : here + SUB, :] * (0.5 * rate)
+            v_x = vel_ref[0, at : at + SUB, :] * (0.5 * rate)
+            v_y = vel_ref[1, at : at + SUB, :] * (0.5 * rate)
+            v_z = vel_ref[2, at : at + SUB, :] * (0.5 * rate)
             for part in range(parts):
                 target = lax.rem(me + part, parts)
                 for j in range(group):
@@ -227,7 +229,7 @@
                         v_x * (x_plus - x_minus) + v_y * (y_plus - y_minus) + v_z * (z_plus - z_minus)
                     )
                     value = (
-                        old_share * start_ref[v, here : here + SUB, :]
+                        old_share * start_ref[v, at : at + SUB, :]
                         + (new_share - 6.0 * spread) * center
                         + (spread * around - carried)
                         + mixed
@@ -235,7 +237,21 @@
                     value = jnp.where(is_buffer, center, value)
                     new_ref[v, here : here + SUB, :] = value
                     snaps[part][j, here : here + SUB, :] = value.astype(bf16)
-        writes[t].start()
+
+
+def flush_kernel(plan, *refs):
+    parts, (new_hbm, sem) = refs[: len(plan)], refs[len(plan) :]
+    writes = []
+    for part, segments in zip(parts, plan):
+        at = 0
+        for first, count in segments:
+            writes.append(
+                pltpu.make_async_copy(
+                    part.at[:, pl.ds(at, count), :], new_hbm.at[:, pl.ds(first, count), :], sem.at[len(writes)]
+                )
+            )
+            writes[-1].start()
+            at += count
     for write in writes:
         write.wait()
 
@@ -308,7 +324,7 @@
     for d_y in range(n_y):
         for d_z in range(n_z):
             out = outs[d_y * n_z + d_z]
-            y_to, z_to = lax.rem(my_y + d_y, n_y), lax.rem(my_z + d_z, n_z)
+            y_to, z_to = partner(n_y, my_y, d_y), partner(n_z, my_z, d_z)
             at = pl.multiple_of((y_to * n_z + z_to) * own, own)
             out[:own, :width] = gram[pl.ds(at, own), :].astype(bf16)
             if d_z == 0:
@@ -326,7 +342,7 @@
     width = pieces[0].shape[1] - layers * cols
     my_y = lax.axis_index("gy")
     for d_y in range(n_y):
-        source = lax.rem(my_y - d_y + n_y, n_y)
+        source = origin(n_y, my_y, d_y)
         at = pl.multiple_of(source * y_cells, y_cells)
         for layer in range(layers):
             m_ref[layer, pl.ds(at, y_cells), :] = pieces[d_y * n_z][
@@ -414,38 +430,28 @@
             received.append(lax.ppermute(face, axis, swap_pairs(count, turn)))
         return received
 
-    mix = call(
-        mix_kernel, [sds((variables * SUB, variables * SUB), bf16)], [VMEM, ANY], limit=8
-    )(reaction, y_faces[0])[0]
-
-    def stencil(index, prior, x_halos, z_halos, y_halos):
+    mix, vel = call(
+        mix_kernel,
+        [sds((variables * SUB, variables * SUB), bf16), sds(vel.shape, f32)],
+        [VMEM, ANY, ANY],
+        scratch=[pltpu.SemaphoreType.DMA],
+        limit=8,
+    )(reaction, in_hbm(vel), y_faces[0])
+
+    def stencil(index, x_halos, z_halos, y_halos):
         segments = plan[index]
-        tiles = chunk // tile
-        operands = [diffusivity, in_hbm(s), in_hbm(vel), f, mix, *x_halos, *z_halos, *y_halos]
-        specs = [SMEM, ANY, ANY] + [VMEM] * (len(operands) - 3)
-        aliases = {}
-        if prior is not None:
-            aliases = {len(operands): 0}
-            operands.append(prior)
-            specs.append(ANY)
+        operands = [diffusivity, vel, s, f, mix, *x_halos, *z_halos, *y_halos]
         return pl.pallas_call(
-            functools.partial(stencil_kernel, z_cells, counts, index, segments, prior is not None, bool(y_halos)),
-            out_shape=[sds((variables, rows, lanes), f32)] + [sds((group, chunk, lanes), bf16)] * n_a,
-            in_specs=specs,
-            out_specs=[ANY] + [VMEM] * n_a,
+            functools.partial(stencil_kernel, z_cells, counts, index, segments, bool(y_halos)),
+            out_shape=[sds((variables, chunk, lanes), f32)] + [sds((group, chunk, lanes), bf16)] * n_a,
+            in_specs=[SMEM] + [VMEM] * (len(operands) - 1),
+            out_specs=[VMEM] * (n_a + 1),
             scratch_shapes=[
                 pltpu.VMEM((2, variables, tile + 2 * pad, lanes), f32),
                 pltpu.VMEM((variables, chunk, lanes), f32),
                 pltpu.VMEM((variables, chunk, lanes), f32),
                 pltpu.VMEM((2, variables * SUB, tile // SUB * lanes), f32),
-                pltpu.VMEM((variables, chunk, lanes), f32),
-                pltpu.VMEM((3, chunk, lanes), f32),
-                pltpu.VMEM((variables, chunk, lanes), f32),
-                pltpu.SemaphoreType.DMA((tiles,)),
-                pltpu.SemaphoreType.DMA((tiles,)),
-                pltpu.SemaphoreType.DMA((tiles,)),
             ],
-            input_output_aliases=aliases,
             name="stencil",
             compiler_params=pltpu.CompilerParams(vmem_limit_bytes=20 * MIB),
         )(*operands)
@@ -460,14 +466,23 @@
     z_halos = halo("gz", n_z, early_z)
     x_halos = halo("ga", n_a, x_edges)
     y_halos = halo("gy", n_y, y_faces)
-    results = stencil(0, None, x_halos, z_halos, ())
-    new_fields = results[0]
+    results = stencil(0, x_halos, z_halos, ())
+    news = [results[0]]
     chunks = [exchange(results[1:])]
     late_z, _ = lax.optimization_barrier((tuple(late_z), results[2]))
     z_halos = halo("gz", n_z, late_z)
-    results = stencil(1, new_fields, x_halos, z_halos, y_halos)
-    new_fields = results[0]
+    results = stencil(1, x_halos, z_halos, y_halos)
+    news.append(results[0])
     chunks.append(exchange(results[1:]))
+    new_fields = pl.pallas_call(
+        functools.partial(flush_kernel, plan),
+        out_shape=sds((variables, rows, lanes), f32),
+        in_specs=[VMEM] * len(plan),
+        out_specs=ANY,
+        scratch_shapes=[pltpu.SemaphoreType.DMA((sum(len(segments) for segments in plan),))],
+        name="flush",
+        compiler_params=pltpu.CompilerParams(vmem_limit_bytes=4 * MIB),
+    )(*news)
 
     scratch = [pltpu.VMEM((group * chunk, x_size), bf16), pltpu.VMEM((group * chunk, rank), f32)]
     gram, projs = None, []
@@ -499,7 +514,7 @@
             for d_z in range(n_z):
                 if d_y or d_z:
                     pairs = [
-                        (y * n_z + z, (y + d_y) % n_y * n_z + (z + d_z) % n_z)
+                        (y * n_z + z, partner(n_y, y, d_y) * n_z + partner(n_z, z, d_z))
                         for y in range(n_y)
                         for z in range(n_z)
                     ]
@@ -517,11 +532,11 @@
         received = []
         for d_y in range(n_y):
             for d_z in range(n_z):
-                source = (g_y - d_y + n_y) % n_y * n_z + (g_z - d_z + n_z) % n_z
+                source = origin(n_y, g_y, d_y) * n_z + origin(n_z, g_z, d_z)
                 block = lax.dynamic_index_in_dim(blocks, source, 0, keepdims=False)
                 if d_z == 0:
                     block = jnp.pad(block, ((0, piece_rows - own), (0, 0)))
-                    side = lax.dynamic_index_in_dim(full, (g_y - d_y + n_y) % n_y, 0, keepdims=False)
+                    side = lax.dynamic_index_in_dim(full, origin(n_y, g_y, d_y), 0, keepdims=False)
                     side = jnp.pad(side, ((0, piece_rows - y_cells), (0, 0)))
                     block = jnp.concatenate([block, side], axis=1)
                 received.append(block)

time: 68.2 us -> 66.3 us (0.972)
  waiting for transfers between devices: 25.1 us -> 21.3 us
  starting transfers between devices: 29.1 us -> 31.9 us
  Pallas kernels: 13 us -> 12.2 us
    pallas_call x2, Pallas kernels: 7.24 us -> 4.27 us  [stencil(): pl.pallas_call(functools.partial(stencil_kernel, z_cells, counts, index,...]
    ppermute x7, starting transfers between devices: 5.83 us -> 8.24 us  [shards(): received.append(lax.ppermute(pieces[d_y * n_z + d_z], ('gy', 'gz'), pairs))]
    ppermute x3, waiting for transfers between devices: 9.44 us -> 7.25 us  [shards(): lax.ppermute(payload, 'ga', ring_pairs(n_a, k))]
    pallas_call x1 -> x2, Pallas kernels: 0.29 us -> 2.34 us  [the longest x1 1.33 us: shards(): pl.pallas_call(functools.partial(flush_kernel, plan), out_shape=sds((vari...]
    ppermute x7, waiting for transfers between devices: 5.92 us -> 4.99 us  [shards(): received.append(lax.ppermute(pieces[d_y * n_z + d_z], ('gy', 'gz'), pairs))]
    ppermute x6, waiting for transfers between devices: 2.76 us -> 2.05 us  [halo(): received.append(lax.ppermute(face, axis, swap_pairs(count, turn)))]
  transfers between devices with their start and end apart: 22 -> 22, of which waited for: 8 -> 7; matrix products, arithmetic and copies ran while one was open for 0% -> 0% of each run, Pallas kernels for 7% -> 8%
where the time goes in v2:
time: 66.3 us; the launch traced here: 66.1 us
  starting transfers between devices  31.9 us (48%)
  waiting for transfers between devices  21.3 us (32%)
  Pallas kernels  12.2 us (18%)
  between operations  0.76 us (1%)
    ppermute x6, starting transfers between devices, exchange(): received.append(lax.ppermute(snaps[k], 'ga', ring_pairs(n_a, k)))  9.54 us
    ppermute x6, starting transfers between devices, halo(): received.append(lax.ppermute(face, axis, swap_pairs(count, turn)))  9.29 us
    ppermute x7, starting transfers between devices, shards(): received.append(lax.ppermute(pieces[d_y * n_z + d_z], ('gy', 'gz'), pairs))  8.24 us
    ppermute x3, waiting for transfers between devices, shards(): lax.ppermute(payload, 'ga', ring_pairs(n_a, k))  7.25 us
    ppermute x6, waiting for transfers between devices, exchange(): received.append(lax.ppermute(snaps[k], 'ga', ring_pairs(n_a, k)))  6.99 us
    ppermute x7, waiting for transfers between devices, shards(): received.append(lax.ppermute(pieces[d_y * n_z + d_z], ('gy', 'gz'), pairs))  4.99 us
    ppermute x3, starting transfers between devices, shards(): lax.ppermute(payload, 'ga', ring_pairs(n_a, k))  4.81 us
    pallas_call x2, Pallas kernels, stencil(): pl.pallas_call(functools.partial(stencil_kernel, z_cells, counts, index,...  4.27 us
  transfers between devices with their start and end apart: 22, of which 7 were waited for; matrix products, arithmetic and copies ran while one was open for 0% of the time, Pallas kernels for 8%

profile of v2, /device:TPU:0, one launch (start us, length us, event | category | flops | bytes accessed | tf_op | source)
XLA Modules:
  0.0 66.1 jit_solution(15697913597027608845)
XLA Ops:
  0.7 2.7 %shard_map.94 = (f32[16,256,128]{2,1,0:T(8,128)S(1)}, f32[16,4,128]{2,1,0:T(4,128)S(1)}, f32[16,4,128]{2,1,0:T(4,128)S(1)}, f32[2,2048]{1,0:T(2,128)S(1)}, f32[2...) custom-call(f32[16,256,128]{2,1,0:T(8,128)} %bitcast.12), custom_call_target="tpu_custom_call" | custom-call | tf_op jit(solution)/shard_map/pallas_call | solution.py:413
  3.4 3.1 %collective-permute-start.2 = (bf16[16,32,128]{2,1,0:T(8,128)(2,1)S(1)}, bf16[16,32,128]{2,1,0:T(8,128)(2,1)S(1)}, u32[]{:S(2)}, u32[]{:S(2)}) collective-permute-start(bf16[16,32,128]{2,1,0:T(8,128)(2,1)S(1)} %get-tuple-element.41), channel_id=1, source_target_pairs={{0,4},{4,0},{1,5},{5,1},{2,6},{6,2},{3,7},{7,3},{8,12},{12,8},{9,1... | collective-permute-start | bytes 393224 | tf_op jit(solution)/shard_map/ppermute | solution.py:430
  6.5 1.6 %collective-permute-start = (f32[2,2048]{1,0:T(2,128)S(1)}, f32[2,2048]{1,0:T(2,128)S(1)}, u32[]{:S(2)}, u32[]{:S(2)}) collective-permute-start(f32[2,2048]{1,0:T(2,128)S(1)} %get-tuple-element.39), channel_id=1, source_target_pairs={{0,1},{1,0},{2,3},{3,2},{4,5},{5,4},{6,7},{7,6},{8,9},{9,8},{10,11... | collective-permute-start | bytes 49160 | tf_op jit(solution)/shard_map/ppermute | solution.py:430
  8.0 2.5 %collective-permute-start.1 = (f32[2,2048]{1,0:T(2,128)S(1)}, f32[2,2048]{1,0:T(2,128)S(1)}, u32[]{:S(2)}, u32[]{:S(2)}) collective-permute-start(f32[2,2048]{1,0:T(2,128)S(1)} %get-tuple-element.40), channel_id=1, source_target_pairs={{0,3},{1,2},{2,1},{3,0},{4,7},{5,6},{6,5},{7,4},{8,11},{9,10},{10,... | collective-permute-start | bytes 49160 | tf_op jit(solution)/shard_map/ppermute | solution.py:430
  10.5 1.0 %shard_map.95 = (bf16[256,256]{1,0:T(8,128)(2,1)S(1)}, f32[3,256,128]{2,1,0:T(8,128)S(1)}) custom-call(f32[16,16]{1,0:T(8,128)S(1)} %copy-done.3, f32[3,256,128]{2,1,0:T(8,128)} %bitcast.14, f32[16,4,128]{2,1,0:T(4,128)S(1)} %get-tuple-element.35.after), custom_call_target="tpu_custom_call" | custom-call | tf_op jit(solution)/shard_map/pallas_call | solution.py:433
  11.5 2.0 %collective-permute-done.1.rest_1_ = f32[2,2048]{1,0:T(2,128)S(1)} collective-permute-done((f32[2,2048]{1,0:T(2,128)S(1)}, f32[2,2048]{1,0:T(2,128)S(1)}, u32[]{:S(2)}, u32[]{:S(2)}) %collective-permute-start.1) | collective-permute-done | bytes 16416 | tf_op jit(solution)/shard_map/ppermute | solution.py:430
  13.6 2.1 %stencil.2 = (f32[16,128,128]{2,1,0:T(8,128)S(1)}, bf16[4,128,128]{2,1,0:T(8,128)(2,1)S(1)}, bf16[4,128,128]{2,1,0:T(8,128)(2,1)S(1)}, bf16[4,128,128]{2,1,0:T(8,128)(2,1)S(1)}, bf16[4,128,128]{2,1,0:T(8,128)(2,1)S(1)}) custom-call(f32[16]{0:T(128)S(1)} %copy-done.4, f32[3,256,128]{2,1,0:T(8,128)S(1)} %get-tuple-element.36.vel_ref, ...), custom_call_target="tpu_custom_call" | custom-call | tf_op jit(solution)/shard_map/stencil/pallas_call | solution.py:444
  17.1 1.6 %collective-permute-start.4 = (f32[16,4,128]{2,1,0:T(4,128)S(1)}, f32[16,4,128]{2,1,0:T(4,128)S(1)}, u32[]{:S(2)}, u32[]{:S(2)}) collective-permute-start(f32[16,4,128]{2,1,0:T(4,128)S(1)} %get-tuple-element.35.after), channel_id=1, source_target_pairs={{0,8},{8,0},{16,24},{24,16},{1,9},{9,1},{17,25},{25,17},{2,10},{10... | collective-permute-start | bytes 98312 | tf_op jit(solution)/shard_map/ppermute | solution.py:430
  18.7 2.3 %collective-permute-start.9 = (bf16[4,128,128]{2,1,0:T(8,128)(2,1)S(1)}, bf16[4,128,128]{2,1,0:T(8,128)(2,1)S(1)}, u32[]{:S(2)}, u32[]{:S(2)}) collective-permute-start(bf16[4,128,128]{2,1,0:T(8,128)(2,1)S(1)} %get-tuple-element.44), channel_id=1, source_target_pairs={{0,1},{1,2},{2,3},{3,0},{4,5},{5,6},{6,7},{7,4},{8,9},{9,10},{10,1... | collective-permute-start | bytes 393224 | tf_op jit(solution)/shard_map/ppermute | solution.py:462
  21.0 1.6 %collective-permute-start.11 = (bf16[4,128,128]{2,1,0:T(8,128)(2,1)S(1)}, bf16[4,128,128]{2,1,0:T(8,128)(2,1)S(1)}, u32[]{:S(2)}, u32[]{:S(2)}) collective-permute-start(bf16[4,128,128]{2,1,0:T(8,128)(2,1)S(1)} %get-tuple-element.54), channel_id=1, source_target_pairs={{0,3},{1,0},{2,1},{3,2},{4,7},{5,4},{6,5},{7,6},{8,11},{9,8},{10,9... | collective-permute-start | bytes 393224 | tf_op jit(solution)/shard_map/ppermute | solution.py:462
  22.5 2.2 %stencil.3 = (f32[16,128,128]{2,1,0:T(8,128)S(1)}, bf16[4,128,128]{2,1,0:T(8,128)(2,1)S(1)}, bf16[4,128,128]{2,1,0:T(8,128)(2,1)S(1)}, bf16[4,128,128]{2,1,0:T(8,128)(2,1)S(1)}, bf16[4,128,128]{2,1,0:T(8,128)(2,1)S(1)}) custom-call(f32[16]{0:T(128)S(1)} %copy-done.4, f32[3,256,128]{2,1,0:T(8,128)S(1)} %get-tuple-element.36.vel_ref, ...), custom_call_target="tpu_custom_call" | custom-call | tf_op jit(solution)/shard_map/stencil/pallas_call | solution.py:444
  25.3 1.9 %collective-permute-start.7 = (bf16[4,128,128]{2,1,0:T(8,128)(2,1)S(1)}, bf16[4,128,128]{2,1,0:T(8,128)(2,1)S(1)}, u32[]{:S(2)}, u32[]{:S(2)}) collective-permute-start(bf16[4,128,128]{2,1,0:T(8,128)(2,1)S(1)} %get-tuple-element.50), channel_id=1, source_target_pairs={{0,2},{1,3},{2,0},{3,1},{4,6},{5,7},{6,4},{7,5},{8,10},{9,11},{10,... | collective-permute-start | bytes 393224 | tf_op jit(solution)/shard_map/ppermute | solution.py:462
  27.2 2.5 %collective-permute-start.8 = (bf16[4,128,128]{2,1,0:T(8,128)(2,1)S(1)}, bf16[4,128,128]{2,1,0:T(8,128)(2,1)S(1)}, u32[]{:S(2)}, u32[]{:S(2)}) collective-permute-start(bf16[4,128,128]{2,1,0:T(8,128)(2,1)S(1)} %get-tuple-element.51), channel_id=1, source_target_pairs={{0,3},{1,0},{2,1},{3,2},{4,7},{5,4},{6,5},{7,6},{8,11},{9,8},{10,9... | collective-permute-start | bytes 393224 | tf_op jit(solution)/shard_map/ppermute | solution.py:462
  30.5 2.5 %collective-permute-done.6.refs_1_ = bf16[4,128,128]{2,1,0:T(8,128)(2,1)S(1)} collective-permute-done((bf16[4,128,128]{2,1,0:T(8,128)(2,1)S(1)}, bf16[4,128,128]{2,1,0:T(8,128)(2,1)S(1)}, u32[]{:S(2)}, u32[]{:S(2)}) %collective-permute-start.6) | collective-permute-done | bytes 131104 | tf_op jit(solution)/shard_map/ppermute | solution.py:462
  33.0 4.5 %collective-permute-done.7.refs_2_ = bf16[4,128,128]{2,1,0:T(8,128)(2,1)S(1)} collective-permute-done((bf16[4,128,128]{2,1,0:T(8,128)(2,1)S(1)}, bf16[4,128,128]{2,1,0:T(8,128)(2,1)S(1)}, u32[]{:S(2)}, u32[]{:S(2)}) %collective-permute-start.7) | collective-permute-done | bytes 131104 | tf_op jit(solution)/shard_map/ppermute | solution.py:462
  38.2 1.5 %collective-permute-start.12 = (bf16[64,512]{1,0:T(8,128)(2,1)S(1)}, bf16[64,512]{1,0:T(8,128)(2,1)S(1)}, u32[]{:S(2)}, u32[]{:S(2)}) collective-permute-start(bf16[64,512]{1,0:T(8,128)(2,1)S(1)} %get-tuple-element.58), channel_id=1, source_target_pairs={{0,4},{4,0},{8,12},{12,8},{16,20},{20,16},{24,28},{28,24},{1,5},{5... | collective-permute-start | bytes 196616 | tf_op jit(solution)/shard_map/ppermute | solution.py:521
  40.4 2.2 %collective-permute-start.15 = (bf16[64,768]{1,0:T(8,128)(2,1)S(1)}, bf16[64,768]{1,0:T(8,128)(2,1)S(1)}, u32[]{:S(2)}, u32[]{:S(2)}) collective-permute-start(bf16[64,768]{1,0:T(8,128)(2,1)S(1)} %get-tuple-element.61), channel_id=1, source_target_pairs={{0,16},{4,20},{8,24},{12,28},{16,0},{20,4},{24,8},{28,12},{1,17},{... | collective-permute-start | bytes 294920 | tf_op jit(solution)/shard_map/ppermute | solution.py:521
  42.6 3.7 %collective-permute-start.16 = (bf16[64,512]{1,0:T(8,128)(2,1)S(1)}, bf16[64,512]{1,0:T(8,128)(2,1)S(1)}, u32[]{:S(2)}, u32[]{:S(2)}) collective-permute-start(bf16[64,512]{1,0:T(8,128)(2,1)S(1)} %get-tuple-element.62), channel_id=1, source_target_pairs={{0,20},{4,16},{8,28},{12,24},{16,4},{20,0},{24,12},{28,8},{1,21},{... | collective-permute-start | bytes 196616 | tf_op jit(solution)/shard_map/ppermute | solution.py:521
  46.5 3.5 %collective-permute-done.16.refs_5_ = bf16[64,512]{1,0:T(8,128)(2,1)S(1)} collective-permute-done((bf16[64,512]{1,0:T(8,128)(2,1)S(1)}, bf16[64,512]{1,0:T(8,128)(2,1)S(1)}, u32[]{:S(2)}, u32[]{:S(2)}) %collective-permute-start.16) | collective-permute-done | bytes 65568 | tf_op jit(solution)/shard_map/ppermute | solution.py:521
  50.0 1.4 %collective-permute-done.18.refs_7_ = bf16[64,512]{1,0:T(8,128)(2,1)S(1)} collective-permute-done((bf16[64,512]{1,0:T(8,128)(2,1)S(1)}, bf16[64,512]{1,0:T(8,128)(2,1)S(1)}, u32[]{:S(2)}, u32[]{:S(2)}) %collective-permute-start.18) | collective-permute-done | bytes 65568 | tf_op jit(solution)/shard_map/ppermute | solution.py:521
  52.0 4.2 %collective-permute-start.21 = (bf16[64,768]{1,0:T(8,128)(2,1)S(1)}, bf16[64,768]{1,0:T(8,128)(2,1)S(1)}, u32[]{:S(2)}, u32[]{:S(2)}) collective-permute-start(bf16[64,768]{1,0:T(8,128)(2,1)S(1)} %shard_map.98.refs_0_), channel_id=1, source_target_pairs={{0,3},{1,0},{2,1},{3,2},{4,7},{5,4},{6,5},{7,6},{8,11},{9,8},{10,9... | collective-permute-start | bytes 294920 | tf_op jit(solution)/shard_map/ppermute | solution.py:551
  56.8 1.3 %flush.1 = f32[16,256,128]{2,1,0:T(8,128)} custom-call(f32[16,128,128]{2,1,0:T(8,128)S(1)} %get-tuple-element.42.refs_0_, f32[16,128,128]{2,1,0:T(8,128)S(1)} %get-tuple-element.47.refs_1_), custom_call_target="tpu_custom_call" | custom-call | tf_op jit(solution)/shard_map/flush/pallas_call | solution.py:477
  58.2 1.2 %collective-permute-done.21.refs_3_ = bf16[64,768]{1,0:T(8,128)(2,1)S(1)} collective-permute-done((bf16[64,768]{1,0:T(8,128)(2,1)S(1)}, bf16[64,768]{1,0:T(8,128)(2,1)S(1)}, u32[]{:S(2)}, u32[]{:S(2)}) %collective-permute-start.21) | collective-permute-done | bytes 98336 | tf_op jit(solution)/shard_map/ppermute | solution.py:551
  59.4 6.0 %collective-permute-done.20.refs_2_ = bf16[64,768]{1,0:T(8,128)(2,1)S(1)} collective-permute-done((bf16[64,768]{1,0:T(8,128)(2,1)S(1)}, bf16[64,768]{1,0:T(8,128)(2,1)S(1)}, u32[]{:S(2)}, u32[]{:S(2)}) %collective-permute-start.20) | collective-permute-done | bytes 98336 | tf_op jit(solution)/shard_map/ppermute | solution.py:551
  (39 shorter events, 6.2 us)
Async XLA Ops:
  0.6 12.9 %copy-start.4 = (f32[16]{0:T(128)S(1)}, f32[16]{0:T(128)}, u32[]{:S(2)}) copy-start(f32[16]{0:T(128)} %diffusion.3) | copy-start | bytes 196
  3.4 10.2 %collective-permute-start.2 = (bf16[16,32,128]{2,1,0:T(8,128)(2,1)S(1)}, bf16[16,32,128]{2,1,0:T(8,128)(2,1)S(1)}, u32[]{:S(2)}, u32[]{:S(2)}) collective-permute-start(bf16[16,32,128]{2,1,0:T(8,128)(2,1)S(1)} %get-tuple-element.41), channel_id=1, source_target_pairs={{0,4},{4,0},{1,5},{5,1},{2,6},{6,2},{3,7},{7,3},{8,12},{12,8},{9,1... | collective-permute-start | bytes 393224 | tf_op jit(solution)/shard_map/ppermute | solution.py:430
  6.5 5.1 %collective-permute-start = (f32[2,2048]{1,0:T(2,128)S(1)}, f32[2,2048]{1,0:T(2,128)S(1)}, u32[]{:S(2)}, u32[]{:S(2)}) collective-permute-start(f32[2,2048]{1,0:T(2,128)S(1)} %get-tuple-element.39), channel_id=1, source_target_pairs={{0,1},{1,0},{2,3},{3,2},{4,5},{5,4},{6,7},{7,6},{8,9},{9,8},{10,11... | collective-permute-start | bytes 49160 | tf_op jit(solution)/shard_map/ppermute | solution.py:430
  8.0 5.5 %collective-permute-start.1 = (f32[2,2048]{1,0:T(2,128)S(1)}, f32[2,2048]{1,0:T(2,128)S(1)}, u32[]{:S(2)}, u32[]{:S(2)}) collective-permute-start(f32[2,2048]{1,0:T(2,128)S(1)} %get-tuple-element.40), channel_id=1, source_target_pairs={{0,3},{1,2},{2,1},{3,0},{4,7},{5,6},{6,5},{7,4},{8,11},{9,10},{10,... | collective-permute-start | bytes 49160 | tf_op jit(solution)/shard_map/ppermute | solution.py:430
  15.7 6.8 %collective-permute-start.3 = (bf16[16,32,128]{2,1,0:T(8,128)(2,1)S(1)}, bf16[16,32,128]{2,1,0:T(8,128)(2,1)S(1)}, u32[]{:S(2)}, u32[]{:S(2)}) collective-permute-start(bf16[16,32,128]{2,1,0:T(8,128)(2,1)S(1)} %get-tuple-element.45), channel_id=1, source_target_pairs={{0,4},{4,0},{1,5},{5,1},{2,6},{6,2},{3,7},{7,3},{8,12},{12,8},{9,1... | collective-permute-start | bytes 393224 | tf_op jit(solution)/shard_map/ppermute | solution.py:430
  16.3 10.9 %collective-permute-start.10 = (bf16[4,128,128]{2,1,0:T(8,128)(2,1)S(1)}, bf16[4,128,128]{2,1,0:T(8,128)(2,1)S(1)}, u32[]{:S(2)}, u32[]{:S(2)}) collective-permute-start(bf16[4,128,128]{2,1,0:T(8,128)(2,1)S(1)} %get-tuple-element.53), channel_id=1, source_target_pairs={{0,2},{1,3},{2,0},{3,1},{4,6},{5,7},{6,4},{7,5},{8,10},{9,11},{10,... | collective-permute-start | bytes 393224 | tf_op jit(solution)/shard_map/ppermute | solution.py:462
  17.1 3.9 %collective-permute-start.5 = (f32[16,4,128]{2,1,0:T(4,128)S(1)}, f32[16,4,128]{2,1,0:T(4,128)S(1)}, u32[]{:S(2)}, u32[]{:S(2)}) collective-permute-start(f32[16,4,128]{2,1,0:T(4,128)S(1)} %get-tuple-element.46), channel_id=1, source_target_pairs={{0,24},{8,16},{16,8},{24,0},{1,25},{9,17},{17,9},{25,1},{2,26},{10... | collective-permute-start | bytes 98312 | tf_op jit(solution)/shard_map/ppermute | solution.py:430
  17.1 5.4 %collective-permute-start.4 = (f32[16,4,128]{2,1,0:T(4,128)S(1)}, f32[16,4,128]{2,1,0:T(4,128)S(1)}, u32[]{:S(2)}, u32[]{:S(2)}) collective-permute-start(f32[16,4,128]{2,1,0:T(4,128)S(1)} %get-tuple-element.35.after), channel_id=1, source_target_pairs={{0,8},{8,0},{16,24},{24,16},{1,9},{9,1},{17,25},{25,17},{2,10},{10... | collective-permute-start | bytes 98312 | tf_op jit(solution)/shard_map/ppermute | solution.py:430
  18.7 10.9 %collective-permute-start.9 = (bf16[4,128,128]{2,1,0:T(8,128)(2,1)S(1)}, bf16[4,128,128]{2,1,0:T(8,128)(2,1)S(1)}, u32[]{:S(2)}, u32[]{:S(2)}) collective-permute-start(bf16[4,128,128]{2,1,0:T(8,128)(2,1)S(1)} %get-tuple-element.44), channel_id=1, source_target_pairs={{0,1},{1,2},{2,3},{3,0},{4,5},{5,6},{6,7},{7,4},{8,9},{9,10},{10,1... | collective-permute-start | bytes 393224 | tf_op jit(solution)/shard_map/ppermute | solution.py:462
  21.0 8.7 %collective-permute-start.11 = (bf16[4,128,128]{2,1,0:T(8,128)(2,1)S(1)}, bf16[4,128,128]{2,1,0:T(8,128)(2,1)S(1)}, u32[]{:S(2)}, u32[]{:S(2)}) collective-permute-start(bf16[4,128,128]{2,1,0:T(8,128)(2,1)S(1)} %get-tuple-element.54), channel_id=1, source_target_pairs={{0,3},{1,0},{2,1},{3,2},{4,7},{5,4},{6,5},{7,6},{8,11},{9,8},{10,9... | collective-permute-start | bytes 393224 | tf_op jit(solution)/shard_map/ppermute | solution.py:462
  24.7 26.8 %copy-start.2 = (f32[256,64]{0,1:T(8,128)S(1)}, f32[256,64]{0,1:T(8,128)}, u32[]{:S(2)}) copy-start(f32[256,64]{0,1:T(8,128)} %param.13) | copy-start | bytes 196612
  24.7 8.3 %collective-permute-start.6 = (bf16[4,128,128]{2,1,0:T(8,128)(2,1)S(1)}, bf16[4,128,128]{2,1,0:T(8,128)(2,1)S(1)}, u32[]{:S(2)}, u32[]{:S(2)}) collective-permute-start(bf16[4,128,128]{2,1,0:T(8,128)(2,1)S(1)} %get-tuple-element.49), channel_id=1, source_target_pairs={{0,1},{1,2},{2,3},{3,0},{4,5},{5,6},{6,7},{7,4},{8,9},{9,10},{10,1... | collective-permute-start | bytes 393224 | tf_op jit(solution)/shard_map/ppermute | solution.py:462
  25.3 12.2 %collective-permute-start.7 = (bf16[4,128,128]{2,1,0:T(8,128)(2,1)S(1)}, bf16[4,128,128]{2,1,0:T(8,128)(2,1)S(1)}, u32[]{:S(2)}, u32[]{:S(2)}) collective-permute-start(bf16[4,128,128]{2,1,0:T(8,128)(2,1)S(1)} %get-tuple-element.50), channel_id=1, source_target_pairs={{0,2},{1,3},{2,0},{3,1},{4,6},{5,7},{6,4},{7,5},{8,10},{9,11},{10,... | collective-permute-start | bytes 393224 | tf_op jit(solution)/shard_map/ppermute | solution.py:462
  27.2 10.3 %collective-permute-start.8 = (bf16[4,128,128]{2,1,0:T(8,128)(2,1)S(1)}, bf16[4,128,128]{2,1,0:T(8,128)(2,1)S(1)}, u32[]{:S(2)}, u32[]{:S(2)}) collective-permute-start(bf16[4,128,128]{2,1,0:T(8,128)(2,1)S(1)} %get-tuple-element.51), channel_id=1, source_target_pairs={{0,3},{1,0},{2,1},{3,2},{4,7},{5,4},{6,5},{7,6},{8,11},{9,8},{10,9... | collective-permute-start | bytes 393224 | tf_op jit(solution)/shard_map/ppermute | solution.py:462
  38.2 4.4 %collective-permute-start.12 = (bf16[64,512]{1,0:T(8,128)(2,1)S(1)}, bf16[64,512]{1,0:T(8,128)(2,1)S(1)}, u32[]{:S(2)}, u32[]{:S(2)}) collective-permute-start(bf16[64,512]{1,0:T(8,128)(2,1)S(1)} %get-tuple-element.58), channel_id=1, source_target_pairs={{0,4},{4,0},{8,12},{12,8},{16,20},{20,16},{24,28},{28,24},{1,5},{5... | collective-permute-start | bytes 196616 | tf_op jit(solution)/shard_map/ppermute | solution.py:521
  39.8 6.6 %collective-permute-start.14 = (bf16[64,512]{1,0:T(8,128)(2,1)S(1)}, bf16[64,512]{1,0:T(8,128)(2,1)S(1)}, u32[]{:S(2)}, u32[]{:S(2)}) collective-permute-start(bf16[64,512]{1,0:T(8,128)(2,1)S(1)} %get-tuple-element.60), channel_id=1, source_target_pairs={{0,12},{4,8},{8,4},{12,0},{16,28},{20,24},{24,20},{28,16},{1,13},{... | collective-permute-start | bytes 196616 | tf_op jit(solution)/shard_map/ppermute | solution.py:521
  39.8 11.7 %collective-permute-start.13 = (bf16[64,768]{1,0:T(8,128)(2,1)S(1)}, bf16[64,768]{1,0:T(8,128)(2,1)S(1)}, u32[]{:S(2)}, u32[]{:S(2)}) collective-permute-start(bf16[64,768]{1,0:T(8,128)(2,1)S(1)} %get-tuple-element.59), channel_id=1, source_target_pairs={{0,8},{4,12},{8,0},{12,4},{16,24},{20,28},{24,16},{28,20},{1,9},{5... | collective-permute-start | bytes 294920 | tf_op jit(solution)/shard_map/ppermute | solution.py:521
  40.4 11.0 %collective-permute-start.15 = (bf16[64,768]{1,0:T(8,128)(2,1)S(1)}, bf16[64,768]{1,0:T(8,128)(2,1)S(1)}, u32[]{:S(2)}, u32[]{:S(2)}) collective-permute-start(bf16[64,768]{1,0:T(8,128)(2,1)S(1)} %get-tuple-element.61), channel_id=1, source_target_pairs={{0,16},{4,20},{8,24},{12,28},{16,0},{20,4},{24,8},{28,12},{1,17},{... | collective-permute-start | bytes 294920 | tf_op jit(solution)/shard_map/ppermute | solution.py:521
  42.6 8.8 %collective-permute-start.17 = (bf16[64,768]{1,0:T(8,128)(2,1)S(1)}, bf16[64,768]{1,0:T(8,128)(2,1)S(1)}, u32[]{:S(2)}, u32[]{:S(2)}) collective-permute-start(bf16[64,768]{1,0:T(8,128)(2,1)S(1)} %get-tuple-element.63), channel_id=1, source_target_pairs={{0,24},{4,28},{8,16},{12,20},{16,8},{20,12},{24,0},{28,4},{1,25},{... | collective-permute-start | bytes 294920 | tf_op jit(solution)/shard_map/ppermute | solution.py:521
  42.6 7.4 %collective-permute-start.16 = (bf16[64,512]{1,0:T(8,128)(2,1)S(1)}, bf16[64,512]{1,0:T(8,128)(2,1)S(1)}, u32[]{:S(2)}, u32[]{:S(2)}) collective-permute-start(bf16[64,512]{1,0:T(8,128)(2,1)S(1)} %get-tuple-element.62), channel_id=1, source_target_pairs={{0,20},{4,16},{8,28},{12,24},{16,4},{20,0},{24,12},{28,8},{1,21},{... | collective-permute-start | bytes 196616 | tf_op jit(solution)/shard_map/ppermute | solution.py:521
  46.3 5.1 %collective-permute-start.18 = (bf16[64,512]{1,0:T(8,128)(2,1)S(1)}, bf16[64,512]{1,0:T(8,128)(2,1)S(1)}, u32[]{:S(2)}, u32[]{:S(2)}) collective-permute-start(bf16[64,512]{1,0:T(8,128)(2,1)S(1)} %get-tuple-element.64), channel_id=1, source_target_pairs={{0,28},{4,24},{8,20},{12,16},{16,12},{20,8},{24,4},{28,0},{1,29},{... | collective-permute-start | bytes 196616 | tf_op jit(solution)/shard_map/ppermute | solution.py:521
  52.0 7.4 %collective-permute-start.21 = (bf16[64,768]{1,0:T(8,128)(2,1)S(1)}, bf16[64,768]{1,0:T(8,128)(2,1)S(1)}, u32[]{:S(2)}, u32[]{:S(2)}) collective-permute-start(bf16[64,768]{1,0:T(8,128)(2,1)S(1)} %shard_map.98.refs_0_), channel_id=1, source_target_pairs={{0,3},{1,0},{2,1},{3,2},{4,7},{5,4},{6,5},{7,6},{8,11},{9,8},{10,9... | collective-permute-start | bytes 294920 | tf_op jit(solution)/shard_map/ppermute | solution.py:551
  56.2 9.2 %collective-permute-start.20 = (bf16[64,768]{1,0:T(8,128)(2,1)S(1)}, bf16[64,768]{1,0:T(8,128)(2,1)S(1)}, u32[]{:S(2)}, u32[]{:S(2)}) collective-permute-start(bf16[64,768]{1,0:T(8,128)(2,1)S(1)} %shard_map.98.refs_0_), channel_id=1, source_target_pairs={{0,2},{1,3},{2,0},{3,1},{4,6},{5,7},{6,4},{7,5},{8,10},{9,11},{10,... | collective-permute-start | bytes 294920 | tf_op jit(solution)/shard_map/ppermute | solution.py:551
  56.2 9.2 %collective-permute-start.19 = (bf16[64,768]{1,0:T(8,128)(2,1)S(1)}, bf16[64,768]{1,0:T(8,128)(2,1)S(1)}, u32[]{:S(2)}, u32[]{:S(2)}) collective-permute-start(bf16[64,768]{1,0:T(8,128)(2,1)S(1)} %shard_map.98.refs_0_), channel_id=1, source_target_pairs={{0,1},{1,2},{2,3},{3,0},{4,5},{5,6},{6,7},{7,4},{8,9},{9,10},{10,1... | collective-permute-start | bytes 294920 | tf_op jit(solution)/shard_map/ppermute | solution.py:551
  (3 other events, 31.5 us)

commit v3 on v2

--- a/solution.py
+++ b/solution.py
@@ -24,12 +24,6 @@
     if turn == 0:
         return [(i, i ^ 1) for i in range(count)]
     return [(i, (i + (1 if i % 2 else -1)) % count) for i in range(count)]
-
-
-def partner(count, index, step):
-    if count & (count - 1) == 0:
-        return index ^ step
-    return (index + step) % count
 
 
 def origin(count, index, step):
@@ -297,7 +291,7 @@
     pieces, refs = refs[:parts], refs[parts:]
     prior, refs = refs[0], refs[1:]
     prior_proj, refs = refs[:priors], refs[priors:]
-    outs, (wide, proj, gram, full) = refs[: n_y * n_z], refs[n_y * n_z :]
+    outs, (wide, proj, gram, full) = refs[:2], refs[2:]
     group, rows, _ = pieces[0].shape
     me, my_y, my_z = (lax.axis_index(a) for a in ("ga", "gy", "gz"))
     gather_rows(parts, me, pieces, wide)
@@ -321,33 +315,51 @@
     width = gram.shape[1]
     layers = z_cells // n_y
     cols = full.shape[2]
-    for d_y in range(n_y):
-        for d_z in range(n_z):
-            out = outs[d_y * n_z + d_z]
-            y_to, z_to = partner(n_y, my_y, d_y), partner(n_z, my_z, d_z)
-            at = pl.multiple_of((y_to * n_z + z_to) * own, own)
-            out[:own, :width] = gram[pl.ds(at, own), :].astype(bf16)
-            if d_z == 0:
-                for layer in range(layers):
-                    out[: full.shape[1], width + layer * cols : width + (layer + 1) * cols] = full[
-                        y_to * layers + layer
-                    ]
-
-
-def layer_kernel(n_y, n_z, own, layers, y_scale, x_scale, yf_ref, *refs):
-    pieces, (out_ref, m_ref) = refs[: n_y * n_z], refs[n_y * n_z :]
+    y_cells = full.shape[1]
+    for flip, out in enumerate(outs):
+        out[...] = jnp.zeros_like(out)
+        for d_x in range(n_y // 2):
+            for d_z in range(n_z):
+                block = d_x * n_z + d_z
+                y_to, z_to = my_y ^ (2 * d_x + flip), my_z ^ d_z
+                at = pl.multiple_of((y_to * n_z + z_to) * own, own)
+                out[block, :own, :width] = gram[pl.ds(at, own), :].astype(bf16)
+                if d_z == 0:
+                    for layer in range(layers):
+                        out[block, :y_cells, width + layer * cols : width + (layer + 1) * cols] = full[
+                            y_to * layers + layer
+                        ]
+
+
+def pair_kernel(n_z, own, width, keep_ref, other_ref, *outs):
+    for block, out in enumerate(outs):
+        both = keep_ref[block, :own, :width].astype(f32) + other_ref[block, :own, :width].astype(f32)
+        if block % n_z:
+            out[...] = both.astype(bf16)
+        else:
+            side = keep_ref.shape[2] - width
+            if out.shape[0] != own:
+                out[...] = jnp.zeros_like(out)
+            out[:own, :width] = both.astype(bf16)
+            out[:, width : width + side] = keep_ref[block, :, width:]
+            out[:, width + side :] = other_ref[block, :, width:]
+
+
+def layer_kernel(n_y, n_z, paired, own, layers, y_scale, x_scale, yf_ref, *refs):
+    pieces, (out_ref, m_ref) = refs[:-2], refs[-2:]
     rank, y_size = yf_ref.shape
     y_cells = y_size // n_y
     cols = m_ref.shape[2]
-    width = pieces[0].shape[1] - layers * cols
+    senders = 2 if paired else 1
+    width = pieces[0].shape[1] - senders * layers * cols
     my_y = lax.axis_index("gy")
-    for d_y in range(n_y):
-        source = origin(n_y, my_y, d_y)
-        at = pl.multiple_of(source * y_cells, y_cells)
-        for layer in range(layers):
-            m_ref[layer, pl.ds(at, y_cells), :] = pieces[d_y * n_z][
-                :y_cells, width + layer * cols : width + (layer + 1) * cols
-            ]
+    for d in range(n_y // senders):
+        for sender in range(senders):
+            source = my_y ^ (2 * d + sender) if paired else origin(n_y, my_y, d)
+            at = pl.multiple_of(source * y_cells, y_cells)
+            for layer in range(layers):
+                start = width + (sender * layers + layer) * cols
+                m_ref[layer, pl.ds(at, y_cells), :] = pieces[d * n_z][:y_cells, start : start + cols]
     for layer in range(layers):
         m = m_ref[layer]
         y_gram = lax.dot_general(m, m, (((1,), (1,)), ((), ())), preferred_element_type=f32) * y_scale
@@ -359,8 +371,8 @@
             out_ref[...] = jnp.zeros_like(out_ref)
         out_ref[:rank, width + layer * y_size : width + (layer + 1) * y_size] = prod.astype(bf16)
     total = pieces[0][:own, :width].astype(f32)
-    for i in range(1, n_y * n_z):
-        total = total + pieces[i][:own, :width].astype(f32)
+    for piece in pieces[1:]:
+        total = total + piece[:own, :width].astype(f32)
     out_ref[:own, :width] = (total * x_scale).astype(bf16)
 
 
@@ -486,7 +498,7 @@
 
     scratch = [pltpu.VMEM((group * chunk, x_size), bf16), pltpu.VMEM((group * chunk, rank), f32)]
     gram, projs = None, []
-    direct = owners <= 8
+    direct = owners <= 8 and n_y in (2, 4, 8) and n_z in (1, 2, 4)
     for index in range(len(plan) - 1 if direct else len(plan)):
         gram, proj = call(
             functools.partial(part_gram_kernel, z_cells, n_a, gram is not None),
@@ -498,27 +510,30 @@
     cols = layers * group * rank
     piece_rows = max(own, y_cells)
     if direct:
-        pieces = call(
+        blocks = n_y // 2 * n_z
+        keep, send = call(
             functools.partial(last_gram_kernel, z_cells, n_a, n_y, n_z, plan),
-            [
-                sds((piece_rows if d_z == 0 else own, x_size + (cols if d_z == 0 else 0)), bf16)
-                for _ in range(n_y)
-                for d_z in range(n_z)
-            ],
+            [sds((blocks, piece_rows, x_size + cols), bf16)] * 2,
             [VMEM] * (n_a + 2 + len(projs)),
             scratch=scratch
             + [pltpu.VMEM((x_size, x_size), f32), pltpu.VMEM((z_cells, y_cells, group * rank), bf16)],
         )(x_factor.T, *chunks[-1], gram, *projs)
-        received = [pieces[0]]
-        for d_y in range(n_y):
-            for d_z in range(n_z):
-                if d_y or d_z:
-                    pairs = [
-                        (y * n_z + z, partner(n_y, y, d_y) * n_z + partner(n_z, z, d_z))
-                        for y in range(n_y)
-                        for z in range(n_z)
-                    ]
-                    received.append(lax.ppermute(pieces[d_y * n_z + d_z], ("gy", "gz"), pairs))
+        other = lax.ppermute(send, "gy", swap_pairs(n_y, 0))
+        sums = call(
+            functools.partial(pair_kernel, n_z, own, x_size),
+            [
+                sds((own, x_size), bf16) if block % n_z else sds((piece_rows, x_size + 2 * cols), bf16)
+                for block in range(blocks)
+            ],
+            [VMEM] * 2,
+        )(keep, other)
+        received = [sums[0]]
+        for block in range(1, blocks):
+            d_x, d_z = block // n_z, block % n_z
+            pairs = [
+                (y * n_z + z, (y ^ (2 * d_x)) * n_z + (z ^ d_z)) for y in range(n_y) for z in range(n_z)
+            ]
+            received.append(lax.ppermute(sums[block], ("gy", "gz"), pairs))
     else:
         half = quarter // z_cells
         proj = jnp.concatenate([projs[1][:, :half], projs[0], projs[1][:, half:]], axis=1)
@@ -542,10 +557,10 @@
                 received.append(block)
     payload = call(
         functools.partial(
-            layer_kernel, n_y, n_z, own, layers, 1.0 / (variables * rank), 1.0 / (variables * rows * owners)
+            layer_kernel, n_y, n_z, direct, own, layers, 1.0 / (variables * rank), 1.0 / (variables * rows * owners)
         ),
         [sds((max(own, y_rank), x_size + layers * y_size), bf16)],
-        [VMEM] * (1 + owners),
+        [VMEM] * (1 + len(received)),
         scratch=[pltpu.VMEM((layers, y_size, group * rank), bf16)],
     )(y_factor.T, *received)[0]
     payloads = [payload] + [lax.ppermute(payload, "ga", ring_pairs(n_a, k)) for k in range(1, n_a)]

time: 66.3 us -> 62.6 us (0.944)
  starting transfers between devices: 31.9 us -> 27.3 us
  waiting for transfers between devices: 21.3 us -> 22.1 us
    ppermute x7 -> x4, starting transfers between devices: 8.24 us -> 3.88 us  [the longest x3 3.81 us: shards(): received.append(lax.ppermute(sums[block], ('gy', 'gz'), pairs))]
    ppermute x7 -> x4, waiting for transfers between devices: 4.99 us -> 6.85 us  [the longest x3 5.14 us: shards(): received.append(lax.ppermute(sums[block], ('gy', 'gz'), pairs))]
    ppermute x3, waiting for transfers between devices: 7.25 us -> 6.24 us  [shards(): lax.ppermute(payload, 'ga', ring_pairs(n_a, k))]
  transfers between devices with their start and end apart: 22 -> 19, of which waited for: 7 -> 8; matrix products, arithmetic and copies ran while one was open for 0% -> 0% of each run, Pallas kernels for 8% -> 9%
where the time goes in v3:
time: 62.6 us; the launch traced here: 62.5 us
  starting transfers between devices  27.3 us (44%)
  waiting for transfers between devices  22.1 us (35%)
  Pallas kernels  12.2 us (19%)
  between operations  0.75 us (1%)
    ppermute x6, starting transfers between devices, exchange(): received.append(lax.ppermute(snaps[k], 'ga', ring_pairs(n_a, k)))  9.54 us
    ppermute x6, starting transfers between devices, halo(): received.append(lax.ppermute(face, axis, swap_pairs(count, turn)))  9.29 us
    ppermute x6, waiting for transfers between devices, exchange(): received.append(lax.ppermute(snaps[k], 'ga', ring_pairs(n_a, k)))  6.99 us
    ppermute x3, waiting for transfers between devices, shards(): lax.ppermute(payload, 'ga', ring_pairs(n_a, k))  6.24 us
    ppermute x3, waiting for transfers between devices, shards(): received.append(lax.ppermute(sums[block], ('gy', 'gz'), pairs))  5.14 us
    ppermute x3, starting transfers between devices, shards(): lax.ppermute(payload, 'ga', ring_pairs(n_a, k))  4.63 us
    pallas_call x2, Pallas kernels, stencil(): pl.pallas_call(functools.partial(stencil_kernel, z_cells, counts, index,...  4.27 us
    ppermute x3, starting transfers between devices, shards(): received.append(lax.ppermute(sums[block], ('gy', 'gz'), pairs))  3.81 us
  transfers between devices with their start and end apart: 19, of which 8 were waited for; matrix products, arithmetic and copies ran while one was open for 0% of the time, Pallas kernels for 9%

profile of v3, /device:TPU:0, one launch (start us, length us, event | category | flops | bytes accessed | tf_op | source)
XLA Modules:
  0.0 62.5 jit_solution(17602809202957886407)
XLA Ops:
  0.7 2.7 %shard_map.94 = (f32[16,256,128]{2,1,0:T(8,128)S(1)}, f32[16,4,128]{2,1,0:T(4,128)S(1)}, f32[16,4,128]{2,1,0:T(4,128)S(1)}, f32[2,2048]{1,0:T(2,128)S(1)}, f32[2...) custom-call(f32[16,256,128]{2,1,0:T(8,128)} %bitcast.12), custom_call_target="tpu_custom_call" | custom-call | tf_op jit(solution)/shard_map/pallas_call | solution.py:425
  3.4 3.1 %collective-permute-start.2 = (bf16[16,32,128]{2,1,0:T(8,128)(2,1)S(1)}, bf16[16,32,128]{2,1,0:T(8,128)(2,1)S(1)}, u32[]{:S(2)}, u32[]{:S(2)}) collective-permute-start(bf16[16,32,128]{2,1,0:T(8,128)(2,1)S(1)} %get-tuple-element.39), channel_id=1, source_target_pairs={{0,4},{4,0},{1,5},{5,1},{2,6},{6,2},{3,7},{7,3},{8,12},{12,8},{9,1... | collective-permute-start | bytes 393224 | tf_op jit(solution)/shard_map/ppermute | solution.py:442
  6.5 1.6 %collective-permute-start = (f32[2,2048]{1,0:T(2,128)S(1)}, f32[2,2048]{1,0:T(2,128)S(1)}, u32[]{:S(2)}, u32[]{:S(2)}) collective-permute-start(f32[2,2048]{1,0:T(2,128)S(1)} %get-tuple-element.37), channel_id=1, source_target_pairs={{0,1},{1,0},{2,3},{3,2},{4,5},{5,4},{6,7},{7,6},{8,9},{9,8},{10,11... | collective-permute-start | bytes 49160 | tf_op jit(solution)/shard_map/ppermute | solution.py:442
  8.0 2.5 %collective-permute-start.1 = (f32[2,2048]{1,0:T(2,128)S(1)}, f32[2,2048]{1,0:T(2,128)S(1)}, u32[]{:S(2)}, u32[]{:S(2)}) collective-permute-start(f32[2,2048]{1,0:T(2,128)S(1)} %get-tuple-element.38), channel_id=1, source_target_pairs={{0,3},{1,2},{2,1},{3,0},{4,7},{5,6},{6,5},{7,4},{8,11},{9,10},{10,... | collective-permute-start | bytes 49160 | tf_op jit(solution)/shard_map/ppermute | solution.py:442
  10.5 1.0 %shard_map.95 = (bf16[256,256]{1,0:T(8,128)(2,1)S(1)}, f32[3,256,128]{2,1,0:T(8,128)S(1)}) custom-call(f32[16,16]{1,0:T(8,128)S(1)} %copy-done.3, f32[3,256,128]{2,1,0:T(8,128)} %bitcast.14, f32[16,4,128]{2,1,0:T(4,128)S(1)} %get-tuple-element.33.after), custom_call_target="tpu_custom_call" | custom-call | tf_op jit(solution)/shard_map/pallas_call | solution.py:445
  11.5 2.0 %collective-permute-done.1.rest_1_ = f32[2,2048]{1,0:T(2,128)S(1)} collective-permute-done((f32[2,2048]{1,0:T(2,128)S(1)}, f32[2,2048]{1,0:T(2,128)S(1)}, u32[]{:S(2)}, u32[]{:S(2)}) %collective-permute-start.1) | collective-permute-done | bytes 16416 | tf_op jit(solution)/shard_map/ppermute | solution.py:442
  13.6 2.1 %stencil.2 = (f32[16,128,128]{2,1,0:T(8,128)S(1)}, bf16[4,128,128]{2,1,0:T(8,128)(2,1)S(1)}, bf16[4,128,128]{2,1,0:T(8,128)(2,1)S(1)}, bf16[4,128,128]{2,1,0:T(8,128)(2,1)S(1)}, bf16[4,128,128]{2,1,0:T(8,128)(2,1)S(1)}) custom-call(f32[16]{0:T(128)S(1)} %copy-done.4, f32[3,256,128]{2,1,0:T(8,128)S(1)} %get-tuple-element.34.vel_ref, ...), custom_call_target="tpu_custom_call" | custom-call | tf_op jit(solution)/shard_map/stencil/pallas_call | solution.py:456
  17.1 1.6 %collective-permute-start.4 = (f32[16,4,128]{2,1,0:T(4,128)S(1)}, f32[16,4,128]{2,1,0:T(4,128)S(1)}, u32[]{:S(2)}, u32[]{:S(2)}) collective-permute-start(f32[16,4,128]{2,1,0:T(4,128)S(1)} %get-tuple-element.33.after), channel_id=1, source_target_pairs={{0,8},{8,0},{16,24},{24,16},{1,9},{9,1},{17,25},{25,17},{2,10},{10... | collective-permute-start | bytes 98312 | tf_op jit(solution)/shard_map/ppermute | solution.py:442
  18.7 2.3 %collective-permute-start.9 = (bf16[4,128,128]{2,1,0:T(8,128)(2,1)S(1)}, bf16[4,128,128]{2,1,0:T(8,128)(2,1)S(1)}, u32[]{:S(2)}, u32[]{:S(2)}) collective-permute-start(bf16[4,128,128]{2,1,0:T(8,128)(2,1)S(1)} %get-tuple-element.42), channel_id=1, source_target_pairs={{0,1},{1,2},{2,3},{3,0},{4,5},{5,6},{6,7},{7,4},{8,9},{9,10},{10,1... | collective-permute-start | bytes 393224 | tf_op jit(solution)/shard_map/ppermute | solution.py:474
  21.0 1.6 %collective-permute-start.11 = (bf16[4,128,128]{2,1,0:T(8,128)(2,1)S(1)}, bf16[4,128,128]{2,1,0:T(8,128)(2,1)S(1)}, u32[]{:S(2)}, u32[]{:S(2)}) collective-permute-start(bf16[4,128,128]{2,1,0:T(8,128)(2,1)S(1)} %get-tuple-element.52), channel_id=1, source_target_pairs={{0,3},{1,0},{2,1},{3,2},{4,7},{5,4},{6,5},{7,6},{8,11},{9,8},{10,9... | collective-permute-start | bytes 393224 | tf_op jit(solution)/shard_map/ppermute | solution.py:474
  22.5 2.2 %stencil.3 = (f32[16,128,128]{2,1,0:T(8,128)S(1)}, bf16[4,128,128]{2,1,0:T(8,128)(2,1)S(1)}, bf16[4,128,128]{2,1,0:T(8,128)(2,1)S(1)}, bf16[4,128,128]{2,1,0:T(8,128)(2,1)S(1)}, bf16[4,128,128]{2,1,0:T(8,128)(2,1)S(1)}) custom-call(f32[16]{0:T(128)S(1)} %copy-done.4, f32[3,256,128]{2,1,0:T(8,128)S(1)} %get-tuple-element.34.vel_ref, ...), custom_call_target="tpu_custom_call" | custom-call | tf_op jit(solution)/shard_map/stencil/pallas_call | solution.py:456
  25.3 1.9 %collective-permute-start.7 = (bf16[4,128,128]{2,1,0:T(8,128)(2,1)S(1)}, bf16[4,128,128]{2,1,0:T(8,128)(2,1)S(1)}, u32[]{:S(2)}, u32[]{:S(2)}) collective-permute-start(bf16[4,128,128]{2,1,0:T(8,128)(2,1)S(1)} %get-tuple-element.48), channel_id=1, source_target_pairs={{0,2},{1,3},{2,0},{3,1},{4,6},{5,7},{6,4},{7,5},{8,10},{9,11},{10,... | collective-permute-start | bytes 393224 | tf_op jit(solution)/shard_map/ppermute | solution.py:474
  27.2 2.5 %collective-permute-start.8 = (bf16[4,128,128]{2,1,0:T(8,128)(2,1)S(1)}, bf16[4,128,128]{2,1,0:T(8,128)(2,1)S(1)}, u32[]{:S(2)}, u32[]{:S(2)}) collective-permute-start(bf16[4,128,128]{2,1,0:T(8,128)(2,1)S(1)} %get-tuple-element.49), channel_id=1, source_target_pairs={{0,3},{1,0},{2,1},{3,2},{4,7},{5,4},{6,5},{7,6},{8,11},{9,8},{10,9... | collective-permute-start | bytes 393224 | tf_op jit(solution)/shard_map/ppermute | solution.py:474
  30.5 2.5 %collective-permute-done.6.refs_1_ = bf16[4,128,128]{2,1,0:T(8,128)(2,1)S(1)} collective-permute-done((bf16[4,128,128]{2,1,0:T(8,128)(2,1)S(1)}, bf16[4,128,128]{2,1,0:T(8,128)(2,1)S(1)}, u32[]{:S(2)}, u32[]{:S(2)}) %collective-permute-start.6) | collective-permute-done | bytes 131104 | tf_op jit(solution)/shard_map/ppermute | solution.py:474
  33.0 4.5 %collective-permute-done.7.refs_2_ = bf16[4,128,128]{2,1,0:T(8,128)(2,1)S(1)} collective-permute-done((bf16[4,128,128]{2,1,0:T(8,128)(2,1)S(1)}, bf16[4,128,128]{2,1,0:T(8,128)(2,1)S(1)}, u32[]{:S(2)}, u32[]{:S(2)}) %collective-permute-start.7) | collective-permute-done | bytes 131104 | tf_op jit(solution)/shard_map/ppermute | solution.py:474
  38.3 1.7 %collective-permute-done.12.other_ref = bf16[4,64,768]{2,1,0:T(8,128)(2,1)S(1)} collective-permute-done((bf16[4,64,768]{2,1,0:T(8,128)(2,1)S(1)}, bf16[4,64,768]{2,1,0:T(8,128)(2,1)S(1)}, u32[]{:S(2)}, u32[]{:S(2)}) %collective-permute-start.12) | collective-permute-done | bytes 393248 | tf_op jit(solution)/shard_map/ppermute | solution.py:521
  40.1 2.3 %collective-permute-start.14 = (bf16[64,1024]{1,0:T(8,128)(2,1)S(1)}, bf16[64,1024]{1,0:T(8,128)(2,1)S(1)}, u32[]{:S(2)}, u32[]{:S(2)}) collective-permute-start(bf16[64,1024]{1,0:T(8,128)(2,1)S(1)} %get-tuple-element.59), channel_id=1, source_target_pairs={{0,16},{4,20},{8,24},{12,28},{16,0},{20,4},{24,8},{28,12},{1,17},{... | collective-permute-start | bytes 393224 | tf_op jit(solution)/shard_map/ppermute | solution.py:536
  42.3 1.5 %collective-permute-start.13 = (bf16[64,512]{1,0:T(8,128)(2,1)S(1)}, bf16[64,512]{1,0:T(8,128)(2,1)S(1)}, u32[]{:S(2)}, u32[]{:S(2)}) collective-permute-start(bf16[64,512]{1,0:T(8,128)(2,1)S(1)} %get-tuple-element.58), channel_id=1, source_target_pairs={{0,4},{4,0},{8,12},{12,8},{16,20},{20,16},{24,28},{28,24},{1,5},{5... | collective-permute-start | bytes 196616 | tf_op jit(solution)/shard_map/ppermute | solution.py:536
  43.9 2.7 %collective-permute-done.13.refs_1_ = bf16[64,512]{1,0:T(8,128)(2,1)S(1)} collective-permute-done((bf16[64,512]{1,0:T(8,128)(2,1)S(1)}, bf16[64,512]{1,0:T(8,128)(2,1)S(1)}, u32[]{:S(2)}, u32[]{:S(2)}) %collective-permute-start.13) | collective-permute-done | bytes 65568 | tf_op jit(solution)/shard_map/ppermute | solution.py:536
  46.6 2.4 %collective-permute-done.15.refs_3_ = bf16[64,512]{1,0:T(8,128)(2,1)S(1)} collective-permute-done((bf16[64,512]{1,0:T(8,128)(2,1)S(1)}, bf16[64,512]{1,0:T(8,128)(2,1)S(1)}, u32[]{:S(2)}, u32[]{:S(2)}) %collective-permute-start.15) | collective-permute-done | bytes 65568 | tf_op jit(solution)/shard_map/ppermute | solution.py:536
  49.6 4.0 %collective-permute-start.18 = (bf16[64,768]{1,0:T(8,128)(2,1)S(1)}, bf16[64,768]{1,0:T(8,128)(2,1)S(1)}, u32[]{:S(2)}, u32[]{:S(2)}) collective-permute-start(bf16[64,768]{1,0:T(8,128)(2,1)S(1)} %shard_map.99.refs_0_), channel_id=1, source_target_pairs={{0,3},{1,0},{2,1},{3,2},{4,7},{5,4},{6,5},{7,6},{8,11},{9,8},{10,9... | collective-permute-start | bytes 294920 | tf_op jit(solution)/shard_map/ppermute | solution.py:566
  54.2 1.3 %flush.1 = f32[16,256,128]{2,1,0:T(8,128)} custom-call(f32[16,128,128]{2,1,0:T(8,128)S(1)} %get-tuple-element.40.refs_0_, f32[16,128,128]{2,1,0:T(8,128)S(1)} %get-tuple-element.45.refs_1_), custom_call_target="tpu_custom_call" | custom-call | tf_op jit(solution)/shard_map/flush/pallas_call | solution.py:489
  55.5 1.2 %collective-permute-done.18.refs_3_ = bf16[64,768]{1,0:T(8,128)(2,1)S(1)} collective-permute-done((bf16[64,768]{1,0:T(8,128)(2,1)S(1)}, bf16[64,768]{1,0:T(8,128)(2,1)S(1)}, u32[]{:S(2)}, u32[]{:S(2)}) %collective-permute-start.18) | collective-permute-done | bytes 98336 | tf_op jit(solution)/shard_map/ppermute | solution.py:566
  56.7 5.0 %collective-permute-done.17.refs_2_ = bf16[64,768]{1,0:T(8,128)(2,1)S(1)} collective-permute-done((bf16[64,768]{1,0:T(8,128)(2,1)S(1)}, bf16[64,768]{1,0:T(8,128)(2,1)S(1)}, u32[]{:S(2)}, u32[]{:S(2)}) %collective-permute-start.17) | collective-permute-done | bytes 98336 | tf_op jit(solution)/shard_map/ppermute | solution.py:566
  (34 shorter events, 5.6 us)
Async XLA Ops:
  0.6 9.9 %copy-start.3 = (f32[16,16]{1,0:T(8,128)S(1)}, f32[16,16]{1,0:T(8,128)}, u32[]{:S(2)}) copy-start(f32[16,16]{1,0:T(8,128)} %r_ref.1) | copy-start | bytes 3076
  0.6 12.9 %copy-start.4 = (f32[16]{0:T(128)S(1)}, f32[16]{0:T(128)}, u32[]{:S(2)}) copy-start(f32[16]{0:T(128)} %diffusion.3) | copy-start | bytes 196
  0.7 12.9 %copy-start = (f32[16,64,4,128]{3,2,1,0:T(4,128)S(1)}, f32[16,64,4,128]{3,2,1,0:T(4,128)}, u32[]{:S(2)}) copy-start(f32[16,64,4,128]{3,2,1,0:T(4,128)} %param.8) | copy-start | bytes 6291460
  3.4 10.2 %collective-permute-start.2 = (bf16[16,32,128]{2,1,0:T(8,128)(2,1)S(1)}, bf16[16,32,128]{2,1,0:T(8,128)(2,1)S(1)}, u32[]{:S(2)}, u32[]{:S(2)}) collective-permute-start(bf16[16,32,128]{2,1,0:T(8,128)(2,1)S(1)} %get-tuple-element.39), channel_id=1, source_target_pairs={{0,4},{4,0},{1,5},{5,1},{2,6},{6,2},{3,7},{7,3},{8,12},{12,8},{9,1... | collective-permute-start | bytes 393224 | tf_op jit(solution)/shard_map/ppermute | solution.py:442
  6.5 5.1 %collective-permute-start = (f32[2,2048]{1,0:T(2,128)S(1)}, f32[2,2048]{1,0:T(2,128)S(1)}, u32[]{:S(2)}, u32[]{:S(2)}) collective-permute-start(f32[2,2048]{1,0:T(2,128)S(1)} %get-tuple-element.37), channel_id=1, source_target_pairs={{0,1},{1,0},{2,3},{3,2},{4,5},{5,4},{6,7},{7,6},{8,9},{9,8},{10,11... | collective-permute-start | bytes 49160 | tf_op jit(solution)/shard_map/ppermute | solution.py:442
  8.0 5.5 %collective-permute-start.1 = (f32[2,2048]{1,0:T(2,128)S(1)}, f32[2,2048]{1,0:T(2,128)S(1)}, u32[]{:S(2)}, u32[]{:S(2)}) collective-permute-start(f32[2,2048]{1,0:T(2,128)S(1)} %get-tuple-element.38), channel_id=1, source_target_pairs={{0,3},{1,2},{2,1},{3,0},{4,7},{5,6},{6,5},{7,4},{8,11},{9,10},{10,... | collective-permute-start | bytes 49160 | tf_op jit(solution)/shard_map/ppermute | solution.py:442
  15.7 6.8 %collective-permute-start.3 = (bf16[16,32,128]{2,1,0:T(8,128)(2,1)S(1)}, bf16[16,32,128]{2,1,0:T(8,128)(2,1)S(1)}, u32[]{:S(2)}, u32[]{:S(2)}) collective-permute-start(bf16[16,32,128]{2,1,0:T(8,128)(2,1)S(1)} %get-tuple-element.43), channel_id=1, source_target_pairs={{0,4},{4,0},{1,5},{5,1},{2,6},{6,2},{3,7},{7,3},{8,12},{12,8},{9,1... | collective-permute-start | bytes 393224 | tf_op jit(solution)/shard_map/ppermute | solution.py:442
  16.3 10.9 %collective-permute-start.10 = (bf16[4,128,128]{2,1,0:T(8,128)(2,1)S(1)}, bf16[4,128,128]{2,1,0:T(8,128)(2,1)S(1)}, u32[]{:S(2)}, u32[]{:S(2)}) collective-permute-start(bf16[4,128,128]{2,1,0:T(8,128)(2,1)S(1)} %get-tuple-element.51), channel_id=1, source_target_pairs={{0,2},{1,3},{2,0},{3,1},{4,6},{5,7},{6,4},{7,5},{8,10},{9,11},{10,... | collective-permute-start | bytes 393224 | tf_op jit(solution)/shard_map/ppermute | solution.py:474
  17.1 3.9 %collective-permute-start.5 = (f32[16,4,128]{2,1,0:T(4,128)S(1)}, f32[16,4,128]{2,1,0:T(4,128)S(1)}, u32[]{:S(2)}, u32[]{:S(2)}) collective-permute-start(f32[16,4,128]{2,1,0:T(4,128)S(1)} %get-tuple-element.44), channel_id=1, source_target_pairs={{0,24},{8,16},{16,8},{24,0},{1,25},{9,17},{17,9},{25,1},{2,26},{10... | collective-permute-start | bytes 98312 | tf_op jit(solution)/shard_map/ppermute | solution.py:442
  17.1 5.4 %collective-permute-start.4 = (f32[16,4,128]{2,1,0:T(4,128)S(1)}, f32[16,4,128]{2,1,0:T(4,128)S(1)}, u32[]{:S(2)}, u32[]{:S(2)}) collective-permute-start(f32[16,4,128]{2,1,0:T(4,128)S(1)} %get-tuple-element.33.after), channel_id=1, source_target_pairs={{0,8},{8,0},{16,24},{24,16},{1,9},{9,1},{17,25},{25,17},{2,10},{10... | collective-permute-start | bytes 98312 | tf_op jit(solution)/shard_map/ppermute | solution.py:442
  18.7 10.9 %collective-permute-start.9 = (bf16[4,128,128]{2,1,0:T(8,128)(2,1)S(1)}, bf16[4,128,128]{2,1,0:T(8,128)(2,1)S(1)}, u32[]{:S(2)}, u32[]{:S(2)}) collective-permute-start(bf16[4,128,128]{2,1,0:T(8,128)(2,1)S(1)} %get-tuple-element.42), channel_id=1, source_target_pairs={{0,1},{1,2},{2,3},{3,0},{4,5},{5,6},{6,7},{7,4},{8,9},{9,10},{10,1... | collective-permute-start | bytes 393224 | tf_op jit(solution)/shard_map/ppermute | solution.py:474
  21.0 8.7 %copy-start.1 = (bf16[512,64]{0,1:T(8,128)(2,1)S(1)}, bf16[512,64]{0,1:T(8,128)(2,1)}, u32[]{:S(2)}) copy-start(bf16[512,64]{0,1:T(8,128)(2,1)} %param.12) | copy-start | bytes 196612
  21.0 8.7 %collective-permute-start.11 = (bf16[4,128,128]{2,1,0:T(8,128)(2,1)S(1)}, bf16[4,128,128]{2,1,0:T(8,128)(2,1)S(1)}, u32[]{:S(2)}, u32[]{:S(2)}) collective-permute-start(bf16[4,128,128]{2,1,0:T(8,128)(2,1)S(1)} %get-tuple-element.52), channel_id=1, source_target_pairs={{0,3},{1,0},{2,1},{3,2},{4,7},{5,4},{6,5},{7,6},{8,11},{9,8},{10,9... | collective-permute-start | bytes 393224 | tf_op jit(solution)/shard_map/ppermute | solution.py:474
  24.7 24.3 %copy-start.2 = (f32[256,64]{0,1:T(8,128)S(1)}, f32[256,64]{0,1:T(8,128)}, u32[]{:S(2)}) copy-start(f32[256,64]{0,1:T(8,128)} %param.13) | copy-start | bytes 196612
  24.7 8.3 %collective-permute-start.6 = (bf16[4,128,128]{2,1,0:T(8,128)(2,1)S(1)}, bf16[4,128,128]{2,1,0:T(8,128)(2,1)S(1)}, u32[]{:S(2)}, u32[]{:S(2)}) collective-permute-start(bf16[4,128,128]{2,1,0:T(8,128)(2,1)S(1)} %get-tuple-element.47), channel_id=1, source_target_pairs={{0,1},{1,2},{2,3},{3,0},{4,5},{5,6},{6,7},{7,4},{8,9},{9,10},{10,1... | collective-permute-start | bytes 393224 | tf_op jit(solution)/shard_map/ppermute | solution.py:474
  25.3 12.2 %collective-permute-start.7 = (bf16[4,128,128]{2,1,0:T(8,128)(2,1)S(1)}, bf16[4,128,128]{2,1,0:T(8,128)(2,1)S(1)}, u32[]{:S(2)}, u32[]{:S(2)}) collective-permute-start(bf16[4,128,128]{2,1,0:T(8,128)(2,1)S(1)} %get-tuple-element.48), channel_id=1, source_target_pairs={{0,2},{1,3},{2,0},{3,1},{4,6},{5,7},{6,4},{7,5},{8,10},{9,11},{10,... | collective-permute-start | bytes 393224 | tf_op jit(solution)/shard_map/ppermute | solution.py:474
  27.2 10.3 %collective-permute-start.8 = (bf16[4,128,128]{2,1,0:T(8,128)(2,1)S(1)}, bf16[4,128,128]{2,1,0:T(8,128)(2,1)S(1)}, u32[]{:S(2)}, u32[]{:S(2)}) collective-permute-start(bf16[4,128,128]{2,1,0:T(8,128)(2,1)S(1)} %get-tuple-element.49), channel_id=1, source_target_pairs={{0,3},{1,0},{2,1},{3,2},{4,7},{5,4},{6,5},{7,6},{8,11},{9,8},{10,9... | collective-permute-start | bytes 393224 | tf_op jit(solution)/shard_map/ppermute | solution.py:474
  38.2 1.8 %collective-permute-start.12 = (bf16[4,64,768]{2,1,0:T(8,128)(2,1)S(1)}, bf16[4,64,768]{2,1,0:T(8,128)(2,1)S(1)}, u32[]{:S(2)}, u32[]{:S(2)}) collective-permute-start(bf16[4,64,768]{2,1,0:T(8,128)(2,1)S(1)} %get-tuple-element.56), channel_id=1, source_target_pairs={{0,8},{8,0},{16,24},{24,16},{1,9},{9,1},{17,25},{25,17},{2,10},{10... | collective-permute-start | bytes 1179656 | tf_op jit(solution)/shard_map/ppermute | solution.py:521
  40.1 8.9 %collective-permute-start.14 = (bf16[64,1024]{1,0:T(8,128)(2,1)S(1)}, bf16[64,1024]{1,0:T(8,128)(2,1)S(1)}, u32[]{:S(2)}, u32[]{:S(2)}) collective-permute-start(bf16[64,1024]{1,0:T(8,128)(2,1)S(1)} %get-tuple-element.59), channel_id=1, source_target_pairs={{0,16},{4,20},{8,24},{12,28},{16,0},{20,4},{24,8},{28,12},{1,17},{... | collective-permute-start | bytes 393224 | tf_op jit(solution)/shard_map/ppermute | solution.py:536
  42.3 4.3 %collective-permute-start.13 = (bf16[64,512]{1,0:T(8,128)(2,1)S(1)}, bf16[64,512]{1,0:T(8,128)(2,1)S(1)}, u32[]{:S(2)}, u32[]{:S(2)}) collective-permute-start(bf16[64,512]{1,0:T(8,128)(2,1)S(1)} %get-tuple-element.58), channel_id=1, source_target_pairs={{0,4},{4,0},{8,12},{12,8},{16,20},{20,16},{24,28},{28,24},{1,5},{5... | collective-permute-start | bytes 196616 | tf_op jit(solution)/shard_map/ppermute | solution.py:536
  43.9 5.2 %collective-permute-start.15 = (bf16[64,512]{1,0:T(8,128)(2,1)S(1)}, bf16[64,512]{1,0:T(8,128)(2,1)S(1)}, u32[]{:S(2)}, u32[]{:S(2)}) collective-permute-start(bf16[64,512]{1,0:T(8,128)(2,1)S(1)} %get-tuple-element.60), channel_id=1, source_target_pairs={{0,20},{4,16},{8,28},{12,24},{16,4},{20,0},{24,12},{28,8},{1,21},{... | collective-permute-start | bytes 196616 | tf_op jit(solution)/shard_map/ppermute | solution.py:536
  49.6 7.2 %collective-permute-start.18 = (bf16[64,768]{1,0:T(8,128)(2,1)S(1)}, bf16[64,768]{1,0:T(8,128)(2,1)S(1)}, u32[]{:S(2)}, u32[]{:S(2)}) collective-permute-start(bf16[64,768]{1,0:T(8,128)(2,1)S(1)} %shard_map.99.refs_0_), channel_id=1, source_target_pairs={{0,3},{1,0},{2,1},{3,2},{4,7},{5,4},{6,5},{7,6},{8,11},{9,8},{10,9... | collective-permute-start | bytes 294920 | tf_op jit(solution)/shard_map/ppermute | solution.py:566
  53.6 8.2 %collective-permute-start.17 = (bf16[64,768]{1,0:T(8,128)(2,1)S(1)}, bf16[64,768]{1,0:T(8,128)(2,1)S(1)}, u32[]{:S(2)}, u32[]{:S(2)}) collective-permute-start(bf16[64,768]{1,0:T(8,128)(2,1)S(1)} %shard_map.99.refs_0_), channel_id=1, source_target_pairs={{0,2},{1,3},{2,0},{3,1},{4,6},{5,7},{6,4},{7,5},{8,10},{9,11},{10,... | collective-permute-start | bytes 294920 | tf_op jit(solution)/shard_map/ppermute | solution.py:566
  53.6 8.2 %collective-permute-start.16 = (bf16[64,768]{1,0:T(8,128)(2,1)S(1)}, bf16[64,768]{1,0:T(8,128)(2,1)S(1)}, u32[]{:S(2)}, u32[]{:S(2)}) collective-permute-start(bf16[64,768]{1,0:T(8,128)(2,1)S(1)} %shard_map.99.refs_0_), channel_id=1, source_target_pairs={{0,1},{1,2},{2,3},{3,0},{4,5},{5,6},{6,7},{7,4},{8,9},{9,10},{10,1... | collective-permute-start | bytes 294920 | tf_op jit(solution)/shard_map/ppermute | solution.py:566

commit v4 on v3

--- a/solution.py
+++ b/solution.py
@@ -24,6 +24,12 @@
     if turn == 0:
         return [(i, i ^ 1) for i in range(count)]
     return [(i, (i + (1 if i % 2 else -1)) % count) for i in range(count)]
+
+
+def partner(count, index, step):
+    if count & (count - 1) == 0:
+        return index ^ step
+    return (index + step) % count
 
 
 def origin(count, index, step):
@@ -331,35 +337,33 @@
                         ]
 
 
-def pair_kernel(n_z, own, width, keep_ref, other_ref, *outs):
-    for block, out in enumerate(outs):
+def pair_kernel(n_z, own, y_cells, width, keep_ref, other_ref, *outs):
+    blocks = keep_ref.shape[0]
+    side = keep_ref.shape[2] - width
+    for block in range(blocks):
+        if block % n_z == 0:
+            out = outs[blocks + block // n_z]
+            out[:, :side] = keep_ref[block, :y_cells, width:]
+            out[:, side:] = other_ref[block, :y_cells, width:]
+    for block in range(blocks):
         both = keep_ref[block, :own, :width].astype(f32) + other_ref[block, :own, :width].astype(f32)
-        if block % n_z:
-            out[...] = both.astype(bf16)
-        else:
-            side = keep_ref.shape[2] - width
-            if out.shape[0] != own:
-                out[...] = jnp.zeros_like(out)
-            out[:own, :width] = both.astype(bf16)
-            out[:, width : width + side] = keep_ref[block, :, width:]
-            out[:, width + side :] = other_ref[block, :, width:]
-
-
-def layer_kernel(n_y, n_z, paired, own, layers, y_scale, x_scale, yf_ref, *refs):
+        outs[block][...] = both.astype(bf16)
+
+
+def layer_kernel(n_y, paired, layers, y_scale, yf_ref, *refs):
     pieces, (out_ref, m_ref) = refs[:-2], refs[-2:]
-    rank, y_size = yf_ref.shape
+    _, y_size = yf_ref.shape
     y_cells = y_size // n_y
     cols = m_ref.shape[2]
     senders = 2 if paired else 1
-    width = pieces[0].shape[1] - senders * layers * cols
     my_y = lax.axis_index("gy")
-    for d in range(n_y // senders):
+    for d, piece in enumerate(pieces):
         for sender in range(senders):
             source = my_y ^ (2 * d + sender) if paired else origin(n_y, my_y, d)
             at = pl.multiple_of(source * y_cells, y_cells)
             for layer in range(layers):
-                start = width + (sender * layers + layer) * cols
-                m_ref[layer, pl.ds(at, y_cells), :] = pieces[d * n_z][:y_cells, start : start + cols]
+                start = (sender * layers + layer) * cols
+                m_ref[layer, pl.ds(at, y_cells), :] = piece[:, start : start + cols]
     for layer in range(layers):
         m = m_ref[layer]
         y_gram = lax.dot_general(m, m, (((1,), (1,)), ((), ())), preferred_element_type=f32) * y_scale
@@ -367,24 +371,31 @@
             yf_ref[...], y_gram, (((1,), (0,)), ((), ())), preferred_element_type=f32,
             precision=lax.Precision.HIGHEST,
         )
-        if own != rank:
-            out_ref[...] = jnp.zeros_like(out_ref)
-        out_ref[:rank, width + layer * y_size : width + (layer + 1) * y_size] = prod.astype(bf16)
-    total = pieces[0][:own, :width].astype(f32)
+        out_ref[:, layer * y_size : (layer + 1) * y_size] = prod.astype(bf16)
+
+
+def total_of(pieces):
+    total = pieces[0][...].astype(f32)
     for piece in pieces[1:]:
-        total = total + piece[:own, :width].astype(f32)
-    out_ref[:own, :width] = (total * x_scale).astype(bf16)
-
-
-def last_kernel(width, parts, *refs):
-    pieces, (gram_ref, prod_ref) = refs[:parts], refs[parts:]
-    total = pieces[0][...].astype(f32)
-    for i in range(1, parts):
-        total = total + pieces[i][...].astype(f32)
-    gram_ref[...] = total[: gram_ref.shape[0], :width]
-    layers, rank, y_size = prod_ref.shape
+        total = total + piece[...].astype(f32)
+    return total
+
+
+def sum_kernel(scale, after, *refs):
+    refs[-1][...] = (total_of(refs[:-1]) * scale).astype(bf16)
+
+
+def mark_kernel(value_ref, out_ref):
+    out_ref[...] = value_ref[:16, :128]
+
+
+def last_kernel(parts, *refs):
+    grams, prods, (gram_ref, prod_ref) = refs[:parts], refs[parts : 2 * parts], refs[2 * parts :]
+    total = total_of(prods)
+    layers, _, y_size = prod_ref.shape
     for layer in range(layers):
-        prod_ref[layer] = total[:rank, width + layer * y_size : width + (layer + 1) * y_size]
+        prod_ref[layer] = total[:, layer * y_size : (layer + 1) * y_size]
+    gram_ref[...] = total_of(grams)
 
 
 def call(kernel, out_shapes, in_specs, scratch=(), limit=16, flops=0, moved=0):
@@ -403,7 +414,7 @@
     variables, y_cells, z_cells, lanes = fields.shape
     rows = y_cells * z_cells
     n_y, n_z, n_a = (lax.axis_size(a) for a in ("gy", "gz", "ga"))
-    g_y, g_z, _ = (lax.axis_index(a) for a in ("gy", "gz", "ga"))
+    g_y, _, _ = (lax.axis_index(a) for a in ("gy", "gz", "ga"))
     f = fields.reshape(variables, rows, lanes)
     s = section_start.reshape(variables, rows, lanes)
     vel = velocity.reshape(3, rows, lanes)
@@ -520,13 +531,14 @@
         )(x_factor.T, *chunks[-1], gram, *projs)
         other = lax.ppermute(send, "gy", swap_pairs(n_y, 0))
         sums = call(
-            functools.partial(pair_kernel, n_z, own, x_size),
-            [
-                sds((own, x_size), bf16) if block % n_z else sds((piece_rows, x_size + 2 * cols), bf16)
-                for block in range(blocks)
-            ],
+            functools.partial(pair_kernel, n_z, own, y_cells, x_size),
+            [sds((own, x_size), bf16)] * blocks + [sds((y_cells, 2 * cols), bf16)] * (n_y // 2),
             [VMEM] * 2,
         )(keep, other)
+        sums, sides = sums[:blocks], sums[blocks:]
+        side_parts = [sides[0]]
+        for d_x in range(1, n_y // 2):
+            side_parts.append(lax.ppermute(sides[d_x], "gy", [(y, y ^ (2 * d_x)) for y in range(n_y)]))
         received = [sums[0]]
         for block in range(1, blocks):
             d_x, d_z = block // n_z, block % n_z
@@ -544,32 +556,35 @@
             gram.astype(bf16).reshape(owners, own, x_size), ("gy", "gz"), split_axis=0, concat_axis=0, tiled=True
         )
         full = full.transpose(0, 2, 1, 3).reshape(n_y, y_cells, cols)
-        received = []
-        for d_y in range(n_y):
-            for d_z in range(n_z):
-                source = origin(n_y, g_y, d_y) * n_z + origin(n_z, g_z, d_z)
-                block = lax.dynamic_index_in_dim(blocks, source, 0, keepdims=False)
-                if d_z == 0:
-                    block = jnp.pad(block, ((0, piece_rows - own), (0, 0)))
-                    side = lax.dynamic_index_in_dim(full, origin(n_y, g_y, d_y), 0, keepdims=False)
-                    side = jnp.pad(side, ((0, piece_rows - y_cells), (0, 0)))
-                    block = jnp.concatenate([block, side], axis=1)
-                received.append(block)
-    payload = call(
-        functools.partial(
-            layer_kernel, n_y, n_z, direct, own, layers, 1.0 / (variables * rank), 1.0 / (variables * rows * owners)
-        ),
-        [sds((max(own, y_rank), x_size + layers * y_size), bf16)],
-        [VMEM] * (1 + len(received)),
+        received = list(blocks)
+        side_parts = [
+            lax.dynamic_index_in_dim(full, origin(n_y, g_y, d_y), 0, keepdims=False) for d_y in range(n_y)
+        ]
+    prods = call(
+        functools.partial(layer_kernel, n_y, direct, layers, 1.0 / (variables * rank)),
+        [sds((y_rank, layers * y_size), bf16)],
+        [VMEM] * (1 + len(side_parts)),
         scratch=[pltpu.VMEM((layers, y_size, group * rank), bf16)],
-    )(y_factor.T, *received)[0]
-    payloads = [payload] + [lax.ppermute(payload, "ga", ring_pairs(n_a, k)) for k in range(1, n_a)]
+    )(y_factor.T, *side_parts)[0]
+    mark = call(mark_kernel, [sds((16, 128), bf16)], [VMEM], limit=2)(prods)[0]
+    gram = call(
+        functools.partial(sum_kernel, 1.0 / (variables * rows * owners)),
+        [sds((own, x_size), bf16)],
+        [ANY] + [VMEM] * len(received),
+    )(mark, *received)[0]
+
+    def spread(value):
+        values = [value]
+        for k in range(1, n_a):
+            values.append(lax.ppermute(value, "ga", [(i, partner(n_a, i, k)) for i in range(n_a)]))
+        return values
+
     x_gram, products = call(
-        functools.partial(last_kernel, x_size, n_a),
+        functools.partial(last_kernel, n_a),
         [sds((own, x_size), f32), sds((layers, y_rank, y_size), f32)],
-        [VMEM] * n_a,
+        [VMEM] * (2 * n_a),
         limit=8,
-    )(*payloads)
+    )(*spread(gram), *spread(prods))
     return (
         new_fields.reshape(fields.shape),
         x_gram,

time: 62.6 us -> 61.5 us (0.982)
  waiting for transfers between devices: 22.1 us -> 11.3 us
  starting transfers between devices: 27.3 us -> 36.9 us
    ppermute x3 -> x7, starting transfers between devices: 4.63 us -> 14.5 us  [the longest x6 12.2 us: spread(): lax.ppermute(value, 'ga', [(i, partner(n_a, i, k)) for i in range(n_a)])]
    ppermute x3 -> x7, waiting for transfers between devices: 6.24 us -> 0.55 us  [the longest x6 0.55 us: spread(): lax.ppermute(value, 'ga', [(i, partner(n_a, i, k)) for i in range(n_a)])]
    ppermute x3, waiting for transfers between devices: 5.14 us -> 0.01 us  [shards(): received.append(lax.ppermute(sums[block], ('gy', 'gz'), pairs))]
    pallas_call x3 -> x5, Pallas kernels: 1.3 us -> 1.36 us  [the longest x1 0.71 us: shards(): call(functools.partial(last_kernel, n_a), [sds((own, x_size), f32), sds((...]
  transfers between devices with their start and end apart: 19 -> 23, of which waited for: 8 -> 5; matrix products, arithmetic and copies ran while one was open for 0% -> 0% of each run, Pallas kernels for 9% -> 10%
where the time goes in v4:
time: 61.5 us; the launch traced here: 61.3 us
  starting transfers between devices  36.9 us (60%)
  Pallas kernels  12.3 us (20%)
  waiting for transfers between devices  11.3 us (18%)
  between operations  0.77 us (1%)
    ppermute x6, starting transfers between devices, spread(): lax.ppermute(value, 'ga', [(i, partner(n_a, i, k)) for i in range(n_a)])  12.2 us
    ppermute x6, starting transfers between devices, exchange(): received.append(lax.ppermute(snaps[k], 'ga', ring_pairs(n_a, k)))  9.54 us
    ppermute x6, starting transfers between devices, halo(): received.append(lax.ppermute(face, axis, swap_pairs(count, turn)))  9.29 us
    ppermute x6, waiting for transfers between devices, exchange(): received.append(lax.ppermute(snaps[k], 'ga', ring_pairs(n_a, k)))  6.99 us
    pallas_call x2, Pallas kernels, stencil(): pl.pallas_call(functools.partial(stencil_kernel, z_cells, counts, index,...  4.27 us
    ppermute x3, starting transfers between devices, shards(): received.append(lax.ppermute(sums[block], ('gy', 'gz'), pairs))  3.49 us
    pallas_call x1, Pallas kernels, shards(): call(functools.partial(pack_kernel, z_cells, counts, plan), [sds((variabl...  2.74 us
    ppermute x1, starting transfers between devices, shards(): lax.ppermute(sides[d_x], 'gy', [(y, y ^ 2 * d_x) for y in range(n_y)])  2.27 us
  transfers between devices with their start and end apart: 23, of which 5 were waited for; matrix products, arithmetic and copies ran while one was open for 0% of the time, Pallas kernels for 10%

profile of v4, /device:TPU:0, one launch (start us, length us, event | category | flops | bytes accessed | tf_op | source)
XLA Modules:
  0.0 61.3 jit_solution(14687608123496394519)
XLA Ops:
  0.7 2.7 %shard_map.94 = (f32[16,256,128]{2,1,0:T(8,128)S(1)}, f32[16,4,128]{2,1,0:T(4,128)S(1)}, f32[16,4,128]{2,1,0:T(4,128)S(1)}, f32[2,2048]{1,0:T(2,128)S(1)}, f32[2...) custom-call(f32[16,256,128]{2,1,0:T(8,128)} %bitcast.12), custom_call_target="tpu_custom_call" | custom-call | tf_op jit(solution)/shard_map/pallas_call | solution.py:436
  3.4 3.1 %collective-permute-start.2 = (bf16[16,32,128]{2,1,0:T(8,128)(2,1)S(1)}, bf16[16,32,128]{2,1,0:T(8,128)(2,1)S(1)}, u32[]{:S(2)}, u32[]{:S(2)}) collective-permute-start(bf16[16,32,128]{2,1,0:T(8,128)(2,1)S(1)} %get-tuple-element.41), channel_id=1, source_target_pairs={{0,4},{4,0},{1,5},{5,1},{2,6},{6,2},{3,7},{7,3},{8,12},{12,8},{9,1... | collective-permute-start | bytes 393224 | tf_op jit(solution)/shard_map/ppermute | solution.py:453
  6.5 1.6 %collective-permute-start = (f32[2,2048]{1,0:T(2,128)S(1)}, f32[2,2048]{1,0:T(2,128)S(1)}, u32[]{:S(2)}, u32[]{:S(2)}) collective-permute-start(f32[2,2048]{1,0:T(2,128)S(1)} %get-tuple-element.39), channel_id=1, source_target_pairs={{0,1},{1,0},{2,3},{3,2},{4,5},{5,4},{6,7},{7,6},{8,9},{9,8},{10,11... | collective-permute-start | bytes 49160 | tf_op jit(solution)/shard_map/ppermute | solution.py:453
  8.0 2.5 %collective-permute-start.1 = (f32[2,2048]{1,0:T(2,128)S(1)}, f32[2,2048]{1,0:T(2,128)S(1)}, u32[]{:S(2)}, u32[]{:S(2)}) collective-permute-start(f32[2,2048]{1,0:T(2,128)S(1)} %get-tuple-element.40), channel_id=1, source_target_pairs={{0,3},{1,2},{2,1},{3,0},{4,7},{5,6},{6,5},{7,4},{8,11},{9,10},{10,... | collective-permute-start | bytes 49160 | tf_op jit(solution)/shard_map/ppermute | solution.py:453
  11.5 2.0 %collective-permute-done.1.rest_1_ = f32[2,2048]{1,0:T(2,128)S(1)} collective-permute-done((f32[2,2048]{1,0:T(2,128)S(1)}, f32[2,2048]{1,0:T(2,128)S(1)}, u32[]{:S(2)}, u32[]{:S(2)}) %collective-permute-start.1) | collective-permute-done | bytes 16416 | tf_op jit(solution)/shard_map/ppermute | solution.py:453
  13.6 2.1 %stencil.2 = (f32[16,128,128]{2,1,0:T(8,128)S(1)}, bf16[4,128,128]{2,1,0:T(8,128)(2,1)S(1)}, bf16[4,128,128]{2,1,0:T(8,128)(2,1)S(1)}, bf16[4,128,128]{2,1,0:T(8,128)(2,1)S(1)}, bf16[4,128,128]{2,1,0:T(8,128)(2,1)S(1)}) custom-call(f32[16]{0:T(128)S(1)} %copy-done.4, f32[3,256,128]{2,1,0:T(8,128)S(1)} %get-tuple-element.36.vel_ref, ...), custom_call_target="tpu_custom_call" | custom-call | tf_op jit(solution)/shard_map/stencil/pallas_call | solution.py:467
  17.1 1.6 %collective-permute-start.4 = (f32[16,4,128]{2,1,0:T(4,128)S(1)}, f32[16,4,128]{2,1,0:T(4,128)S(1)}, u32[]{:S(2)}, u32[]{:S(2)}) collective-permute-start(f32[16,4,128]{2,1,0:T(4,128)S(1)} %get-tuple-element.35.after), channel_id=1, source_target_pairs={{0,8},{8,0},{16,24},{24,16},{1,9},{9,1},{17,25},{25,17},{2,10},{10... | collective-permute-start | bytes 98312 | tf_op jit(solution)/shard_map/ppermute | solution.py:453
  18.7 2.3 %collective-permute-start.9 = (bf16[4,128,128]{2,1,0:T(8,128)(2,1)S(1)}, bf16[4,128,128]{2,1,0:T(8,128)(2,1)S(1)}, u32[]{:S(2)}, u32[]{:S(2)}) collective-permute-start(bf16[4,128,128]{2,1,0:T(8,128)(2,1)S(1)} %get-tuple-element.44), channel_id=1, source_target_pairs={{0,1},{1,2},{2,3},{3,0},{4,5},{5,6},{6,7},{7,4},{8,9},{9,10},{10,1... | collective-permute-start | bytes 393224 | tf_op jit(solution)/shard_map/ppermute | solution.py:485
  21.0 1.6 %collective-permute-start.11 = (bf16[4,128,128]{2,1,0:T(8,128)(2,1)S(1)}, bf16[4,128,128]{2,1,0:T(8,128)(2,1)S(1)}, u32[]{:S(2)}, u32[]{:S(2)}) collective-permute-start(bf16[4,128,128]{2,1,0:T(8,128)(2,1)S(1)} %get-tuple-element.54), channel_id=1, source_target_pairs={{0,3},{1,0},{2,1},{3,2},{4,7},{5,4},{6,5},{7,6},{8,11},{9,8},{10,9... | collective-permute-start | bytes 393224 | tf_op jit(solution)/shard_map/ppermute | solution.py:485
  22.5 2.2 %stencil.3 = (f32[16,128,128]{2,1,0:T(8,128)S(1)}, bf16[4,128,128]{2,1,0:T(8,128)(2,1)S(1)}, bf16[4,128,128]{2,1,0:T(8,128)(2,1)S(1)}, bf16[4,128,128]{2,1,0:T(8,128)(2,1)S(1)}, bf16[4,128,128]{2,1,0:T(8,128)(2,1)S(1)}) custom-call(f32[16]{0:T(128)S(1)} %copy-done.4, f32[3,256,128]{2,1,0:T(8,128)S(1)} %get-tuple-element.36.vel_ref, ...), custom_call_target="tpu_custom_call" | custom-call | tf_op jit(solution)/shard_map/stencil/pallas_call | solution.py:467
  25.3 1.9 %collective-permute-start.7 = (bf16[4,128,128]{2,1,0:T(8,128)(2,1)S(1)}, bf16[4,128,128]{2,1,0:T(8,128)(2,1)S(1)}, u32[]{:S(2)}, u32[]{:S(2)}) collective-permute-start(bf16[4,128,128]{2,1,0:T(8,128)(2,1)S(1)} %get-tuple-element.50), channel_id=1, source_target_pairs={{0,2},{1,3},{2,0},{3,1},{4,6},{5,7},{6,4},{7,5},{8,10},{9,11},{10,... | collective-permute-start | bytes 393224 | tf_op jit(solution)/shard_map/ppermute | solution.py:485
  27.2 2.5 %collective-permute-start.8 = (bf16[4,128,128]{2,1,0:T(8,128)(2,1)S(1)}, bf16[4,128,128]{2,1,0:T(8,128)(2,1)S(1)}, u32[]{:S(2)}, u32[]{:S(2)}) collective-permute-start(bf16[4,128,128]{2,1,0:T(8,128)(2,1)S(1)} %get-tuple-element.51), channel_id=1, source_target_pairs={{0,3},{1,0},{2,1},{3,2},{4,7},{5,4},{6,5},{7,6},{8,11},{9,8},{10,9... | collective-permute-start | bytes 393224 | tf_op jit(solution)/shard_map/ppermute | solution.py:485
  30.5 2.5 %collective-permute-done.6.refs_1_ = bf16[4,128,128]{2,1,0:T(8,128)(2,1)S(1)} collective-permute-done((bf16[4,128,128]{2,1,0:T(8,128)(2,1)S(1)}, bf16[4,128,128]{2,1,0:T(8,128)(2,1)S(1)}, u32[]{:S(2)}, u32[]{:S(2)}) %collective-permute-start.6) | collective-permute-done | bytes 131104 | tf_op jit(solution)/shard_map/ppermute | solution.py:485
  33.0 4.5 %collective-permute-done.7.refs_2_ = bf16[4,128,128]{2,1,0:T(8,128)(2,1)S(1)} collective-permute-done((bf16[4,128,128]{2,1,0:T(8,128)(2,1)S(1)}, bf16[4,128,128]{2,1,0:T(8,128)(2,1)S(1)}, u32[]{:S(2)}, u32[]{:S(2)}) %collective-permute-start.7) | collective-permute-done | bytes 131104 | tf_op jit(solution)/shard_map/ppermute | solution.py:485
  38.3 1.7 %collective-permute-done.12.other_ref = bf16[4,64,768]{2,1,0:T(8,128)(2,1)S(1)} collective-permute-done((bf16[4,64,768]{2,1,0:T(8,128)(2,1)S(1)}, bf16[4,64,768]{2,1,0:T(8,128)(2,1)S(1)}, u32[]{:S(2)}, u32[]{:S(2)}) %collective-permute-start.12) | collective-permute-done | bytes 393248 | tf_op jit(solution)/shard_map/ppermute | solution.py:532
  40.1 2.3 %collective-permute-start.13 = (bf16[64,512]{1,0:T(8,128)(2,1)S(1)}, bf16[64,512]{1,0:T(8,128)(2,1)S(1)}, u32[]{:S(2)}, u32[]{:S(2)}) collective-permute-start(bf16[64,512]{1,0:T(8,128)(2,1)S(1)} %get-tuple-element.60), channel_id=1, source_target_pairs={{0,16},{8,24},{16,0},{24,8},{1,17},{9,25},{17,1},{25,9},{2,18},{10... | collective-permute-start | bytes 196616 | tf_op jit(solution)/shard_map/ppermute | solution.py:541
  42.4 1.5 %collective-permute-start.14 = (bf16[64,512]{1,0:T(8,128)(2,1)S(1)}, bf16[64,512]{1,0:T(8,128)(2,1)S(1)}, u32[]{:S(2)}, u32[]{:S(2)}) collective-permute-start(bf16[64,512]{1,0:T(8,128)(2,1)S(1)} %get-tuple-element.62), channel_id=1, source_target_pairs={{0,4},{4,0},{8,12},{12,8},{16,20},{20,16},{24,28},{28,24},{1,5},{5... | collective-permute-start | bytes 196616 | tf_op jit(solution)/shard_map/ppermute | solution.py:548
  43.9 1.9 %collective-permute-start.16 = (bf16[64,512]{1,0:T(8,128)(2,1)S(1)}, bf16[64,512]{1,0:T(8,128)(2,1)S(1)}, u32[]{:S(2)}, u32[]{:S(2)}) collective-permute-start(bf16[64,512]{1,0:T(8,128)(2,1)S(1)} %get-tuple-element.64), channel_id=1, source_target_pairs={{0,20},{4,16},{8,28},{12,24},{16,4},{20,0},{24,12},{28,8},{1,21},{... | collective-permute-start | bytes 196616 | tf_op jit(solution)/shard_map/ppermute | solution.py:548
  46.4 4.0 %collective-permute-start.22 = (bf16[64,256]{1,0:T(8,128)(2,1)S(1)}, bf16[64,256]{1,0:T(8,128)(2,1)S(1)}, u32[]{:S(2)}, u32[]{:S(2)}) collective-permute-start(bf16[64,256]{1,0:T(8,128)(2,1)S(1)} %shard_map.99.value_ref.refs_4_), channel_id=1, source_target_pairs={{0,3},{1,2},{2,1},{3,0},{4,7},{5,6},{6,5},{7,4},{8,11},{9,10},{10,... | collective-permute-start | bytes 98312 | tf_op jit(solution)/shard_map/ppermute | solution.py:579
  50.5 3.3 %collective-permute-start.19 = (bf16[64,512]{1,0:T(8,128)(2,1)S(1)}, bf16[64,512]{1,0:T(8,128)(2,1)S(1)}, u32[]{:S(2)}, u32[]{:S(2)}) collective-permute-start(bf16[64,512]{1,0:T(8,128)(2,1)S(1)} %shard_map.101.refs_0_), channel_id=1, source_target_pairs={{0,3},{1,2},{2,1},{3,0},{4,7},{5,6},{6,5},{7,4},{8,11},{9,10},{10,... | collective-permute-start | bytes 196616 | tf_op jit(solution)/shard_map/ppermute | solution.py:579
  53.7 1.2 %collective-permute-start.17 = (bf16[64,512]{1,0:T(8,128)(2,1)S(1)}, bf16[64,512]{1,0:T(8,128)(2,1)S(1)}, u32[]{:S(2)}, u32[]{:S(2)}) collective-permute-start(bf16[64,512]{1,0:T(8,128)(2,1)S(1)} %shard_map.101.refs_0_), channel_id=1, source_target_pairs={{0,1},{1,0},{2,3},{3,2},{4,5},{5,4},{6,7},{7,6},{8,9},{9,8},{10,11... | collective-permute-start | bytes 196616 | tf_op jit(solution)/shard_map/ppermute | solution.py:579
  54.9 1.8 %collective-permute-start.21 = (bf16[64,256]{1,0:T(8,128)(2,1)S(1)}, bf16[64,256]{1,0:T(8,128)(2,1)S(1)}, u32[]{:S(2)}, u32[]{:S(2)}) collective-permute-start(bf16[64,256]{1,0:T(8,128)(2,1)S(1)} %shard_map.99.value_ref.refs_4_), channel_id=1, source_target_pairs={{0,2},{1,3},{2,0},{3,1},{4,6},{5,7},{6,4},{7,5},{8,10},{9,11},{10,... | collective-permute-start | bytes 98312 | tf_op jit(solution)/shard_map/ppermute | solution.py:579
  56.7 2.0 %collective-permute-start.20 = (bf16[64,256]{1,0:T(8,128)(2,1)S(1)}, bf16[64,256]{1,0:T(8,128)(2,1)S(1)}, u32[]{:S(2)}, u32[]{:S(2)}) collective-permute-start(bf16[64,256]{1,0:T(8,128)(2,1)S(1)} %shard_map.99.value_ref.refs_4_), channel_id=1, source_target_pairs={{0,1},{1,0},{2,3},{3,2},{4,5},{5,4},{6,7},{7,6},{8,9},{9,8},{10,11... | collective-permute-start | bytes 98312 | tf_op jit(solution)/shard_map/ppermute | solution.py:579
  58.7 1.3 %flush.1 = f32[16,256,128]{2,1,0:T(8,128)} custom-call(f32[16,128,128]{2,1,0:T(8,128)S(1)} %get-tuple-element.42.refs_0_, f32[16,128,128]{2,1,0:T(8,128)S(1)} %get-tuple-element.47.refs_1_), custom_call_target="tpu_custom_call" | custom-call | tf_op jit(solution)/shard_map/flush/pallas_call | solution.py:500
  (44 shorter events, 6.6 us)
Async XLA Ops:
  3.4 10.2 %collective-permute-start.2 = (bf16[16,32,128]{2,1,0:T(8,128)(2,1)S(1)}, bf16[16,32,128]{2,1,0:T(8,128)(2,1)S(1)}, u32[]{:S(2)}, u32[]{:S(2)}) collective-permute-start(bf16[16,32,128]{2,1,0:T(8,128)(2,1)S(1)} %get-tuple-element.41), channel_id=1, source_target_pairs={{0,4},{4,0},{1,5},{5,1},{2,6},{6,2},{3,7},{7,3},{8,12},{12,8},{9,1... | collective-permute-start | bytes 393224 | tf_op jit(solution)/shard_map/ppermute | solution.py:453
  6.5 5.1 %collective-permute-start = (f32[2,2048]{1,0:T(2,128)S(1)}, f32[2,2048]{1,0:T(2,128)S(1)}, u32[]{:S(2)}, u32[]{:S(2)}) collective-permute-start(f32[2,2048]{1,0:T(2,128)S(1)} %get-tuple-element.39), channel_id=1, source_target_pairs={{0,1},{1,0},{2,3},{3,2},{4,5},{5,4},{6,7},{7,6},{8,9},{9,8},{10,11... | collective-permute-start | bytes 49160 | tf_op jit(solution)/shard_map/ppermute | solution.py:453
  8.0 5.5 %collective-permute-start.1 = (f32[2,2048]{1,0:T(2,128)S(1)}, f32[2,2048]{1,0:T(2,128)S(1)}, u32[]{:S(2)}, u32[]{:S(2)}) collective-permute-start(f32[2,2048]{1,0:T(2,128)S(1)} %get-tuple-element.40), channel_id=1, source_target_pairs={{0,3},{1,2},{2,1},{3,0},{4,7},{5,6},{6,5},{7,4},{8,11},{9,10},{10,... | collective-permute-start | bytes 49160 | tf_op jit(solution)/shard_map/ppermute | solution.py:453
  15.7 6.8 %collective-permute-start.3 = (bf16[16,32,128]{2,1,0:T(8,128)(2,1)S(1)}, bf16[16,32,128]{2,1,0:T(8,128)(2,1)S(1)}, u32[]{:S(2)}, u32[]{:S(2)}) collective-permute-start(bf16[16,32,128]{2,1,0:T(8,128)(2,1)S(1)} %get-tuple-element.45), channel_id=1, source_target_pairs={{0,4},{4,0},{1,5},{5,1},{2,6},{6,2},{3,7},{7,3},{8,12},{12,8},{9,1... | collective-permute-start | bytes 393224 | tf_op jit(solution)/shard_map/ppermute | solution.py:453
  16.3 10.9 %collective-permute-start.10 = (bf16[4,128,128]{2,1,0:T(8,128)(2,1)S(1)}, bf16[4,128,128]{2,1,0:T(8,128)(2,1)S(1)}, u32[]{:S(2)}, u32[]{:S(2)}) collective-permute-start(bf16[4,128,128]{2,1,0:T(8,128)(2,1)S(1)} %get-tuple-element.53), channel_id=1, source_target_pairs={{0,2},{1,3},{2,0},{3,1},{4,6},{5,7},{6,4},{7,5},{8,10},{9,11},{10,... | collective-permute-start | bytes 393224 | tf_op jit(solution)/shard_map/ppermute | solution.py:485
  17.1 3.9 %collective-permute-start.5 = (f32[16,4,128]{2,1,0:T(4,128)S(1)}, f32[16,4,128]{2,1,0:T(4,128)S(1)}, u32[]{:S(2)}, u32[]{:S(2)}) collective-permute-start(f32[16,4,128]{2,1,0:T(4,128)S(1)} %get-tuple-element.46), channel_id=1, source_target_pairs={{0,24},{8,16},{16,8},{24,0},{1,25},{9,17},{17,9},{25,1},{2,26},{10... | collective-permute-start | bytes 98312 | tf_op jit(solution)/shard_map/ppermute | solution.py:453
  17.1 5.4 %collective-permute-start.4 = (f32[16,4,128]{2,1,0:T(4,128)S(1)}, f32[16,4,128]{2,1,0:T(4,128)S(1)}, u32[]{:S(2)}, u32[]{:S(2)}) collective-permute-start(f32[16,4,128]{2,1,0:T(4,128)S(1)} %get-tuple-element.35.after), channel_id=1, source_target_pairs={{0,8},{8,0},{16,24},{24,16},{1,9},{9,1},{17,25},{25,17},{2,10},{10... | collective-permute-start | bytes 98312 | tf_op jit(solution)/shard_map/ppermute | solution.py:453
  18.7 10.9 %collective-permute-start.9 = (bf16[4,128,128]{2,1,0:T(8,128)(2,1)S(1)}, bf16[4,128,128]{2,1,0:T(8,128)(2,1)S(1)}, u32[]{:S(2)}, u32[]{:S(2)}) collective-permute-start(bf16[4,128,128]{2,1,0:T(8,128)(2,1)S(1)} %get-tuple-element.44), channel_id=1, source_target_pairs={{0,1},{1,2},{2,3},{3,0},{4,5},{5,6},{6,7},{7,4},{8,9},{9,10},{10,1... | collective-permute-start | bytes 393224 | tf_op jit(solution)/shard_map/ppermute | solution.py:485
  21.0 8.7 %collective-permute-start.11 = (bf16[4,128,128]{2,1,0:T(8,128)(2,1)S(1)}, bf16[4,128,128]{2,1,0:T(8,128)(2,1)S(1)}, u32[]{:S(2)}, u32[]{:S(2)}) collective-permute-start(bf16[4,128,128]{2,1,0:T(8,128)(2,1)S(1)} %get-tuple-element.54), channel_id=1, source_target_pairs={{0,3},{1,0},{2,1},{3,2},{4,7},{5,4},{6,5},{7,6},{8,11},{9,8},{10,9... | collective-permute-start | bytes 393224 | tf_op jit(solution)/shard_map/ppermute | solution.py:485
  24.7 21.2 %copy-start.2 = (f32[256,64]{0,1:T(8,128)S(1)}, f32[256,64]{0,1:T(8,128)}, u32[]{:S(2)}) copy-start(f32[256,64]{0,1:T(8,128)} %param.13) | copy-start | bytes 196612
  24.7 8.3 %collective-permute-start.6 = (bf16[4,128,128]{2,1,0:T(8,128)(2,1)S(1)}, bf16[4,128,128]{2,1,0:T(8,128)(2,1)S(1)}, u32[]{:S(2)}, u32[]{:S(2)}) collective-permute-start(bf16[4,128,128]{2,1,0:T(8,128)(2,1)S(1)} %get-tuple-element.49), channel_id=1, source_target_pairs={{0,1},{1,2},{2,3},{3,0},{4,5},{5,6},{6,7},{7,4},{8,9},{9,10},{10,1... | collective-permute-start | bytes 393224 | tf_op jit(solution)/shard_map/ppermute | solution.py:485
  25.3 12.2 %collective-permute-start.7 = (bf16[4,128,128]{2,1,0:T(8,128)(2,1)S(1)}, bf16[4,128,128]{2,1,0:T(8,128)(2,1)S(1)}, u32[]{:S(2)}, u32[]{:S(2)}) collective-permute-start(bf16[4,128,128]{2,1,0:T(8,128)(2,1)S(1)} %get-tuple-element.50), channel_id=1, source_target_pairs={{0,2},{1,3},{2,0},{3,1},{4,6},{5,7},{6,4},{7,5},{8,10},{9,11},{10,... | collective-permute-start | bytes 393224 | tf_op jit(solution)/shard_map/ppermute | solution.py:485
  27.2 10.3 %collective-permute-start.8 = (bf16[4,128,128]{2,1,0:T(8,128)(2,1)S(1)}, bf16[4,128,128]{2,1,0:T(8,128)(2,1)S(1)}, u32[]{:S(2)}, u32[]{:S(2)}) collective-permute-start(bf16[4,128,128]{2,1,0:T(8,128)(2,1)S(1)} %get-tuple-element.51), channel_id=1, source_target_pairs={{0,3},{1,0},{2,1},{3,2},{4,7},{5,4},{6,5},{7,6},{8,11},{9,8},{10,9... | collective-permute-start | bytes 393224 | tf_op jit(solution)/shard_map/ppermute | solution.py:485
  38.2 1.8 %collective-permute-start.12 = (bf16[4,64,768]{2,1,0:T(8,128)(2,1)S(1)}, bf16[4,64,768]{2,1,0:T(8,128)(2,1)S(1)}, u32[]{:S(2)}, u32[]{:S(2)}) collective-permute-start(bf16[4,64,768]{2,1,0:T(8,128)(2,1)S(1)} %get-tuple-element.58), channel_id=1, source_target_pairs={{0,8},{8,0},{16,24},{24,16},{1,9},{9,1},{17,25},{25,17},{2,10},{10... | collective-permute-start | bytes 1179656 | tf_op jit(solution)/shard_map/ppermute | solution.py:532
  40.1 5.8 %collective-permute-start.13 = (bf16[64,512]{1,0:T(8,128)(2,1)S(1)}, bf16[64,512]{1,0:T(8,128)(2,1)S(1)}, u32[]{:S(2)}, u32[]{:S(2)}) collective-permute-start(bf16[64,512]{1,0:T(8,128)(2,1)S(1)} %get-tuple-element.60), channel_id=1, source_target_pairs={{0,16},{8,24},{16,0},{24,8},{1,17},{9,25},{17,1},{25,9},{2,18},{10... | collective-permute-start | bytes 196616 | tf_op jit(solution)/shard_map/ppermute | solution.py:541
  42.4 8.0 %collective-permute-start.14 = (bf16[64,512]{1,0:T(8,128)(2,1)S(1)}, bf16[64,512]{1,0:T(8,128)(2,1)S(1)}, u32[]{:S(2)}, u32[]{:S(2)}) collective-permute-start(bf16[64,512]{1,0:T(8,128)(2,1)S(1)} %get-tuple-element.62), channel_id=1, source_target_pairs={{0,4},{4,0},{8,12},{12,8},{16,20},{20,16},{24,28},{28,24},{1,5},{5... | collective-permute-start | bytes 196616 | tf_op jit(solution)/shard_map/ppermute | solution.py:548
  43.9 6.5 %collective-permute-start.15 = (bf16[64,512]{1,0:T(8,128)(2,1)S(1)}, bf16[64,512]{1,0:T(8,128)(2,1)S(1)}, u32[]{:S(2)}, u32[]{:S(2)}) collective-permute-start(bf16[64,512]{1,0:T(8,128)(2,1)S(1)} %get-tuple-element.63), channel_id=1, source_target_pairs={{0,16},{4,20},{8,24},{12,28},{16,0},{20,4},{24,8},{28,12},{1,17},{... | collective-permute-start | bytes 196616 | tf_op jit(solution)/shard_map/ppermute | solution.py:548
  43.9 6.5 %collective-permute-start.16 = (bf16[64,512]{1,0:T(8,128)(2,1)S(1)}, bf16[64,512]{1,0:T(8,128)(2,1)S(1)}, u32[]{:S(2)}, u32[]{:S(2)}) collective-permute-start(bf16[64,512]{1,0:T(8,128)(2,1)S(1)} %get-tuple-element.64), channel_id=1, source_target_pairs={{0,20},{4,16},{8,28},{12,24},{16,4},{20,0},{24,12},{28,8},{1,21},{... | collective-permute-start | bytes 196616 | tf_op jit(solution)/shard_map/ppermute | solution.py:548
  46.4 10.3 %collective-permute-start.22 = (bf16[64,256]{1,0:T(8,128)(2,1)S(1)}, bf16[64,256]{1,0:T(8,128)(2,1)S(1)}, u32[]{:S(2)}, u32[]{:S(2)}) collective-permute-start(bf16[64,256]{1,0:T(8,128)(2,1)S(1)} %shard_map.99.value_ref.refs_4_), channel_id=1, source_target_pairs={{0,3},{1,2},{2,1},{3,0},{4,7},{5,6},{6,5},{7,4},{8,11},{9,10},{10,... | collective-permute-start | bytes 98312 | tf_op jit(solution)/shard_map/ppermute | solution.py:579
  50.5 10.1 %collective-permute-start.19 = (bf16[64,512]{1,0:T(8,128)(2,1)S(1)}, bf16[64,512]{1,0:T(8,128)(2,1)S(1)}, u32[]{:S(2)}, u32[]{:S(2)}) collective-permute-start(bf16[64,512]{1,0:T(8,128)(2,1)S(1)} %shard_map.101.refs_0_), channel_id=1, source_target_pairs={{0,3},{1,2},{2,1},{3,0},{4,7},{5,6},{6,5},{7,4},{8,11},{9,10},{10,... | collective-permute-start | bytes 196616 | tf_op jit(solution)/shard_map/ppermute | solution.py:579
  53.7 6.9 %collective-permute-start.18 = (bf16[64,512]{1,0:T(8,128)(2,1)S(1)}, bf16[64,512]{1,0:T(8,128)(2,1)S(1)}, u32[]{:S(2)}, u32[]{:S(2)}) collective-permute-start(bf16[64,512]{1,0:T(8,128)(2,1)S(1)} %shard_map.101.refs_0_), channel_id=1, source_target_pairs={{0,2},{1,3},{2,0},{3,1},{4,6},{5,7},{6,4},{7,5},{8,10},{9,11},{10,... | collective-permute-start | bytes 196616 | tf_op jit(solution)/shard_map/ppermute | solution.py:579
  53.7 6.9 %collective-permute-start.17 = (bf16[64,512]{1,0:T(8,128)(2,1)S(1)}, bf16[64,512]{1,0:T(8,128)(2,1)S(1)}, u32[]{:S(2)}, u32[]{:S(2)}) collective-permute-start(bf16[64,512]{1,0:T(8,128)(2,1)S(1)} %shard_map.101.refs_0_), channel_id=1, source_target_pairs={{0,1},{1,0},{2,3},{3,2},{4,5},{5,4},{6,7},{7,6},{8,9},{9,8},{10,11... | collective-permute-start | bytes 196616 | tf_op jit(solution)/shard_map/ppermute | solution.py:579
  54.9 5.1 %collective-permute-start.21 = (bf16[64,256]{1,0:T(8,128)(2,1)S(1)}, bf16[64,256]{1,0:T(8,128)(2,1)S(1)}, u32[]{:S(2)}, u32[]{:S(2)}) collective-permute-start(bf16[64,256]{1,0:T(8,128)(2,1)S(1)} %shard_map.99.value_ref.refs_4_), channel_id=1, source_target_pairs={{0,2},{1,3},{2,0},{3,1},{4,6},{5,7},{6,4},{7,5},{8,10},{9,11},{10,... | collective-permute-start | bytes 98312 | tf_op jit(solution)/shard_map/ppermute | solution.py:579
  56.7 3.9 %collective-permute-start.20 = (bf16[64,256]{1,0:T(8,128)(2,1)S(1)}, bf16[64,256]{1,0:T(8,128)(2,1)S(1)}, u32[]{:S(2)}, u32[]{:S(2)}) collective-permute-start(bf16[64,256]{1,0:T(8,128)(2,1)S(1)} %shard_map.99.value_ref.refs_4_), channel_id=1, source_target_pairs={{0,1},{1,0},{2,3},{3,2},{4,5},{5,4},{6,7},{7,6},{8,9},{9,8},{10,11... | collective-permute-start | bytes 98312 | tf_op jit(solution)/shard_map/ppermute | solution.py:579
  (4 other events, 44.5 us)

commit v5 on v4

--- a/solution.py
+++ b/solution.py
@@ -119,11 +119,11 @@
     return pick
 
 
-def mix_kernel(r_ref, vel_hbm, after, out_ref, vel_ref, sem):
+def mix_kernel(r_ref, vel_hbm, f_ref, out_ref, vel_ref, sem):
     load = pltpu.make_async_copy(vel_hbm, vel_ref, sem)
     load.start()
     count = r_ref.shape[0]
-    size = out_ref.shape[0]
+    size = out_ref.shape[1]
     spread = jnp.where(
         lax.broadcasted_iota(jnp.int32, (size, count), 0) // SUB
         == lax.broadcasted_iota(jnp.int32, (size, count), 1),
@@ -137,43 +137,55 @@
     )
     row = lax.broadcasted_iota(jnp.int32, (size, size), 0)
     col = lax.broadcasted_iota(jnp.int32, (size, size), 1)
-    out_ref[...] = jnp.where(row % SUB == col % SUB, both, 0.0).astype(bf16)
+    mix = jnp.where(row % SUB == col % SUB, both, 0.0).astype(bf16)
+    for t in range(out_ref.shape[0]):
+        blocks = []
+        for at in range(t * TILE, (t + 1) * TILE, SUB):
+            blocks.append(
+                jnp.concatenate([f_ref[w, at : at + SUB, :].astype(bf16) for w in range(count)], axis=0)
+            )
+        out_ref[t] = jnp.dot(mix, jnp.concatenate(blocks, axis=1), preferred_element_type=f32)
     load.wait()
 
 
 def stencil_kernel(
-    z_cells, counts, index, segments, has_y, diffusion, vel_ref, start_ref, f_ref, mix_ref, *rest
+    z_cells, counts, index, segments, chosen, has_y, diffusion, vel_ref, start_ref, f_ref, react, *rest
 ):
     n_y, n_z, parts = counts
     x_refs, rest = rest[: turns(parts)], rest[turns(parts) :]
     z_refs, rest = rest[: turns(n_z)], rest[turns(n_z) :]
     if has_y:
         y_refs, rest = rest[: turns(n_y)], rest[turns(n_y) :]
-    new_ref, rest = rest[0], rest[1:]
-    snaps, (ends, edge, zface, react) = rest[:parts], rest[parts:]
+    many = len(chosen)
+    news, snaps, (ends, edge, zface) = rest[:many], rest[many : 2 * many], rest[2 * many :]
     variables, rows, lanes = f_ref.shape
     pad = -(-z_cells // 8) * 8
     tile = TILE
+    group = variables // parts
     chunk = sum(count for _, count in segments)
     me = lax.axis_index("ga")
     is_buffer = me == parts - 1
-
     tile_rows = [first + k * tile for first, count in segments for k in range(count // tile)]
+    picked = []
+    for i, part in enumerate(chosen):
+        target = lax.rem(me + part, parts)
+        picked += [(i, j, target * group + j) for j in range(group)]
 
     put = corner_mask(lanes)
     side = lax.broadcasted_iota(jnp.int32, (8, chunk), 0)
     y_count = chunk // z_cells
     x_pair = low_high("ga", parts, x_refs)
     z_pair = low_high("gz", n_z, z_refs)
-    for v in range(variables):
-        first, second = x_pair(lambda ref: ref[index : index + 1, v * chunk : (v + 1) * chunk])
+    for slot, (_, _, v) in enumerate(picked):
+        at = pl.ds(pl.multiple_of(v * chunk, 128), chunk)
+        first, second = x_pair(lambda ref: ref[index : index + 1, at])
         first = jnp.broadcast_to(first, (8, chunk))
         second = jnp.broadcast_to(second, (8, chunk))
         both = jnp.where(side == 0, first, jnp.where(side == 1, second, 0.0)).astype(bf16)
-        edge[v] = lax.dot_general(both, put, (((0,), (0,)), ((), ())), preferred_element_type=f32)
+        edge[slot] = lax.dot_general(both, put, (((0,), (0,)), ((), ())), preferred_element_type=f32)
         first, second = z_pair(lambda ref: ref[v].astype(f32))
-        zface[v, pl.ds(0, y_count, stride=z_cells), :] = first
-        zface[v, pl.ds(z_cells - 1, y_count, stride=z_cells), :] = second
+        zface[slot, pl.ds(0, y_count, stride=z_cells), :] = first
+        zface[slot, pl.ds(z_cells - 1, y_count, stride=z_cells), :] = second
     if has_y:
         low, high = low_high("gy", n_y, y_refs)(lambda ref: ref[...])
         ends[0, :, pad - z_cells : pad, :] = low
@@ -182,18 +194,9 @@
         ends[1, :, tile + pad : tile + pad + z_cells, :] = high
 
     rate = new_share * time_step
-    group = variables // parts
     lane = lax.broadcasted_iota(jnp.int32, (SUB, lanes), 1)
     z_at = lax.rem(lax.broadcasted_iota(jnp.int32, (SUB, lanes), 0), z_cells)
     for t, row in enumerate(tile_rows):
-        slot = t % 2
-        blocks = []
-        for sub in range(tile // SUB):
-            at = row + sub * SUB
-            blocks.append(
-                jnp.concatenate([f_ref[w, at : at + SUB, :].astype(bf16) for w in range(variables)], axis=0)
-            )
-        react[slot] = jnp.dot(mix_ref[...], jnp.concatenate(blocks, axis=1), preferred_element_type=f32)
         for sub in range(tile // SUB):
             at, here = row + sub * SUB, t * tile + sub * SUB
 
@@ -207,51 +210,53 @@
             v_x = vel_ref[0, at : at + SUB, :] * (0.5 * rate)
             v_y = vel_ref[1, at : at + SUB, :] * (0.5 * rate)
             v_z = vel_ref[2, at : at + SUB, :] * (0.5 * rate)
-            for part in range(parts):
-                target = lax.rem(me + part, parts)
-                for j in range(group):
-                    v = target * group + j
-                    spread = diffusion[v] * rate
-                    center = rows_at(v, 0)
-                    y_minus = rows_at(v, -z_cells)
-                    y_plus = rows_at(v, z_cells)
-                    face = zface[v, here : here + SUB, :]
-                    z_minus = jnp.where(z_at == 0, face, rows_at(v, -1))
-                    z_plus = jnp.where(z_at == z_cells - 1, face, rows_at(v, 1))
-                    sides = edge[v, here : here + SUB, :]
-                    x_minus = jnp.where(lane == 0, sides, pltpu.roll(center, 1, 1))
-                    x_plus = jnp.where(lane == lanes - 1, sides, pltpu.roll(center, lanes - 1, 1))
-                    mixed = react[
-                        slot, pl.ds(pl.multiple_of(v * SUB, SUB), SUB), sub * lanes : (sub + 1) * lanes
-                    ]
-                    around = (y_plus + y_minus) + (z_plus + z_minus) + (x_plus + x_minus)
-                    carried = (
-                        v_x * (x_plus - x_minus) + v_y * (y_plus - y_minus) + v_z * (z_plus - z_minus)
+            for slot, (i, j, v) in enumerate(picked):
+                spread = diffusion[v] * rate
+                center = rows_at(v, 0)
+                y_minus = rows_at(v, -z_cells)
+                y_plus = rows_at(v, z_cells)
+                face = zface[slot, here : here + SUB, :]
+                z_minus = jnp.where(z_at == 0, face, rows_at(v, -1))
+                z_plus = jnp.where(z_at == z_cells - 1, face, rows_at(v, 1))
+                sides = edge[slot, here : here + SUB, :]
+                x_minus = jnp.where(lane == 0, sides, pltpu.roll(center, 1, 1))
+                x_plus = jnp.where(lane == lanes - 1, sides, pltpu.roll(center, lanes - 1, 1))
+                mixed = react[
+                    row // tile, pl.ds(pl.multiple_of(v * SUB, SUB), SUB), sub * lanes : (sub + 1) * lanes
+                ]
+                around = (y_plus + y_minus) + (z_plus + z_minus) + (x_plus + x_minus)
+                carried = v_x * (x_plus - x_minus) + v_y * (y_plus - y_minus) + v_z * (z_plus - z_minus)
+                value = (
+                    old_share * start_ref[v, at : at + SUB, :]
+                    + (new_share - 6.0 * spread) * center
+                    + (spread * around - carried)
+                    + mixed
+                )
+                value = jnp.where(is_buffer, center, value)
+                news[i][j, here : here + SUB, :] = value
+                snaps[i][j, here : here + SUB, :] = value.astype(bf16)
+
+
+def flush_kernel(plan, parts, *refs):
+    news, (new_hbm, sem) = refs[:-2], refs[-2:]
+    me = lax.axis_index("ga")
+    writes = []
+    for c, segments in enumerate(plan):
+        for part in range(parts):
+            ref = news[c * parts + part]
+            group = ref.shape[0]
+            to = pl.ds(lax.rem(me + part, parts) * group, group)
+            at = 0
+            for first, count in segments:
+                writes.append(
+                    pltpu.make_async_copy(
+                        ref.at[:, pl.ds(at, count), :],
+                        new_hbm.at[to, pl.ds(first, count), :],
+                        sem.at[len(writes)],
                     )
-                    value = (
-                        old_share * start_ref[v, at : at + SUB, :]
-                        + (new_share - 6.0 * spread) * center
-                        + (spread * around - carried)
-                        + mixed
-                    )
-                    value = jnp.where(is_buffer, center, value)
-                    new_ref[v, here : here + SUB, :] = value
-                    snaps[part][j, here : here + SUB, :] = value.astype(bf16)
-
-
-def flush_kernel(plan, *refs):
-    parts, (new_hbm, sem) = refs[: len(plan)], refs[len(plan) :]
-    writes = []
-    for part, segments in zip(parts, plan):
-        at = 0
-        for first, count in segments:
-            writes.append(
-                pltpu.make_async_copy(
-                    part.at[:, pl.ds(at, count), :], new_hbm.at[:, pl.ds(first, count), :], sem.at[len(writes)]
                 )
-            )
-            writes[-1].start()
-            at += count
+                writes[-1].start()
+                at += count
     for write in writes:
         write.wait()
 
@@ -453,31 +458,31 @@
             received.append(lax.ppermute(face, axis, swap_pairs(count, turn)))
         return received
 
-    mix, vel = call(
+    react, vel = call(
         mix_kernel,
-        [sds((variables * SUB, variables * SUB), bf16), sds(vel.shape, f32)],
-        [VMEM, ANY, ANY],
+        [sds((rows // tile, variables * SUB, tile // SUB * lanes), f32), sds(vel.shape, f32)],
+        [VMEM, ANY, VMEM],
         scratch=[pltpu.SemaphoreType.DMA],
-        limit=8,
-    )(reaction, in_hbm(vel), y_faces[0])
-
-    def stencil(index, x_halos, z_halos, y_halos):
-        segments = plan[index]
-        operands = [diffusivity, vel, s, f, mix, *x_halos, *z_halos, *y_halos]
-        return pl.pallas_call(
-            functools.partial(stencil_kernel, z_cells, counts, index, segments, bool(y_halos)),
-            out_shape=[sds((variables, chunk, lanes), f32)] + [sds((group, chunk, lanes), bf16)] * n_a,
+        limit=12,
+    )(reaction, in_hbm(vel), f)
+
+    def stencil(index, chosen, x_halos, z_halos, y_halos):
+        operands = [diffusivity, vel, s, f, react, *x_halos, *z_halos, *y_halos]
+        many = len(chosen)
+        results = pl.pallas_call(
+            functools.partial(stencil_kernel, z_cells, counts, index, plan[index], chosen, bool(y_halos)),
+            out_shape=[sds((group, chunk, lanes), f32)] * many + [sds((group, chunk, lanes), bf16)] * many,
             in_specs=[SMEM] + [VMEM] * (len(operands) - 1),
-            out_specs=[VMEM] * (n_a + 1),
+            out_specs=[VMEM] * (2 * many),
             scratch_shapes=[
                 pltpu.VMEM((2, variables, tile + 2 * pad, lanes), f32),
-                pltpu.VMEM((variables, chunk, lanes), f32),
-                pltpu.VMEM((variables, chunk, lanes), f32),
-                pltpu.VMEM((2, variables * SUB, tile // SUB * lanes), f32),
+                pltpu.VMEM((many * group, chunk, lanes), f32),
+                pltpu.VMEM((many * group, chunk, lanes), f32),
             ],
             name="stencil",
             compiler_params=pltpu.CompilerParams(vmem_limit_bytes=20 * MIB),
         )(*operands)
+        return list(results[:many]), list(results[many:])
 
     def exchange(snaps):
         received = [snaps[0]]
@@ -489,20 +494,22 @@
     z_halos = halo("gz", n_z, early_z)
     x_halos = halo("ga", n_a, x_edges)
     y_halos = halo("gy", n_y, y_faces)
-    results = stencil(0, x_halos, z_halos, ())
-    news = [results[0]]
-    chunks = [exchange(results[1:])]
-    late_z, _ = lax.optimization_barrier((tuple(late_z), results[2]))
+    head_news, head = stencil(0, (1,), x_halos, z_halos, ())
+    others = (0,) + tuple(range(2, n_a))
+    rest_news, rest = stencil(0, others, x_halos, z_halos, ())
+    news = rest_news[:1] + head_news + rest_news[1:]
+    chunks = [exchange(rest[:1] + head + rest[1:])]
+    late_z, _ = lax.optimization_barrier((tuple(late_z), head[0]))
     z_halos = halo("gz", n_z, late_z)
-    results = stencil(1, x_halos, z_halos, y_halos)
-    news.append(results[0])
-    chunks.append(exchange(results[1:]))
+    more, snaps = stencil(1, tuple(range(n_a)), x_halos, z_halos, y_halos)
+    news += more
+    chunks.append(exchange(snaps))
     new_fields = pl.pallas_call(
-        functools.partial(flush_kernel, plan),
+        functools.partial(flush_kernel, plan, n_a),
         out_shape=sds((variables, rows, lanes), f32),
-        in_specs=[VMEM] * len(plan),
+        in_specs=[VMEM] * len(news),
         out_specs=ANY,
-        scratch_shapes=[pltpu.SemaphoreType.DMA((sum(len(segments) for segments in plan),))],
+        scratch_shapes=[pltpu.SemaphoreType.DMA((n_a * sum(len(segments) for segments in plan),))],
         name="flush",
         compiler_params=pltpu.CompilerParams(vmem_limit_bytes=4 * MIB),
     )(*news)

time: 61.5 us -> 64.7 us (1.052)
  waiting for transfers between devices: 11.3 us -> 14.1 us
    ppermute x6, waiting for transfers between devices: 6.99 us -> 9.7 us  [exchange(): received.append(lax.ppermute(snaps[k], 'ga', ring_pairs(n_a, k)))]
    ppermute x6, starting transfers between devices: 12.2 us -> 14.5 us  [spread(): lax.ppermute(value, 'ga', [(i, partner(n_a, i, k)) for i in range(n_a)])]
    ppermute x1, starting transfers between devices: 2.27 us -> 0.64 us  [shards(): lax.ppermute(sides[d_x], 'gy', [(y, y ^ 2 * d_x) for y in range(n_y)])]
    pallas_call x2 -> x3, Pallas kernels: 4.27 us -> 4.66 us  [stencil(): pl.pallas_call(functools.partial(stencil_kernel, z_cells, counts, index,...]
  transfers between devices with their start and end apart: 23 -> 23, of which waited for: 5 -> 6; matrix products, arithmetic and copies ran while one was open for 0% -> 0% of each run, Pallas kernels for 10% -> 12%
where the time goes in v5:
time: 64.7 us; the launch traced here: 64.6 us
  starting transfers between devices  36.9 us (57%)
  waiting for transfers between devices  14.1 us (22%)
  Pallas kernels  12.7 us (20%)
  between operations  0.78 us (1%)
    ppermute x6, starting transfers between devices, spread(): lax.ppermute(value, 'ga', [(i, partner(n_a, i, k)) for i in range(n_a)])  14.5 us
    ppermute x6, waiting for transfers between devices, exchange(): received.append(lax.ppermute(snaps[k], 'ga', ring_pairs(n_a, k)))  9.7 us
    ppermute x6, starting transfers between devices, halo(): received.append(lax.ppermute(face, axis, swap_pairs(count, turn)))  9.29 us
    ppermute x6, starting transfers between devices, exchange(): received.append(lax.ppermute(snaps[k], 'ga', ring_pairs(n_a, k)))  8.9 us
    pallas_call x3, Pallas kernels, stencil(): pl.pallas_call(functools.partial(stencil_kernel, z_cells, counts, index,...  4.66 us
    ppermute x3, starting transfers between devices, shards(): received.append(lax.ppermute(sums[block], ('gy', 'gz'), pairs))  3.49 us
    pallas_call x1, Pallas kernels, shards(): call(functools.partial(pack_kernel, z_cells, counts, plan), [sds((variabl...  2.74 us
    ppermute x6, waiting for transfers between devices, halo(): received.append(lax.ppermute(face, axis, swap_pairs(count, turn)))  2.05 us
  transfers between devices with their start and end apart: 23, of which 6 were waited for; matrix products, arithmetic and copies ran while one was open for 0% of the time, Pallas kernels for 12%

profile of v5, /device:TPU:0, one launch (start us, length us, event | category | flops | bytes accessed | tf_op | source)
XLA Modules:
  0.0 64.6 jit_solution(13389679008524006094)
XLA Ops:
  0.7 2.7 %shard_map.94 = (f32[16,256,128]{2,1,0:T(8,128)S(1)}, f32[16,4,128]{2,1,0:T(4,128)S(1)}, f32[16,4,128]{2,1,0:T(4,128)S(1)}, f32[2,2048]{1,0:T(2,128)S(1)}, f32[2...) custom-call(f32[16,256,128]{2,1,0:T(8,128)} %bitcast.13), custom_call_target="tpu_custom_call" | custom-call | tf_op jit(solution)/shard_map/pallas_call | solution.py:441
  3.4 3.1 %collective-permute-start.2 = (bf16[16,32,128]{2,1,0:T(8,128)(2,1)S(1)}, bf16[16,32,128]{2,1,0:T(8,128)(2,1)S(1)}, u32[]{:S(2)}, u32[]{:S(2)}) collective-permute-start(bf16[16,32,128]{2,1,0:T(8,128)(2,1)S(1)} %get-tuple-element.46), channel_id=1, source_target_pairs={{0,4},{4,0},{1,5},{5,1},{2,6},{6,2},{3,7},{7,3},{8,12},{12,8},{9,1... | collective-permute-start | bytes 393224 | tf_op jit(solution)/shard_map/ppermute | solution.py:458
  6.5 1.6 %collective-permute-start = (f32[2,2048]{1,0:T(2,128)S(1)}, f32[2,2048]{1,0:T(2,128)S(1)}, u32[]{:S(2)}, u32[]{:S(2)}) collective-permute-start(f32[2,2048]{1,0:T(2,128)S(1)} %get-tuple-element.44), channel_id=1, source_target_pairs={{0,1},{1,0},{2,3},{3,2},{4,5},{5,4},{6,7},{7,6},{8,9},{9,8},{10,11... | collective-permute-start | bytes 49160 | tf_op jit(solution)/shard_map/ppermute | solution.py:458
  8.0 2.5 %collective-permute-start.1 = (f32[2,2048]{1,0:T(2,128)S(1)}, f32[2,2048]{1,0:T(2,128)S(1)}, u32[]{:S(2)}, u32[]{:S(2)}) collective-permute-start(f32[2,2048]{1,0:T(2,128)S(1)} %get-tuple-element.45), channel_id=1, source_target_pairs={{0,3},{1,2},{2,1},{3,0},{4,7},{5,6},{6,5},{7,4},{8,11},{9,10},{10,... | collective-permute-start | bytes 49160 | tf_op jit(solution)/shard_map/ppermute | solution.py:458
  10.5 1.0 %shard_map.95 = (f32[8,256,256]{2,1,0:T(8,128)S(1)}, f32[3,256,128]{2,1,0:T(8,128)S(1)}) custom-call(f32[16,16]{1,0:T(8,128)S(1)} %copy-done.3, f32[3,256,128]{2,1,0:T(8,128)} %bitcast.15, f32[16,256,128]{2,1,0:T(8,128)S(1)} %get-tuple-element.41.f_ref), custom_call_target="tpu_custom_call" | custom-call | tf_op jit(solution)/shard_map/pallas_call | solution.py:461
  11.5 2.0 %collective-permute-done.1.rest_1_ = f32[2,2048]{1,0:T(2,128)S(1)} collective-permute-done((f32[2,2048]{1,0:T(2,128)S(1)}, f32[2,2048]{1,0:T(2,128)S(1)}, u32[]{:S(2)}, u32[]{:S(2)}) %collective-permute-start.1) | collective-permute-done | bytes 16416 | tf_op jit(solution)/shard_map/ppermute | solution.py:458
  13.6 1.0 %stencil.4 = (f32[4,128,128]{2,1,0:T(8,128)S(1)}, bf16[4,128,128]{2,1,0:T(8,128)(2,1)S(1)}) custom-call(f32[16]{0:T(128)S(1)} %copy-done.4, f32[3,256,128]{2,1,0:T(8,128)S(1)} %get-tuple-element.42.vel_ref, f32[16,256,128]{2,1,0:T(8,128)S(1)} %bitcast.7, f32[16,256,128]{2,1,0:T(8,128)S(1)} %get-tuple-element.41.f_ref, ...), custom_call_target="tpu_custom_call" | custom-call | tf_op jit(solution)/shard_map/stencil/pallas_call | solution.py:472
  15.2 1.6 %collective-permute-start.5 = (f32[16,4,128]{2,1,0:T(4,128)S(1)}, f32[16,4,128]{2,1,0:T(4,128)S(1)}, u32[]{:S(2)}, u32[]{:S(2)}) collective-permute-start(f32[16,4,128]{2,1,0:T(4,128)S(1)} %get-tuple-element.55), channel_id=1, source_target_pairs={{0,24},{8,16},{16,8},{24,0},{1,25},{9,17},{17,9},{25,1},{2,26},{10... | collective-permute-start | bytes 98312 | tf_op jit(solution)/shard_map/ppermute | solution.py:458
  16.8 1.6 %stencil.3 = (f32[4,128,128]{2,1,0:T(8,128)S(1)}, f32[4,128,128]{2,1,0:T(8,128)S(1)}, f32[4,128,128]{2,1,0:T(8,128)S(1)}, bf16[4,128,128]{2,1,0:T(8,128)(2,1)S(1...) custom-call(f32[16]{0:T(128)S(1)} %copy-done.4, f32[3,256,128]{2,1,0:T(8,128)S(1)} %get-tuple-element.42.vel_ref, ...), custom_call_target="tpu_custom_call" | custom-call | tf_op jit(solution)/shard_map/stencil/pallas_call | solution.py:472
  18.4 3.1 %collective-permute-start.10 = (bf16[4,128,128]{2,1,0:T(8,128)(2,1)S(1)}, bf16[4,128,128]{2,1,0:T(8,128)(2,1)S(1)}, u32[]{:S(2)}, u32[]{:S(2)}) collective-permute-start(bf16[4,128,128]{2,1,0:T(8,128)(2,1)S(1)} %get-tuple-element.65), channel_id=1, source_target_pairs={{0,2},{1,3},{2,0},{3,1},{4,6},{5,7},{6,4},{7,5},{8,10},{9,11},{10,... | collective-permute-start | bytes 393224 | tf_op jit(solution)/shard_map/ppermute | solution.py:490
  22.4 2.0 %stencil.5 = (f32[4,128,128]{2,1,0:T(8,128)S(1)}, f32[4,128,128]{2,1,0:T(8,128)S(1)}, f32[4,128,128]{2,1,0:T(8,128)S(1)}, f32[4,128,128]{2,1,0:T(8,128)S(1)}, bf...) custom-call(f32[16]{0:T(128)S(1)} %copy-done.4, ...), custom_call_target="tpu_custom_call" | custom-call | tf_op jit(solution)/shard_map/stencil/pallas_call | solution.py:472
  24.4 1.2 %collective-permute-start.6 = (bf16[4,128,128]{2,1,0:T(8,128)(2,1)S(1)}, bf16[4,128,128]{2,1,0:T(8,128)(2,1)S(1)}, u32[]{:S(2)}, u32[]{:S(2)}) collective-permute-start(bf16[4,128,128]{2,1,0:T(8,128)(2,1)S(1)} %get-tuple-element.61), channel_id=1, source_target_pairs={{0,1},{1,2},{2,3},{3,0},{4,5},{5,6},{6,7},{7,4},{8,9},{9,10},{10,1... | collective-permute-start | bytes 393224 | tf_op jit(solution)/shard_map/ppermute | solution.py:490
  25.7 0.9 %collective-permute-start.7 = (bf16[4,128,128]{2,1,0:T(8,128)(2,1)S(1)}, bf16[4,128,128]{2,1,0:T(8,128)(2,1)S(1)}, u32[]{:S(2)}, u32[]{:S(2)}) collective-permute-start(bf16[4,128,128]{2,1,0:T(8,128)(2,1)S(1)} %get-tuple-element.62), channel_id=1, source_target_pairs={{0,2},{1,3},{2,0},{3,1},{4,6},{5,7},{6,4},{7,5},{8,10},{9,11},{10,... | collective-permute-start | bytes 393224 | tf_op jit(solution)/shard_map/ppermute | solution.py:490
  26.5 2.8 %collective-permute-start.8 = (bf16[4,128,128]{2,1,0:T(8,128)(2,1)S(1)}, bf16[4,128,128]{2,1,0:T(8,128)(2,1)S(1)}, u32[]{:S(2)}, u32[]{:S(2)}) collective-permute-start(bf16[4,128,128]{2,1,0:T(8,128)(2,1)S(1)} %get-tuple-element.63), channel_id=1, source_target_pairs={{0,3},{1,0},{2,1},{3,2},{4,7},{5,4},{6,5},{7,6},{8,11},{9,8},{10,9... | collective-permute-start | bytes 393224 | tf_op jit(solution)/shard_map/ppermute | solution.py:490
  30.2 2.6 %collective-permute-done.6.refs_1_ = bf16[4,128,128]{2,1,0:T(8,128)(2,1)S(1)} collective-permute-done((bf16[4,128,128]{2,1,0:T(8,128)(2,1)S(1)}, bf16[4,128,128]{2,1,0:T(8,128)(2,1)S(1)}, u32[]{:S(2)}, u32[]{:S(2)}) %collective-permute-start.6) | collective-permute-done | bytes 131104 | tf_op jit(solution)/shard_map/ppermute | solution.py:490
  32.8 7.1 %collective-permute-done.7.refs_2_ = bf16[4,128,128]{2,1,0:T(8,128)(2,1)S(1)} collective-permute-done((bf16[4,128,128]{2,1,0:T(8,128)(2,1)S(1)}, bf16[4,128,128]{2,1,0:T(8,128)(2,1)S(1)}, u32[]{:S(2)}, u32[]{:S(2)}) %collective-permute-start.7) | collective-permute-done | bytes 131104 | tf_op jit(solution)/shard_map/ppermute | solution.py:490
  40.7 1.7 %collective-permute-done.12.other_ref = bf16[4,64,768]{2,1,0:T(8,128)(2,1)S(1)} collective-permute-done((bf16[4,64,768]{2,1,0:T(8,128)(2,1)S(1)}, bf16[4,64,768]{2,1,0:T(8,128)(2,1)S(1)}, u32[]{:S(2)}, u32[]{:S(2)}) %collective-permute-start.12) | collective-permute-done | bytes 393248 | tf_op jit(solution)/shard_map/ppermute | solution.py:539
  43.2 1.5 %collective-permute-start.14 = (bf16[64,512]{1,0:T(8,128)(2,1)S(1)}, bf16[64,512]{1,0:T(8,128)(2,1)S(1)}, u32[]{:S(2)}, u32[]{:S(2)}) collective-permute-start(bf16[64,512]{1,0:T(8,128)(2,1)S(1)} %get-tuple-element.74), channel_id=1, source_target_pairs={{0,4},{4,0},{8,12},{12,8},{16,20},{20,16},{24,28},{28,24},{1,5},{5... | collective-permute-start | bytes 196616 | tf_op jit(solution)/shard_map/ppermute | solution.py:555
  44.7 1.4 %collective-permute-start.15 = (bf16[64,512]{1,0:T(8,128)(2,1)S(1)}, bf16[64,512]{1,0:T(8,128)(2,1)S(1)}, u32[]{:S(2)}, u32[]{:S(2)}) collective-permute-start(bf16[64,512]{1,0:T(8,128)(2,1)S(1)} %get-tuple-element.75), channel_id=1, source_target_pairs={{0,16},{4,20},{8,24},{12,28},{16,0},{20,4},{24,8},{28,12},{1,17},{... | collective-permute-start | bytes 196616 | tf_op jit(solution)/shard_map/ppermute | solution.py:555
  47.4 5.7 %collective-permute-start.22 = (bf16[64,256]{1,0:T(8,128)(2,1)S(1)}, bf16[64,256]{1,0:T(8,128)(2,1)S(1)}, u32[]{:S(2)}, u32[]{:S(2)}) collective-permute-start(bf16[64,256]{1,0:T(8,128)(2,1)S(1)} %shard_map.99.value_ref.refs_4_), channel_id=1, source_target_pairs={{0,3},{1,2},{2,1},{3,0},{4,7},{5,6},{6,5},{7,4},{8,11},{9,10},{10,... | collective-permute-start | bytes 98312 | tf_op jit(solution)/shard_map/ppermute | solution.py:586
  53.2 3.9 %collective-permute-start.19 = (bf16[64,512]{1,0:T(8,128)(2,1)S(1)}, bf16[64,512]{1,0:T(8,128)(2,1)S(1)}, u32[]{:S(2)}, u32[]{:S(2)}) collective-permute-start(bf16[64,512]{1,0:T(8,128)(2,1)S(1)} %shard_map.101.refs_0_), channel_id=1, source_target_pairs={{0,3},{1,2},{2,1},{3,0},{4,7},{5,6},{6,5},{7,4},{8,11},{9,10},{10,... | collective-permute-start | bytes 196616 | tf_op jit(solution)/shard_map/ppermute | solution.py:586
  57.7 2.3 %collective-permute-start.21 = (bf16[64,256]{1,0:T(8,128)(2,1)S(1)}, bf16[64,256]{1,0:T(8,128)(2,1)S(1)}, u32[]{:S(2)}, u32[]{:S(2)}) collective-permute-start(bf16[64,256]{1,0:T(8,128)(2,1)S(1)} %shard_map.99.value_ref.refs_4_), channel_id=1, source_target_pairs={{0,2},{1,3},{2,0},{3,1},{4,6},{5,7},{6,4},{7,5},{8,10},{9,11},{10,... | collective-permute-start | bytes 98312 | tf_op jit(solution)/shard_map/ppermute | solution.py:586
  59.9 2.0 %collective-permute-start.20 = (bf16[64,256]{1,0:T(8,128)(2,1)S(1)}, bf16[64,256]{1,0:T(8,128)(2,1)S(1)}, u32[]{:S(2)}, u32[]{:S(2)}) collective-permute-start(bf16[64,256]{1,0:T(8,128)(2,1)S(1)} %shard_map.99.value_ref.refs_4_), channel_id=1, source_target_pairs={{0,1},{1,0},{2,3},{3,2},{4,5},{5,4},{6,7},{7,6},{8,9},{9,8},{10,11... | collective-permute-start | bytes 98312 | tf_op jit(solution)/shard_map/ppermute | solution.py:586
  62.0 1.4 %flush.1 = f32[16,256,128]{2,1,0:T(8,128)} custom-call(f32[4,128,128]{2,1,0:T(8,128)S(1)} %get-tuple-element.47.refs_0_, f32[4,128,128]{2,1,0:T(8,128)S(1)} %get-tuple-element.48.refs_1_, f32[4,128,128]{2,1,0:T(8,128)S(1)} %get-tuple-element.49.refs_2_, f32[4,128,128]{2,1,0:T(8,128)S(1)} %get-tuple-element.50.refs_3_, ...), custom_call_target="tpu_custom_call" | custom-call | tf_op jit(solution)/shard_map/flush/pallas_call | solution.py:507
  (45 shorter events, 7.0 us)
Async XLA Ops:
  3.4 10.2 %collective-permute-start.2 = (bf16[16,32,128]{2,1,0:T(8,128)(2,1)S(1)}, bf16[16,32,128]{2,1,0:T(8,128)(2,1)S(1)}, u32[]{:S(2)}, u32[]{:S(2)}) collective-permute-start(bf16[16,32,128]{2,1,0:T(8,128)(2,1)S(1)} %get-tuple-element.46), channel_id=1, source_target_pairs={{0,4},{4,0},{1,5},{5,1},{2,6},{6,2},{3,7},{7,3},{8,12},{12,8},{9,1... | collective-permute-start | bytes 393224 | tf_op jit(solution)/shard_map/ppermute | solution.py:458
  6.5 5.1 %collective-permute-start = (f32[2,2048]{1,0:T(2,128)S(1)}, f32[2,2048]{1,0:T(2,128)S(1)}, u32[]{:S(2)}, u32[]{:S(2)}) collective-permute-start(f32[2,2048]{1,0:T(2,128)S(1)} %get-tuple-element.44), channel_id=1, source_target_pairs={{0,1},{1,0},{2,3},{3,2},{4,5},{5,4},{6,7},{7,6},{8,9},{9,8},{10,11... | collective-permute-start | bytes 49160 | tf_op jit(solution)/shard_map/ppermute | solution.py:458
  8.0 5.5 %collective-permute-start.1 = (f32[2,2048]{1,0:T(2,128)S(1)}, f32[2,2048]{1,0:T(2,128)S(1)}, u32[]{:S(2)}, u32[]{:S(2)}) collective-permute-start(f32[2,2048]{1,0:T(2,128)S(1)} %get-tuple-element.45), channel_id=1, source_target_pairs={{0,3},{1,2},{2,1},{3,0},{4,7},{5,6},{6,5},{7,4},{8,11},{9,10},{10,... | collective-permute-start | bytes 49160 | tf_op jit(solution)/shard_map/ppermute | solution.py:458
  14.6 7.8 %collective-permute-start.3 = (bf16[16,32,128]{2,1,0:T(8,128)(2,1)S(1)}, bf16[16,32,128]{2,1,0:T(8,128)(2,1)S(1)}, u32[]{:S(2)}, u32[]{:S(2)}) collective-permute-start(bf16[16,32,128]{2,1,0:T(8,128)(2,1)S(1)} %get-tuple-element.53), channel_id=1, source_target_pairs={{0,4},{4,0},{1,5},{5,1},{2,6},{6,2},{3,7},{7,3},{8,12},{12,8},{9,1... | collective-permute-start | bytes 393224 | tf_op jit(solution)/shard_map/ppermute | solution.py:458
  15.2 11.4 %collective-permute-start.9 = (bf16[4,128,128]{2,1,0:T(8,128)(2,1)S(1)}, bf16[4,128,128]{2,1,0:T(8,128)(2,1)S(1)}, u32[]{:S(2)}, u32[]{:S(2)}) collective-permute-start(bf16[4,128,128]{2,1,0:T(8,128)(2,1)S(1)} %get-tuple-element.52), channel_id=1, source_target_pairs={{0,1},{1,2},{2,3},{3,0},{4,5},{5,6},{6,7},{7,4},{8,9},{9,10},{10,1... | collective-permute-start | bytes 393224 | tf_op jit(solution)/shard_map/ppermute | solution.py:490
  15.2 6.4 %collective-permute-start.4 = (f32[16,4,128]{2,1,0:T(4,128)S(1)}, f32[16,4,128]{2,1,0:T(4,128)S(1)}, u32[]{:S(2)}, u32[]{:S(2)}) collective-permute-start(f32[16,4,128]{2,1,0:T(4,128)S(1)} %get-tuple-element.54), channel_id=1, source_target_pairs={{0,8},{8,0},{16,24},{24,16},{1,9},{9,1},{17,25},{25,17},{2,10},{10... | collective-permute-start | bytes 98312 | tf_op jit(solution)/shard_map/ppermute | solution.py:458
  15.2 7.2 %collective-permute-start.5 = (f32[16,4,128]{2,1,0:T(4,128)S(1)}, f32[16,4,128]{2,1,0:T(4,128)S(1)}, u32[]{:S(2)}, u32[]{:S(2)}) collective-permute-start(f32[16,4,128]{2,1,0:T(4,128)S(1)} %get-tuple-element.55), channel_id=1, source_target_pairs={{0,24},{8,16},{16,8},{24,0},{1,25},{9,17},{17,9},{25,1},{2,26},{10... | collective-permute-start | bytes 98312 | tf_op jit(solution)/shard_map/ppermute | solution.py:458
  18.4 11.0 %collective-permute-start.10 = (bf16[4,128,128]{2,1,0:T(8,128)(2,1)S(1)}, bf16[4,128,128]{2,1,0:T(8,128)(2,1)S(1)}, u32[]{:S(2)}, u32[]{:S(2)}) collective-permute-start(bf16[4,128,128]{2,1,0:T(8,128)(2,1)S(1)} %get-tuple-element.65), channel_id=1, source_target_pairs={{0,2},{1,3},{2,0},{3,1},{4,6},{5,7},{6,4},{7,5},{8,10},{9,11},{10,... | collective-permute-start | bytes 393224 | tf_op jit(solution)/shard_map/ppermute | solution.py:490
  21.5 7.9 %collective-permute-start.11 = (bf16[4,128,128]{2,1,0:T(8,128)(2,1)S(1)}, bf16[4,128,128]{2,1,0:T(8,128)(2,1)S(1)}, u32[]{:S(2)}, u32[]{:S(2)}) collective-permute-start(bf16[4,128,128]{2,1,0:T(8,128)(2,1)S(1)} %get-tuple-element.66), channel_id=1, source_target_pairs={{0,3},{1,0},{2,1},{3,2},{4,7},{5,4},{6,5},{7,6},{8,11},{9,8},{10,9... | collective-permute-start | bytes 393224 | tf_op jit(solution)/shard_map/ppermute | solution.py:490
  24.4 22.4 %copy-start.2 = (f32[256,64]{0,1:T(8,128)S(1)}, f32[256,64]{0,1:T(8,128)}, u32[]{:S(2)}) copy-start(f32[256,64]{0,1:T(8,128)} %param.13) | copy-start | bytes 196612
  24.4 8.3 %collective-permute-start.6 = (bf16[4,128,128]{2,1,0:T(8,128)(2,1)S(1)}, bf16[4,128,128]{2,1,0:T(8,128)(2,1)S(1)}, u32[]{:S(2)}, u32[]{:S(2)}) collective-permute-start(bf16[4,128,128]{2,1,0:T(8,128)(2,1)S(1)} %get-tuple-element.61), channel_id=1, source_target_pairs={{0,1},{1,2},{2,3},{3,0},{4,5},{5,6},{6,7},{7,4},{8,9},{9,10},{10,1... | collective-permute-start | bytes 393224 | tf_op jit(solution)/shard_map/ppermute | solution.py:490
  25.7 14.2 %collective-permute-start.7 = (bf16[4,128,128]{2,1,0:T(8,128)(2,1)S(1)}, bf16[4,128,128]{2,1,0:T(8,128)(2,1)S(1)}, u32[]{:S(2)}, u32[]{:S(2)}) collective-permute-start(bf16[4,128,128]{2,1,0:T(8,128)(2,1)S(1)} %get-tuple-element.62), channel_id=1, source_target_pairs={{0,2},{1,3},{2,0},{3,1},{4,6},{5,7},{6,4},{7,5},{8,10},{9,11},{10,... | collective-permute-start | bytes 393224 | tf_op jit(solution)/shard_map/ppermute | solution.py:490
  26.5 13.4 %collective-permute-start.8 = (bf16[4,128,128]{2,1,0:T(8,128)(2,1)S(1)}, bf16[4,128,128]{2,1,0:T(8,128)(2,1)S(1)}, u32[]{:S(2)}, u32[]{:S(2)}) collective-permute-start(bf16[4,128,128]{2,1,0:T(8,128)(2,1)S(1)} %get-tuple-element.63), channel_id=1, source_target_pairs={{0,3},{1,0},{2,1},{3,2},{4,7},{5,4},{6,5},{7,6},{8,11},{9,8},{10,9... | collective-permute-start | bytes 393224 | tf_op jit(solution)/shard_map/ppermute | solution.py:490
  40.7 1.8 %collective-permute-start.12 = (bf16[4,64,768]{2,1,0:T(8,128)(2,1)S(1)}, bf16[4,64,768]{2,1,0:T(8,128)(2,1)S(1)}, u32[]{:S(2)}, u32[]{:S(2)}) collective-permute-start(bf16[4,64,768]{2,1,0:T(8,128)(2,1)S(1)} %get-tuple-element.70), channel_id=1, source_target_pairs={{0,8},{8,0},{16,24},{24,16},{1,9},{9,1},{17,25},{25,17},{2,10},{10... | collective-permute-start | bytes 1179656 | tf_op jit(solution)/shard_map/ppermute | solution.py:539
  42.5 4.3 %collective-permute-start.13 = (bf16[64,512]{1,0:T(8,128)(2,1)S(1)}, bf16[64,512]{1,0:T(8,128)(2,1)S(1)}, u32[]{:S(2)}, u32[]{:S(2)}) collective-permute-start(bf16[64,512]{1,0:T(8,128)(2,1)S(1)} %get-tuple-element.72), channel_id=1, source_target_pairs={{0,16},{8,24},{16,0},{24,8},{1,17},{9,25},{17,1},{25,9},{2,18},{10... | collective-permute-start | bytes 196616 | tf_op jit(solution)/shard_map/ppermute | solution.py:548
  43.2 9.9 %collective-permute-start.14 = (bf16[64,512]{1,0:T(8,128)(2,1)S(1)}, bf16[64,512]{1,0:T(8,128)(2,1)S(1)}, u32[]{:S(2)}, u32[]{:S(2)}) collective-permute-start(bf16[64,512]{1,0:T(8,128)(2,1)S(1)} %get-tuple-element.74), channel_id=1, source_target_pairs={{0,4},{4,0},{8,12},{12,8},{16,20},{20,16},{24,28},{28,24},{1,5},{5... | collective-permute-start | bytes 196616 | tf_op jit(solution)/shard_map/ppermute | solution.py:555
  44.7 8.4 %collective-permute-start.15 = (bf16[64,512]{1,0:T(8,128)(2,1)S(1)}, bf16[64,512]{1,0:T(8,128)(2,1)S(1)}, u32[]{:S(2)}, u32[]{:S(2)}) collective-permute-start(bf16[64,512]{1,0:T(8,128)(2,1)S(1)} %get-tuple-element.75), channel_id=1, source_target_pairs={{0,16},{4,20},{8,24},{12,28},{16,0},{20,4},{24,8},{28,12},{1,17},{... | collective-permute-start | bytes 196616 | tf_op jit(solution)/shard_map/ppermute | solution.py:555
  46.1 7.0 %collective-permute-start.16 = (bf16[64,512]{1,0:T(8,128)(2,1)S(1)}, bf16[64,512]{1,0:T(8,128)(2,1)S(1)}, u32[]{:S(2)}, u32[]{:S(2)}) collective-permute-start(bf16[64,512]{1,0:T(8,128)(2,1)S(1)} %get-tuple-element.76), channel_id=1, source_target_pairs={{0,20},{4,16},{8,28},{12,24},{16,4},{20,0},{24,12},{28,8},{1,21},{... | collective-permute-start | bytes 196616 | tf_op jit(solution)/shard_map/ppermute | solution.py:555
  47.4 12.6 %collective-permute-start.22 = (bf16[64,256]{1,0:T(8,128)(2,1)S(1)}, bf16[64,256]{1,0:T(8,128)(2,1)S(1)}, u32[]{:S(2)}, u32[]{:S(2)}) collective-permute-start(bf16[64,256]{1,0:T(8,128)(2,1)S(1)} %shard_map.99.value_ref.refs_4_), channel_id=1, source_target_pairs={{0,3},{1,2},{2,1},{3,0},{4,7},{5,6},{6,5},{7,4},{8,11},{9,10},{10,... | collective-permute-start | bytes 98312 | tf_op jit(solution)/shard_map/ppermute | solution.py:586
  53.2 10.7 %collective-permute-start.19 = (bf16[64,512]{1,0:T(8,128)(2,1)S(1)}, bf16[64,512]{1,0:T(8,128)(2,1)S(1)}, u32[]{:S(2)}, u32[]{:S(2)}) collective-permute-start(bf16[64,512]{1,0:T(8,128)(2,1)S(1)} %shard_map.101.refs_0_), channel_id=1, source_target_pairs={{0,3},{1,2},{2,1},{3,0},{4,7},{5,6},{6,5},{7,4},{8,11},{9,10},{10,... | collective-permute-start | bytes 196616 | tf_op jit(solution)/shard_map/ppermute | solution.py:586
  57.0 6.9 %collective-permute-start.18 = (bf16[64,512]{1,0:T(8,128)(2,1)S(1)}, bf16[64,512]{1,0:T(8,128)(2,1)S(1)}, u32[]{:S(2)}, u32[]{:S(2)}) collective-permute-start(bf16[64,512]{1,0:T(8,128)(2,1)S(1)} %shard_map.101.refs_0_), channel_id=1, source_target_pairs={{0,2},{1,3},{2,0},{3,1},{4,6},{5,7},{6,4},{7,5},{8,10},{9,11},{10,... | collective-permute-start | bytes 196616 | tf_op jit(solution)/shard_map/ppermute | solution.py:586
  57.0 6.9 %collective-permute-start.17 = (bf16[64,512]{1,0:T(8,128)(2,1)S(1)}, bf16[64,512]{1,0:T(8,128)(2,1)S(1)}, u32[]{:S(2)}, u32[]{:S(2)}) collective-permute-start(bf16[64,512]{1,0:T(8,128)(2,1)S(1)} %shard_map.101.refs_0_), channel_id=1, source_target_pairs={{0,1},{1,0},{2,3},{3,2},{4,5},{5,4},{6,7},{7,6},{8,9},{9,8},{10,11... | collective-permute-start | bytes 196616 | tf_op jit(solution)/shard_map/ppermute | solution.py:586
  57.7 5.7 %collective-permute-start.21 = (bf16[64,256]{1,0:T(8,128)(2,1)S(1)}, bf16[64,256]{1,0:T(8,128)(2,1)S(1)}, u32[]{:S(2)}, u32[]{:S(2)}) collective-permute-start(bf16[64,256]{1,0:T(8,128)(2,1)S(1)} %shard_map.99.value_ref.refs_4_), channel_id=1, source_target_pairs={{0,2},{1,3},{2,0},{3,1},{4,6},{5,7},{6,4},{7,5},{8,10},{9,11},{10,... | collective-permute-start | bytes 98312 | tf_op jit(solution)/shard_map/ppermute | solution.py:586
  59.9 3.9 %collective-permute-start.20 = (bf16[64,256]{1,0:T(8,128)(2,1)S(1)}, bf16[64,256]{1,0:T(8,128)(2,1)S(1)}, u32[]{:S(2)}, u32[]{:S(2)}) collective-permute-start(bf16[64,256]{1,0:T(8,128)(2,1)S(1)} %shard_map.99.value_ref.refs_4_), channel_id=1, source_target_pairs={{0,1},{1,0},{2,3},{3,2},{4,5},{5,4},{6,7},{7,6},{8,9},{9,8},{10,11... | collective-permute-start | bytes 98312 | tf_op jit(solution)/shard_map/ppermute | solution.py:586
  (4 other events, 43.7 us)
